TPU v7x, 768 devices: a whole 4x8x12 slice. The times are simulated.
768 devices in a mesh: dom: 64 (over y, x, core), sub: 12 (over z).
Axes of the slice: x: 4, y: 8, z: 12, core: 2. Of those that a mesh axis runs over, the one named last changes fastest.
Arguments:
- velocity: float32 [3, 320, 108, 128], P(None, 'dom', 'sub'), may hold values from -8 to 8, as said below
- displacement: float32 [3, 320, 108, 128], P(None, 'dom', 'sub'), may hold values from -0.02 to 0.02, as said below
- energy: float32 [8, 128, 48, 64], P(None, 'dom', 'sub'), may hold values from 0.5 to 2
- rho_weight: float32 [27, 128, 48, 64], P(None, 'dom', 'sub'), may hold values from 0.5 to 2
- mass_share: float32 [4, 128, 48, 64], P(None, 'dom', 'sub'), may hold values from 0.2 to 2
- energy_share: float32 [4, 128, 48, 64], P(None, 'dom', 'sub'), may hold values from 0.5 to 2
- material_id: int32 [128, 48, 64], P('dom', 'sub'), may hold values from 0 to 3
- mix_mask: int32 [4, 128, 48, 64], P(None, 'dom', 'sub'), may hold values 0 or 1
Outputs:
- accel: float32 [3, 320, 108, 128], P(None, 'dom', 'sub')
- residual: float32 [3, 320, 108, 128], P(None, 'dom', 'sub')
- energy_rate: float32 [8, 128, 48, 64], P(None, 'dom', 'sub')
Inputs may be any that keep to these rules, and one draw needn't show every extreme that they name: `velocity`: every copy of a grid node holds the same value. `displacement`: every copy of a grid node holds the same value.
All inputs are finite; a program needn't handle non-finite values. No bound on the sum of `mix_mask` on one device may be relied on, other than what follows from the above.
Results may differ from a plain program's by a relative error of at most 0.0003.
Values sent between devices are 32-bit elements; how exact they have to be, the bound alone decides.
No kernel may reach another device: no remote copies, remote signals or barrier semaphores. Data moves between devices by JAX's collectives and lax.ppermute only.
A program may use at most 32 MiB of HBM per device.

v0:
```python
import functools
import math

import jax
import jax.numpy as jnp
import numpy as np
from jax import lax
from jax.sharding import Mesh
from jax.sharding import PartitionSpec as P

MATS = 4
EQ_ITERS = 4
CG_ITERS = 3
DOM_SUB = ("dom_0", "dom_1", "dom_2", "sub")
DOM = ("dom_0", "dom_1", "dom_2")


gammas = (1.4, 1.67, 2.0, 3.0)
cold_terms = (0.3, 1.2, 0.6, 2.4)
highest = lax.Precision.HIGHEST


def extended(block, sides, width):
    for axis, dim in sides:
        count = lax.axis_size(axis)
        forward = [(i, i + 1) for i in range(count - 1)]
        forward.append((count - 1, 0))
        backward = [(target, source) for source, target in forward]
        low = lax.ppermute(
            lax.slice_in_dim(block, block.shape[dim] - width, None, axis=dim), axis, forward
        )
        high = lax.ppermute(lax.slice_in_dim(block, 0, width, axis=dim), axis, backward)
        block = jnp.concatenate([low, block, high], axis=dim)
    return block


def one_axis_at_a_time(shard, axes):
    return functools.reduce(lax.psum, axes, shard)


def tensor_three(first, second, third):
    grid = (
        first[:, None, None, :, None, None]
        * second[None, :, None, None, :, None]
        * third[None, None, :, None, None, :]
    )
    rows = first.shape[0] * second.shape[0] * third.shape[0]
    columns = first.shape[1] * second.shape[1] * third.shape[1]
    return grid.reshape(rows, columns)


def basis_tables():
    spread_root = math.sqrt(0.15)
    points = np.array([0.5 - spread_root, 0.5, 0.5 + spread_root])
    quad_one = np.array([5.0, 8.0, 5.0]) / 18.0
    value_one = np.stack(
        [
            2.0 * (points - 0.5) * (points - 1.0),
            -4.0 * points * (points - 1.0),
            2.0 * points * (points - 0.5),
        ],
        1,
    )
    slope_one = np.stack([4.0 * points - 3.0, 4.0 - 8.0 * points, 4.0 * points - 1.0], 1)
    linear_one = np.stack([1.0 - points, points], 1)
    values = tensor_three(value_one, value_one, value_one)
    slopes = np.stack(
        [
            tensor_three(slope_one, value_one, value_one),
            tensor_three(value_one, slope_one, value_one),
            tensor_three(value_one, value_one, slope_one),
        ]
    )
    linear = tensor_three(linear_one, linear_one, linear_one)
    weights = (quad_one[:, None, None] * quad_one[None, :, None] * quad_one[None, None, :]).reshape(
        27
    )
    return (
        jnp.asarray(values, jnp.float32),
        jnp.asarray(slopes, jnp.float32),
        jnp.asarray(linear, jnp.float32),
        jnp.asarray(weights, jnp.float32),
    )


def depth_table(zone_z):
    layer = jnp.arange(2 * zone_z, dtype=jnp.int32)[:, None, None]
    offset = jnp.arange(3, dtype=jnp.int32)[None, :, None]
    zone_at = jnp.arange(zone_z, dtype=jnp.int32)[None, None, :]
    return jnp.where(layer == (2 * zone_at + offset) % (2 * zone_z), 1.0, 0.0).astype(jnp.float32)


def zone_corners(nodes_in, zone_x, zone_y, table):
    by_depth = jnp.einsum("cxyk,ksz->scxyz", nodes_in, table, precision=highest)
    pieces = []
    for shift_x in range(3):
        for shift_y in range(3):
            for shift_z in range(3):
                pieces.append(
                    by_depth[shift_z][
                        :, shift_x : shift_x + 2 * zone_x : 2, shift_y : shift_y + 2 * zone_y : 2
                    ]
                )
    return jnp.stack(pieces, 0)


def weave_axis(contrib, axis_at):
    lower_part, middle_part, upper_part = (contrib[0], contrib[1], contrib[2])
    zone_count = lower_part.shape[axis_at]
    high_pad = [(0, 0)] * lower_part.ndim
    high_pad[axis_at] = (0, 1)
    low_pad = [(0, 0)] * lower_part.ndim
    low_pad[axis_at] = (1, 0)
    even_rows = jnp.pad(lower_part, high_pad) + jnp.pad(upper_part, low_pad)
    even_head = lax.slice_in_dim(even_rows, 0, zone_count, axis=axis_at)
    even_tail = lax.slice_in_dim(even_rows, zone_count, zone_count + 1, axis=axis_at)
    woven_rows = jnp.stack([even_head, middle_part], axis_at + 1)
    extent = list(even_head.shape)
    extent[axis_at] = 2 * zone_count
    return jnp.concatenate([woven_rows.reshape(extent), even_tail], axis_at)


def place_zones(contrib, table):
    spread = contrib.reshape((3, 3, 3) + contrib.shape[1:])
    spread = weave_axis(spread, 3)
    spread = weave_axis(spread, 3)
    return jnp.einsum("scxyz,ksz->cxyk", spread, table, precision=highest)


def adjugate_of(matrix):
    cofactors = []
    for column in range(3):
        entries = []
        for line_at in range(3):
            entries.append(
                matrix[(line_at + 1) % 3, (column + 1) % 3]
                * matrix[(line_at + 2) % 3, (column + 2) % 3]
                - matrix[(line_at + 1) % 3, (column + 2) % 3]
                * matrix[(line_at + 2) % 3, (column + 1) % 3]
            )
        cofactors.append(jnp.stack(entries))
    return jnp.stack(cofactors)


def zone_force(
    displacement,
    velocity,
    energy,
    rho_weight,
    mass_share,
    energy_share,
    material_id,
    mix_mask,
    tables,
    table_z,
):
    value_table, slope_table, linear_table, weight_table = tables
    zone_x, zone_y = (energy.shape[1], energy.shape[2])
    disp_zone = zone_corners(displacement, zone_x, zone_y, table_z)
    vel_zone = zone_corners(velocity, zone_x, zone_y, table_z)
    identity = jnp.eye(3, dtype=jnp.float32)[:, :, None, None, None, None]
    jacobian = jnp.einsum("dqn,ncxyz->cdqxyz", slope_table, disp_zone, precision=highest) + identity
    velgrad = jnp.einsum("dqn,ncxyz->cdqxyz", slope_table, vel_zone, precision=highest)
    adjugate = adjugate_of(jacobian)
    determinant = jnp.sum(jacobian[0] * adjugate[:, 0], axis=0)
    density = rho_weight / determinant
    energy_points = jnp.einsum("qj,jxyz->qxyz", linear_table, energy, precision=highest)
    material = jnp.arange(MATS, dtype=jnp.int32)[:, None, None, None]
    present = jnp.where((mix_mask == 1) | (material_id[None] == material), 1.0, 0.0).astype(
        jnp.float32
    )
    weighted = present * mass_share
    mass_fraction = weighted / jnp.sum(weighted, 0, keepdims=True)
    gamma_less = jnp.asarray(gammas, jnp.float32)[:, None, None, None, None] - 1.0
    cold_part = jnp.asarray(cold_terms, jnp.float32)[:, None, None, None, None]
    pressure_load = (
        gamma_less * density[None] * (mass_fraction * energy_share)[:, None] * energy_points[None]
    )
    fraction = jnp.broadcast_to(
        (present / jnp.sum(present, 0, keepdims=True))[:, None], pressure_load.shape
    )
    for sweep_at in range(EQ_ITERS):
        grown_part = jnp.sqrt(fraction * (pressure_load + cold_part * fraction))
        fraction = grown_part / jnp.sum(grown_part, 0, keepdims=True)
    pressure = jnp.sum(pressure_load + cold_part * fraction, 0)
    stress = weight_table[:, None, None, None] * pressure
    force_zone = jnp.einsum(
        "dqn,dcqxyz->ncxyz", slope_table, adjugate * stress[None, None], precision=highest
    )
    divergence = jnp.sum(velgrad * jnp.swapaxes(adjugate, 0, 1), (0, 1))
    work_rate = jnp.einsum("qj,qxyz->jxyz", linear_table, stress * divergence, precision=highest)
    lumped = jnp.einsum(
        "qj,qxyz->jxyz",
        linear_table,
        weight_table[:, None, None, None] * rho_weight,
        precision=highest,
    )
    return (force_zone, -work_rate / lumped)


def mass_zone(node_field, mass_weight, tables, table_z):
    value_table = tables[0]
    corners = zone_corners(node_field, mass_weight.shape[1], mass_weight.shape[2], table_z)
    at_points = (
        jnp.einsum("qn,ncxyz->cqxyz", value_table, corners, precision=highest) * mass_weight[None]
    )
    return jnp.einsum("qn,cqxyz->ncxyz", value_table, at_points, precision=highest)


def assemble(local_sum):
    widened = extended(local_sum, ((DOM, 1), ("sub", 2)), 1)
    middle_rows = widened[:, :, 1:-1]
    summed = local_sum.at[:, 0].add(middle_rows[:, 0]).at[:, -1].add(middle_rows[:, -1])
    lower_side = widened[:, :, 0]
    upper_side = widened[:, :, -1]
    lower_side = lower_side[:, 1:-1].at[:, 0].add(lower_side[:, 0]).at[:, -1].add(lower_side[:, -1])
    upper_side = upper_side[:, 1:-1].at[:, 0].add(upper_side[:, 0]).at[:, -1].add(upper_side[:, -1])
    return summed.at[:, :, 0].add(lower_side).at[:, :, -1].add(upper_side)


def inner_pair(left_field, right_field):
    owned_left = left_field[:, :-1, :-1]
    owned_right = right_field[:, :-1, :-1]
    return (
        one_axis_at_a_time(jnp.sum(owned_left * owned_left), DOM_SUB),
        one_axis_at_a_time(jnp.sum(owned_left * owned_right), DOM_SUB),
    )


def per_device(
    velocity, displacement, energy, rho_weight, mass_share, energy_share, material_id, mix_mask
):
    tables = basis_tables()
    table_z = depth_table(energy.shape[3])
    force_zone, energy_rate = zone_force(
        displacement,
        velocity,
        energy,
        rho_weight,
        mass_share,
        energy_share,
        material_id,
        mix_mask,
        tables,
        table_z,
    )
    force_total = assemble(place_zones(force_zone, table_z))
    mass_weight = tables[3][:, None, None, None] * rho_weight

    def apply_mass(node_field):
        return assemble(place_zones(mass_zone(node_field, mass_weight, tables, table_z), table_z))

    solution = jnp.zeros_like(force_total)
    residual = force_total
    mapped = apply_mass(residual)
    direction = jnp.zeros_like(force_total)
    direction_image = jnp.zeros_like(force_total)
    image_image = jnp.zeros_like(force_total)
    norm_old = 1.0
    step_old = 1.0
    for sweep_at in range(CG_ITERS):
        norm_now, product = inner_pair(residual, mapped)
        if sweep_at + 1 < CG_ITERS:
            mapped_twice = apply_mass(mapped)
        if sweep_at == 0:
            growth = 0.0
            step_size = norm_now / product
        else:
            growth = norm_now / norm_old
            step_size = norm_now / (product - growth * norm_now / step_old)
        direction = residual + growth * direction
        direction_image = mapped + growth * direction_image
        solution = solution + step_size * direction
        residual = residual - step_size * direction_image
        if sweep_at + 1 < CG_ITERS:
            image_image = mapped_twice + growth * image_image
            mapped = mapped - step_size * image_image
        norm_old = norm_now
        step_old = step_size
    return (solution, residual, energy_rate)


def solution(mesh):
    torus = Mesh(
        mesh.devices.reshape(8, 4, 2, mesh.shape["sub"]), ("dom_0", "dom_1", "dom_2", "sub")
    )
    return jax.shard_map(
        per_device,
        mesh=torus,
        in_specs=(
            P(None, DOM, "sub", None),
            P(None, DOM, "sub", None),
            P(None, DOM, "sub", None),
            P(None, DOM, "sub", None),
            P(None, DOM, "sub", None),
            P(None, DOM, "sub", None),
            P(DOM, "sub", None),
            P(None, DOM, "sub", None),
        ),
        out_specs=(P(None, DOM, "sub", None), P(None, DOM, "sub", None), P(None, DOM, "sub", None)),
        check_vma=False,
    )
```

profile of v0, /device:TPU:1, one launch (start us, length us, event | category | flops | bytes accessed | tf_op | source)
XLA Modules:
  0.0 308.7 jit_solution(20493777421190420)
XLA Ops:
  0.7 1.4 convolution_bitcast_fusion.9
  7.9 1.1 fusion
  9.3 0.7 copy-done.4
  18.4 0.8 fusion.29
  19.2 1.2 fusion.77
  20.4 1.5 fusion.153
  21.9 1.6 add_reduce_fusion
  23.8 1.1 fusion.2
  25.2 0.8 convolution_bitcast_fusion.4
  27.2 4.5 %collective-permute-start = (f32[3,1,9,128]{3,1,0,2:T(1,128)S(1)}, f32[3,1,9,128]{3,1,0,2:T(1,128)S(1)}, u32[]{:S(2)}, u32[]{:S(2)}) collective-permute-start(f32[3,1,9,128]{3,1,0,2:T(1,128)S(1)} %slice.1985), channel_id=1, source_target_pairs={{0,12},{12,24},{24,36},{36,48},{48,60},{60,72},{72,84},{84,96},{96... | collective-permute-start | bytes 41480 | tf_op jit(solution)/shard_map/ppermute | solution.py:29
  31.7 8.6 %collective-permute-done = f32[3,1,9,128]{3,1,0,2:T(1,128)S(1)} collective-permute-done((f32[3,1,9,128]{3,1,0,2:T(1,128)S(1)}, f32[3,1,9,128]{3,1,0,2:T(1,128)S(1)}, u32[]{:S(2)}, u32[]{:S(2)}) %collective-permute-start) | collective-permute-done | bytes 13856 | tf_op jit(solution)/shard_map/ppermute | solution.py:29
  40.3 7.7 %collective-permute-start.1 = (f32[3,1,9,128]{3,1,0,2:T(1,128)S(1)}, f32[3,1,9,128]{3,1,0,2:T(1,128)S(1)}, u32[]{:S(2)}, u32[]{:S(2)}) collective-permute-start(f32[3,1,9,128]{3,1,0,2:T(1,128)S(1)} %get-tuple-element.501), channel_id=1, source_target_pairs={{12,0},{24,12},{36,24},{48,36},{60,48},{72,60},{84,72},{96,84},{10... | collective-permute-start | bytes 41480 | tf_op jit(solution)/shard_map/ppermute | solution.py:32
  48.1 0.7 collective-permute-done.1
  48.8 5.4 %collective-permute-start.3 = (f32[3,7,1,128]{3,2,1,0:T(1,128)S(1)}, f32[3,7,1,128]{3,2,1,0:T(1,128)S(1)}, u32[]{:S(2)}, u32[]{:S(2)}) collective-permute-start(f32[3,7,1,128]{3,2,1,0:T(1,128)S(1)} %get-tuple-element.481), channel_id=1, source_target_pairs={{1,0},{2,1},{3,2},{4,3},{5,4},{6,5},{7,6},{8,7},{9,8},{10,9},{11,1... | collective-permute-start | bytes 32264 | tf_op jit(solution)/shard_map/ppermute | solution.py:32
  54.2 1.9 collective-permute-start.2
  56.3 3.6 %collective-permute-done.2 = f32[3,7,1,128]{3,1,0,2:T(8,128)S(1)} collective-permute-done((f32[3,7,1,128]{3,1,0,2:T(8,128)S(1)}, f32[3,7,1,128]{3,1,0,2:T(8,128)S(1)}, u32[]{:S(2)}, u32[]{:S(2)}) %collective-permute-start.2) | collective-permute-done | bytes 10784 | tf_op jit(solution)/shard_map/ppermute | solution.py:29
  69.0 1.9 collective-permute-start.4
  71.0 2.7 collective-permute-done.4
  73.7 7.7 %collective-permute-start.5 = (f32[3,1,9,128]{3,1,0,2:T(1,128)S(1)}, f32[3,1,9,128]{3,1,0,2:T(1,128)S(1)}, u32[]{:S(2)}, u32[]{:S(2)}) collective-permute-start(f32[3,1,9,128]{3,1,0,2:T(1,128)S(1)} %get-tuple-element.499), channel_id=1, source_target_pairs={{12,0},{24,12},{36,24},{48,36},{60,48},{72,60},{84,72},{96,84},{10... | collective-permute-start | bytes 41480 | tf_op jit(solution)/shard_map/ppermute | solution.py:32
  81.4 0.8 collective-permute-done.5
  82.2 1.9 collective-permute-start.7
  84.1 3.4 %collective-permute-start.6 = (f32[3,7,1,128]{3,1,0,2:T(8,128)S(1)}, f32[3,7,1,128]{3,1,0,2:T(8,128)S(1)}, u32[]{:S(2)}, u32[]{:S(2)}) collective-permute-start(f32[3,7,1,128]{3,1,0,2:T(8,128)S(1)} %get-tuple-element.488), channel_id=1, source_target_pairs={{0,1},{1,2},{2,3},{3,4},{4,5},{5,6},{6,7},{7,8},{8,9},{9,10},{10,1... | collective-permute-start | bytes 32264 | tf_op jit(solution)/shard_map/ppermute | solution.py:29
  87.7 2.0 collective-permute-done.6
  98.7 1.9 collective-permute-start.8
  100.8 2.2 collective-permute-done.8
  103.0 7.7 %collective-permute-start.9 = (f32[3,1,9,128]{3,1,0,2:T(1,128)S(1)}, f32[3,1,9,128]{3,1,0,2:T(1,128)S(1)}, u32[]{:S(2)}, u32[]{:S(2)}) collective-permute-start(f32[3,1,9,128]{3,1,0,2:T(1,128)S(1)} %get-tuple-element.497), channel_id=1, source_target_pairs={{12,0},{24,12},{36,24},{48,36},{60,48},{72,60},{84,72},{96,84},{10... | collective-permute-start | bytes 41480 | tf_op jit(solution)/shard_map/ppermute | solution.py:32
  111.3 12.5 %all-reduce.21 = (f32[]{:T(128)}, f32[]{:T(128)}) all-reduce(f32[]{:T(128)} %get-tuple-element.404, f32[]{:T(128)} %get-tuple-element.403), channel_id=1, replica_groups=mesh['dom_0'=8,'dom_1'=4,'dom_2'=2,'sub'=12] {'dom_0'}, use_global_device_ids=true, to_apply=%region_9.10 | all-reduce | flops 2 | bytes 16 | tf_op jit(solution)/shard_map/psum | solution.py:38
  123.8 6.6 %all-reduce.24 = (f32[]{:T(128)}, f32[]{:T(128)}) all-reduce(f32[]{:T(128)} %get-tuple-element.417, f32[]{:T(128)} %get-tuple-element.418), channel_id=1, replica_groups=mesh['dom_0'=8,'dom_1'=4,'dom_2'=2,'sub'=12] {'dom_1'}, use_global_device_ids=true, to_apply=%region_10.11 | all-reduce | flops 2 | bytes 16 | tf_op jit(solution)/shard_map/psum | solution.py:38
  130.5 7.8 %all-reduce.27 = (f32[]{:T(128)}, f32[]{:T(128)}) all-reduce(f32[]{:T(128)} %get-tuple-element.423, f32[]{:T(128)} %get-tuple-element.424), channel_id=1, replica_groups=mesh['dom_0'=8,'dom_1'=4,'dom_2'=2,'sub'=12] {'dom_2'}, use_global_device_ids=true, to_apply=%region_11.12 | all-reduce | flops 2 | bytes 16 | tf_op jit(solution)/shard_map/psum | solution.py:38
  138.2 16.5 %all-reduce.18 = (f32[]{:T(128)}, f32[]{:T(128)}) all-reduce(f32[]{:T(128)} %get-tuple-element.429, f32[]{:T(128)} %get-tuple-element.430), channel_id=1, replica_groups=mesh['dom_0'=8,'dom_1'=4,'dom_2'=2,'sub'=12] {'sub'}, use_global_device_ids=true, to_apply=%region_12.13 | all-reduce | flops 2 | bytes 16 | tf_op jit(solution)/shard_map/psum | solution.py:38
  156.1 3.1 %collective-permute-start.11 = (f32[3,7,1,128]{3,1,0,2:T(8,128)S(1)}, f32[3,7,1,128]{3,1,0,2:T(8,128)S(1)}, u32[]{:S(2)}, u32[]{:S(2)}) collective-permute-start(f32[3,7,1,128]{3,1,0,2:T(8,128)S(1)} %get-tuple-element.485), channel_id=1, source_target_pairs={{1,0},{2,1},{3,2},{4,3},{5,4},{6,5},{7,6},{8,7},{9,8},{10,9},{11,1... | collective-permute-start | bytes 32264 | tf_op jit(solution)/shard_map/ppermute | solution.py:32
  159.2 2.2 collective-permute-start.10
  161.7 3.2 %collective-permute-done.10 = f32[3,7,1,128]{3,1,0,2:T(8,128)S(1)} collective-permute-done((f32[3,7,1,128]{3,1,0,2:T(8,128)S(1)}, f32[3,7,1,128]{3,1,0,2:T(8,128)S(1)}, u32[]{:S(2)}, u32[]{:S(2)}) %collective-permute-start.10) | collective-permute-done | bytes 10784 | tf_op jit(solution)/shard_map/ppermute | solution.py:29
  174.1 10.5 %collective-permute-start.12 = (f32[3,1,9,128]{3,1,0,2:T(1,128)S(1)}, f32[3,1,9,128]{3,1,0,2:T(1,128)S(1)}, u32[]{:S(2)}, u32[]{:S(2)}) collective-permute-start(f32[3,1,9,128]{3,1,0,2:T(1,128)S(1)} %slice.2077), channel_id=1, source_target_pairs={{0,12},{12,24},{24,36},{36,48},{48,60},{60,72},{72,84},{84,96},{96... | collective-permute-start | bytes 41480 | tf_op jit(solution)/shard_map/ppermute | solution.py:29
  185.5 5.9 %collective-permute-start.13 = (f32[3,1,9,128]{3,1,0,2:T(1,128)S(1)}, f32[3,1,9,128]{3,1,0,2:T(1,128)S(1)}, u32[]{:S(2)}, u32[]{:S(2)}) collective-permute-start(f32[3,1,9,128]{3,1,0,2:T(1,128)S(1)} %get-tuple-element.495), channel_id=1, source_target_pairs={{12,0},{24,12},{36,24},{48,36},{60,48},{72,60},{84,72},{96,84},{10... | collective-permute-start | bytes 41480 | tf_op jit(solution)/shard_map/ppermute | solution.py:32
  191.4 0.7 fusion.79
  192.1 13.4 %all-reduce.20 = (f32[]{:T(128)}, f32[]{:T(128)}) all-reduce(f32[]{:T(128)} %get-tuple-element.402, f32[]{:T(128)} %get-tuple-element.401), channel_id=1, replica_groups=mesh['dom_0'=8,'dom_1'=4,'dom_2'=2,'sub'=12] {'dom_0'}, use_global_device_ids=true, to_apply=%region_19.20 | all-reduce | flops 2 | bytes 16 | tf_op jit(solution)/shard_map/psum | solution.py:38
  205.5 6.7 %all-reduce.23 = (f32[]{:T(128)}, f32[]{:T(128)}) all-reduce(f32[]{:T(128)} %get-tuple-element.415, f32[]{:T(128)} %get-tuple-element.416), channel_id=1, replica_groups=mesh['dom_0'=8,'dom_1'=4,'dom_2'=2,'sub'=12] {'dom_1'}, use_global_device_ids=true, to_apply=%region_20.21 | all-reduce | flops 2 | bytes 16 | tf_op jit(solution)/shard_map/psum | solution.py:38
  212.2 8.0 %all-reduce.26 = (f32[]{:T(128)}, f32[]{:T(128)}) all-reduce(f32[]{:T(128)} %get-tuple-element.421, f32[]{:T(128)} %get-tuple-element.422), channel_id=1, replica_groups=mesh['dom_0'=8,'dom_1'=4,'dom_2'=2,'sub'=12] {'dom_2'}, use_global_device_ids=true, to_apply=%region_21.22 | all-reduce | flops 2 | bytes 16 | tf_op jit(solution)/shard_map/psum | solution.py:38
  220.2 16.2 %all-reduce.17 = (f32[]{:T(128)}, f32[]{:T(128)}) all-reduce(f32[]{:T(128)} %get-tuple-element.427, f32[]{:T(128)} %get-tuple-element.428), channel_id=1, replica_groups=mesh['dom_0'=8,'dom_1'=4,'dom_2'=2,'sub'=12] {'sub'}, use_global_device_ids=true, to_apply=%region_22.23 | all-reduce | flops 2 | bytes 16 | tf_op jit(solution)/shard_map/psum | solution.py:38
  241.0 3.5 %collective-permute-start.15 = (f32[3,7,1,128]{3,1,0,2:T(8,128)S(1)}, f32[3,7,1,128]{3,1,0,2:T(8,128)S(1)}, u32[]{:S(2)}, u32[]{:S(2)}) collective-permute-start(f32[3,7,1,128]{3,1,0,2:T(8,128)S(1)} %get-tuple-element.483), channel_id=1, source_target_pairs={{1,0},{2,1},{3,2},{4,3},{5,4},{6,5},{7,6},{8,7},{9,8},{10,9},{11,1... | collective-permute-start | bytes 32264 | tf_op jit(solution)/shard_map/ppermute | solution.py:32
  244.5 1.9 collective-permute-start.14
  246.7 3.5 %collective-permute-done.14 = f32[3,7,1,128]{3,1,0,2:T(8,128)S(1)} collective-permute-done((f32[3,7,1,128]{3,1,0,2:T(8,128)S(1)}, f32[3,7,1,128]{3,1,0,2:T(8,128)S(1)}, u32[]{:S(2)}, u32[]{:S(2)}) %collective-permute-start.14) | collective-permute-done | bytes 10784 | tf_op jit(solution)/shard_map/ppermute | solution.py:29
  251.1 12.5 %all-reduce.19 = (f32[]{:T(128)}, f32[]{:T(128)}) all-reduce(f32[]{:T(128)} %get-tuple-element.400, f32[]{:T(128)} %get-tuple-element.399), channel_id=1, replica_groups=mesh['dom_0'=8,'dom_1'=4,'dom_2'=2,'sub'=12] {'dom_0'}, use_global_device_ids=true, to_apply=%region_29.30 | all-reduce | flops 2 | bytes 16 | tf_op jit(solution)/shard_map/psum | solution.py:38
  263.6 8.3 %all-reduce.22 = (f32[]{:T(128)}, f32[]{:T(128)}) all-reduce(f32[]{:T(128)} %get-tuple-element.413, f32[]{:T(128)} %get-tuple-element.414), channel_id=1, replica_groups=mesh['dom_0'=8,'dom_1'=4,'dom_2'=2,'sub'=12] {'dom_1'}, use_global_device_ids=true, to_apply=%region_30.31 | all-reduce | flops 2 | bytes 16 | tf_op jit(solution)/shard_map/psum | solution.py:38
  272.0 15.2 %all-reduce.25 = (f32[]{:T(128)}, f32[]{:T(128)}) all-reduce(f32[]{:T(128)} %get-tuple-element.419, f32[]{:T(128)} %get-tuple-element.420), channel_id=1, replica_groups=mesh['dom_0'=8,'dom_1'=4,'dom_2'=2,'sub'=12] {'dom_2'}, use_global_device_ids=true, to_apply=%region_31.32 | all-reduce | flops 2 | bytes 16 | tf_op jit(solution)/shard_map/psum | solution.py:38
  287.2 16.1 %all-reduce.16 = (f32[]{:T(128)}, f32[]{:T(128)}) all-reduce(f32[]{:T(128)} %get-tuple-element.425, f32[]{:T(128)} %get-tuple-element.426), channel_id=1, replica_groups=mesh['dom_0'=8,'dom_1'=4,'dom_2'=2,'sub'=12] {'sub'}, use_global_device_ids=true, to_apply=%region_32.33 | all-reduce | flops 2 | bytes 16 | tf_op jit(solution)/shard_map/psum | solution.py:38
  307.3 0.7 copy.358
  (482 shorter events, 45.2 us)
Async XLA Ops:
  0.6 16.7 %copy-start = (f32[8,2,4,64]{3,2,1,0:T(4,128)S(1)}, f32[8,2,4,64]{3,2,1,0:T(4,128)}, u32[]{:S(2)}) copy-start(f32[8,2,4,64]{3,2,1,0:T(4,128)} %param.80) | copy-start | bytes 49156
  0.7 7.3 %copy-start.3 = (f32[3,27,27,1,1,1]{2,1,0,5,4,3:T(8,128)S(1)}, f32[3,27,27,1,1,1]{2,1,0,5,4,3:T(8,128)}, u32[]{:S(2)}) copy-start(f32[3,27,27,1,1,1]{2,1,0,5,4,3:T(8,128)} %constant.789) | copy-start | bytes 26248
  9.1 0.9 copy-start.4
  16.3 0.9 copy-start.2
  16.5 0.9 copy-start.6
  16.5 1.3 copy-start.5
  16.5 1.2 copy-start.7
  16.5 1.2 copy-start.11
  16.5 1.3 copy-start.8
  16.5 1.3 copy-start.9
  16.6 1.3 copy-start.10
  23.6 1.3 copy-start.12
  27.2 13.1 %collective-permute-start = (f32[3,1,9,128]{3,1,0,2:T(1,128)S(1)}, f32[3,1,9,128]{3,1,0,2:T(1,128)S(1)}, u32[]{:S(2)}, u32[]{:S(2)}) collective-permute-start(f32[3,1,9,128]{3,1,0,2:T(1,128)S(1)} %slice.1985), channel_id=1, source_target_pairs={{0,12},{12,24},{24,36},{36,48},{48,60},{60,72},{72,84},{84,96},{96... | collective-permute-start | bytes 41480 | tf_op jit(solution)/shard_map/ppermute | solution.py:29
  40.3 8.5 %collective-permute-start.1 = (f32[3,1,9,128]{3,1,0,2:T(1,128)S(1)}, f32[3,1,9,128]{3,1,0,2:T(1,128)S(1)}, u32[]{:S(2)}, u32[]{:S(2)}) collective-permute-start(f32[3,1,9,128]{3,1,0,2:T(1,128)S(1)} %get-tuple-element.501), channel_id=1, source_target_pairs={{12,0},{24,12},{36,24},{48,36},{60,48},{72,60},{84,72},{96,84},{10... | collective-permute-start | bytes 41480 | tf_op jit(solution)/shard_map/ppermute | solution.py:32
  48.8 7.4 %collective-permute-start.3 = (f32[3,7,1,128]{3,2,1,0:T(1,128)S(1)}, f32[3,7,1,128]{3,2,1,0:T(1,128)S(1)}, u32[]{:S(2)}, u32[]{:S(2)}) collective-permute-start(f32[3,7,1,128]{3,2,1,0:T(1,128)S(1)} %get-tuple-element.481), channel_id=1, source_target_pairs={{1,0},{2,1},{3,2},{4,3},{5,4},{6,5},{7,6},{8,7},{9,8},{10,9},{11,1... | collective-permute-start | bytes 32264 | tf_op jit(solution)/shard_map/ppermute | solution.py:32
  54.2 5.7 %collective-permute-start.2 = (f32[3,7,1,128]{3,1,0,2:T(8,128)S(1)}, f32[3,7,1,128]{3,1,0,2:T(8,128)S(1)}, u32[]{:S(2)}, u32[]{:S(2)}) collective-permute-start(f32[3,7,1,128]{3,1,0,2:T(8,128)S(1)} %copy.395), channel_id=1, source_target_pairs={{0,1},{1,2},{2,3},{3,4},{4,5},{5,6},{6,7},{7,8},{8,9},{9,10},{10,1... | collective-permute-start | bytes 32264 | tf_op jit(solution)/shard_map/ppermute | solution.py:29
  60.2 6.6 %copy-start.1 = (f32[27,27,1,1,1]{1,0,4,3,2:T(8,128)S(1)}, f32[27,27,1,1,1]{1,0,4,3,2:T(8,128)}, u32[]{:S(2)}) copy-start(f32[27,27,1,1,1]{1,0,4,3,2:T(8,128)} %constant.791) | copy-start | bytes 8752
  69.0 4.6 %collective-permute-start.4 = (f32[3,1,9,128]{3,1,0,2:T(1,128)S(1)}, f32[3,1,9,128]{3,1,0,2:T(1,128)S(1)}, u32[]{:S(2)}, u32[]{:S(2)}) collective-permute-start(f32[3,1,9,128]{3,1,0,2:T(1,128)S(1)} %slice.2015), channel_id=1, source_target_pairs={{0,12},{12,24},{24,36},{36,48},{48,60},{60,72},{72,84},{84,96},{96... | collective-permute-start | bytes 41480 | tf_op jit(solution)/shard_map/ppermute | solution.py:29
  73.7 8.5 %collective-permute-start.5 = (f32[3,1,9,128]{3,1,0,2:T(1,128)S(1)}, f32[3,1,9,128]{3,1,0,2:T(1,128)S(1)}, u32[]{:S(2)}, u32[]{:S(2)}) collective-permute-start(f32[3,1,9,128]{3,1,0,2:T(1,128)S(1)} %get-tuple-element.499), channel_id=1, source_target_pairs={{12,0},{24,12},{36,24},{48,36},{60,48},{72,60},{84,72},{96,84},{10... | collective-permute-start | bytes 41480 | tf_op jit(solution)/shard_map/ppermute | solution.py:32
  82.2 5.5 %collective-permute-start.7 = (f32[3,7,1,128]{3,1,0,2:T(8,128)S(1)}, f32[3,7,1,128]{3,1,0,2:T(8,128)S(1)}, u32[]{:S(2)}, u32[]{:S(2)}) collective-permute-start(f32[3,7,1,128]{3,1,0,2:T(8,128)S(1)} %get-tuple-element.487), channel_id=1, source_target_pairs={{1,0},{2,1},{3,2},{4,3},{5,4},{6,5},{7,6},{8,7},{9,8},{10,9},{11,1... | collective-permute-start | bytes 32264 | tf_op jit(solution)/shard_map/ppermute | solution.py:32
  84.1 5.7 %collective-permute-start.6 = (f32[3,7,1,128]{3,1,0,2:T(8,128)S(1)}, f32[3,7,1,128]{3,1,0,2:T(8,128)S(1)}, u32[]{:S(2)}, u32[]{:S(2)}) collective-permute-start(f32[3,7,1,128]{3,1,0,2:T(8,128)S(1)} %get-tuple-element.488), channel_id=1, source_target_pairs={{0,1},{1,2},{2,3},{3,4},{4,5},{5,6},{6,7},{7,8},{8,9},{9,10},{10,1... | collective-permute-start | bytes 32264 | tf_op jit(solution)/shard_map/ppermute | solution.py:29
  98.7 4.3 %collective-permute-start.8 = (f32[3,1,9,128]{3,1,0,2:T(1,128)S(1)}, f32[3,1,9,128]{3,1,0,2:T(1,128)S(1)}, u32[]{:S(2)}, u32[]{:S(2)}) collective-permute-start(f32[3,1,9,128]{3,1,0,2:T(1,128)S(1)} %slice.2046), channel_id=1, source_target_pairs={{0,12},{12,24},{24,36},{36,48},{48,60},{60,72},{72,84},{84,96},{96... | collective-permute-start | bytes 41480 | tf_op jit(solution)/shard_map/ppermute | solution.py:29
  103.0 53.1 %collective-permute-start.9 = (f32[3,1,9,128]{3,1,0,2:T(1,128)S(1)}, f32[3,1,9,128]{3,1,0,2:T(1,128)S(1)}, u32[]{:S(2)}, u32[]{:S(2)}) collective-permute-start(f32[3,1,9,128]{3,1,0,2:T(1,128)S(1)} %get-tuple-element.497), channel_id=1, source_target_pairs={{12,0},{24,12},{36,24},{48,36},{60,48},{72,60},{84,72},{96,84},{10... | collective-permute-start | bytes 41480 | tf_op jit(solution)/shard_map/ppermute | solution.py:32
  156.1 5.5 %collective-permute-start.11 = (f32[3,7,1,128]{3,1,0,2:T(8,128)S(1)}, f32[3,7,1,128]{3,1,0,2:T(8,128)S(1)}, u32[]{:S(2)}, u32[]{:S(2)}) collective-permute-start(f32[3,7,1,128]{3,1,0,2:T(8,128)S(1)} %get-tuple-element.485), channel_id=1, source_target_pairs={{1,0},{2,1},{3,2},{4,3},{5,4},{6,5},{7,6},{8,7},{9,8},{10,9},{11,1... | collective-permute-start | bytes 32264 | tf_op jit(solution)/shard_map/ppermute | solution.py:32
  159.2 5.7 %collective-permute-start.10 = (f32[3,7,1,128]{3,1,0,2:T(8,128)S(1)}, f32[3,7,1,128]{3,1,0,2:T(8,128)S(1)}, u32[]{:S(2)}, u32[]{:S(2)}) collective-permute-start(f32[3,7,1,128]{3,1,0,2:T(8,128)S(1)} %get-tuple-element.486), channel_id=1, source_target_pairs={{0,1},{1,2},{2,3},{3,4},{4,5},{5,6},{6,7},{7,8},{8,9},{9,10},{10,1... | collective-permute-start | bytes 32264 | tf_op jit(solution)/shard_map/ppermute | solution.py:29
  174.1 11.4 %collective-permute-start.12 = (f32[3,1,9,128]{3,1,0,2:T(1,128)S(1)}, f32[3,1,9,128]{3,1,0,2:T(1,128)S(1)}, u32[]{:S(2)}, u32[]{:S(2)}) collective-permute-start(f32[3,1,9,128]{3,1,0,2:T(1,128)S(1)} %slice.2077), channel_id=1, source_target_pairs={{0,12},{12,24},{24,36},{36,48},{48,60},{60,72},{72,84},{84,96},{96... | collective-permute-start | bytes 41480 | tf_op jit(solution)/shard_map/ppermute | solution.py:29
  185.5 55.4 %collective-permute-start.13 = (f32[3,1,9,128]{3,1,0,2:T(1,128)S(1)}, f32[3,1,9,128]{3,1,0,2:T(1,128)S(1)}, u32[]{:S(2)}, u32[]{:S(2)}) collective-permute-start(f32[3,1,9,128]{3,1,0,2:T(1,128)S(1)} %get-tuple-element.495), channel_id=1, source_target_pairs={{12,0},{24,12},{36,24},{48,36},{60,48},{72,60},{84,72},{96,84},{10... | collective-permute-start | bytes 41480 | tf_op jit(solution)/shard_map/ppermute | solution.py:32
  241.0 5.7 %collective-permute-start.15 = (f32[3,7,1,128]{3,1,0,2:T(8,128)S(1)}, f32[3,7,1,128]{3,1,0,2:T(8,128)S(1)}, u32[]{:S(2)}, u32[]{:S(2)}) collective-permute-start(f32[3,7,1,128]{3,1,0,2:T(8,128)S(1)} %get-tuple-element.483), channel_id=1, source_target_pairs={{1,0},{2,1},{3,2},{4,3},{5,4},{6,5},{7,6},{8,7},{9,8},{10,9},{11,1... | collective-permute-start | bytes 32264 | tf_op jit(solution)/shard_map/ppermute | solution.py:32
  244.5 5.7 %collective-permute-start.14 = (f32[3,7,1,128]{3,1,0,2:T(8,128)S(1)}, f32[3,7,1,128]{3,1,0,2:T(8,128)S(1)}, u32[]{:S(2)}, u32[]{:S(2)}) collective-permute-start(f32[3,7,1,128]{3,1,0,2:T(8,128)S(1)} %get-tuple-element.484), channel_id=1, source_target_pairs={{0,1},{1,2},{2,3},{3,4},{4,5},{5,6},{6,7},{7,8},{8,9},{9,10},{10,1... | collective-permute-start | bytes 32264 | tf_op jit(solution)/shard_map/ppermute | solution.py:29
where the time goes:
time: 313 us; the launch traced here: 309 us
  blocking collectives  140 us (45%)
  starting transfers between devices  71.1 us (23%)
  local copies, waits for them, and re-layouts  34.4 us (11%)
  waiting for transfers between devices  27.2 us (9%)
  between operations  13.7 us (4%)
  matrix products  12.2 us (4%)
  other arithmetic  10.3 us (3%)
    psum x12, blocking collectives, one_axis_at_a_time(): return functools.reduce(lax.psum, axes, shard)  140 us
    ppermute x8, starting transfers between devices, extended(): lax.ppermute(lax.slice_in_dim(block, 0, width, axis=dim), axis, backward)  42.8 us
    ppermute x8, starting transfers between devices, extended(): lax.ppermute(lax.slice_in_dim(block, block.shape[dim] - width, None, axis...  28.3 us
    slice x135, local copies, waits for them, and re-layouts, zone_corners(): by_depth[shift_z]  26.6 us
    ppermute x8, waiting for transfers between devices, extended(): lax.ppermute(lax.slice_in_dim(block, block.shape[dim] - width, None, axis...  25.7 us
  transfers between devices with their start and end apart: 16, of which 9 were waited for; matrix products, arithmetic and copies ran while one was open for 1% of the time, Pallas kernels for 0%

commit v1 on v0

--- a/solution.py
+++ b/solution.py
@@ -1,4 +1,3 @@
-import functools
 import math
 
 import jax
@@ -20,22 +19,39 @@
 highest = lax.Precision.HIGHEST
 
 
-def extended(block, sides, width):
-    for axis, dim in sides:
-        count = lax.axis_size(axis)
-        forward = [(i, i + 1) for i in range(count - 1)]
-        forward.append((count - 1, 0))
-        backward = [(target, source) for source, target in forward]
-        low = lax.ppermute(
-            lax.slice_in_dim(block, block.shape[dim] - width, None, axis=dim), axis, forward
-        )
-        high = lax.ppermute(lax.slice_in_dim(block, 0, width, axis=dim), axis, backward)
-        block = jnp.concatenate([low, block, high], axis=dim)
-    return block
-
-
-def one_axis_at_a_time(shard, axes):
-    return functools.reduce(lax.psum, axes, shard)
+def pair_groups(axes, offset):
+    count = 1
+    for axis in axes:
+        count *= lax.axis_size(axis)
+    return [[(i + offset) % count, (i + offset + 1) % count] for i in range(0, count, 2)]
+
+
+def pair_sum(layer, axes, offset):
+    gathered = lax.all_gather(layer, axes, axis_index_groups=pair_groups(axes, offset))
+    return gathered[0] + gathered[1]
+
+
+def join_axis(block, axes, dim):
+    even = lax.axis_index(axes) % 2 == 0
+    last = block.shape[dim] - 1
+    low = lax.slice_in_dim(block, 0, 1, axis=dim)
+    high = lax.slice_in_dim(block, last, last + 1, axis=dim)
+    inner = pair_sum(jnp.where(even, high, low), axes, 0)
+    outer = pair_sum(jnp.where(even, low, high), axes, 1)
+    middle = lax.slice_in_dim(block, 1, last, axis=dim)
+    return jnp.concatenate(
+        [jnp.where(even, outer, inner), middle, jnp.where(even, inner, outer)], dim
+    )
+
+
+def total(values):
+    for axes in (DOM, ("sub",)):
+        count = 1
+        for axis in axes:
+            count *= lax.axis_size(axis)
+        spread = jnp.broadcast_to(values[None], (count, values.shape[0]))
+        values = jnp.sum(lax.all_to_all(spread, axes, 0, 0, tiled=True), 0)
+    return values
 
 
 def tensor_three(first, second, third):
@@ -208,23 +224,57 @@
 
 
 def assemble(local_sum):
-    widened = extended(local_sum, ((DOM, 1), ("sub", 2)), 1)
-    middle_rows = widened[:, :, 1:-1]
-    summed = local_sum.at[:, 0].add(middle_rows[:, 0]).at[:, -1].add(middle_rows[:, -1])
-    lower_side = widened[:, :, 0]
-    upper_side = widened[:, :, -1]
-    lower_side = lower_side[:, 1:-1].at[:, 0].add(lower_side[:, 0]).at[:, -1].add(lower_side[:, -1])
-    upper_side = upper_side[:, 1:-1].at[:, 0].add(upper_side[:, 0]).at[:, -1].add(upper_side[:, -1])
-    return summed.at[:, :, 0].add(lower_side).at[:, :, -1].add(upper_side)
-
-
-def inner_pair(left_field, right_field):
-    owned_left = left_field[:, :-1, :-1]
-    owned_right = right_field[:, :-1, :-1]
-    return (
-        one_axis_at_a_time(jnp.sum(owned_left * owned_left), DOM_SUB),
-        one_axis_at_a_time(jnp.sum(owned_left * owned_right), DOM_SUB),
-    )
+    return join_axis(join_axis(local_sum, ("sub",), 2), DOM, 1)
+
+
+CENTER = 0.196
+HALF_WIDTH = 0.194
+PAIRS = ((0, 0), (0, 1), (0, 2), (0, 3), (1, 1), (1, 2), (1, 3), (2, 2), (2, 3))
+
+
+def dot_in(gram, left, right):
+    value = 0.0
+    for i in range(4):
+        for j in range(4):
+            if left[i] is None or right[j] is None or (i == 3 and j == 3):
+                continue
+            value = value + gram[(min(i, j), max(i, j))] * left[i] * right[j]
+    return value
+
+
+def axpy(scale, left, right):
+    out = []
+    for a, b in zip(left, right):
+        if a is None:
+            out.append(b)
+        elif b is None:
+            out.append(scale * a)
+        else:
+            out.append(scale * a + b)
+    return out
+
+
+def mapped_coefficients(p):
+    p0, p1, p2 = (0.0 if v is None else v for v in p[:3])
+    shifted = [0.5 * p1, p0 + 0.5 * p2, 0.5 * p1, 0.5 * p2]
+    return [HALF_WIDTH * b + CENTER * a for a, b in zip((p0, p1, p2, 0.0), shifted)]
+
+
+def cg_coefficients(gram):
+    accel = [0.0, 0.0, 0.0, 0.0]
+    residual = [1.0, 0.0, 0.0, 0.0]
+    direction = residual
+    norm_now = gram[(0, 0)]
+    for sweep_at in range(CG_ITERS):
+        mapped = mapped_coefficients(direction)
+        step = norm_now / dot_in(gram, direction, mapped)
+        accel = axpy(step, direction, accel)
+        residual = axpy(-step, mapped, residual)
+        if sweep_at + 1 < CG_ITERS:
+            norm_next = dot_in(gram, residual, residual)
+            direction = axpy(norm_next / norm_now, direction, residual)
+            norm_now = norm_next
+    return accel, residual
 
 
 def per_device(
@@ -250,39 +300,25 @@
     def apply_mass(node_field):
         return assemble(place_zones(mass_zone(node_field, mass_weight, tables, table_z), table_z))
 
-    solution = jnp.zeros_like(force_total)
-    residual = force_total
-    mapped = apply_mass(residual)
-    direction = jnp.zeros_like(force_total)
-    direction_image = jnp.zeros_like(force_total)
-    image_image = jnp.zeros_like(force_total)
-    norm_old = 1.0
-    step_old = 1.0
-    for sweep_at in range(CG_ITERS):
-        norm_now, product = inner_pair(residual, mapped)
-        if sweep_at + 1 < CG_ITERS:
-            mapped_twice = apply_mass(mapped)
-        if sweep_at == 0:
-            growth = 0.0
-            step_size = norm_now / product
-        else:
-            growth = norm_now / norm_old
-            step_size = norm_now / (product - growth * norm_now / step_old)
-        direction = residual + growth * direction
-        direction_image = mapped + growth * direction_image
-        solution = solution + step_size * direction
-        residual = residual - step_size * direction_image
-        if sweep_at + 1 < CG_ITERS:
-            image_image = mapped_twice + growth * image_image
-            mapped = mapped - step_size * image_image
-        norm_old = norm_now
-        step_old = step_size
-    return (solution, residual, energy_rate)
+    def shifted(node_field):
+        return (1.0 / HALF_WIDTH) * apply_mass(node_field) - (CENTER / HALF_WIDTH) * node_field
+
+    basis = [force_total, shifted(force_total)]
+    for _ in range(CG_ITERS - 1):
+        basis.append(2.0 * shifted(basis[-1]) - basis[-2])
+    owned = [field[:, :-1, :-1] for field in basis]
+    products = jnp.stack([jnp.sum(owned[i] * owned[j]) for i, j in PAIRS])
+    products = total(jnp.pad(products, (0, 16 - len(PAIRS))))
+    gram = {pair: products[at] for at, pair in enumerate(PAIRS)}
+    accel_of, residual_of = cg_coefficients(gram)
+    accel = sum(accel_of[i] * basis[i] for i in range(3))
+    residual = sum(residual_of[i] * basis[i] for i in range(4))
+    return (accel, residual, energy_rate)
 
 
 def solution(mesh):
     torus = Mesh(
-        mesh.devices.reshape(8, 4, 2, mesh.shape["sub"]), ("dom_0", "dom_1", "dom_2", "sub")
+        mesh.devices.reshape(mesh.shape["dom"] // 8, 4, 2, mesh.shape["sub"]), ("dom_0", "dom_1", "dom_2", "sub")
     )
     return jax.shard_map(
         per_device,

time: 313 us -> 228 us (0.73)
  starting transfers between devices: 71.1 us -> 13.5 us
  blocking collectives: 140 us -> 86.5 us
  between operations: 13.7 us -> 47.8 us
  waiting for transfers between devices: 27.2 us -> 17.1 us
  local copies, waits for them, and re-layouts: 34.4 us -> 40.4 us
    psum x12 -> x0, blocking collectives: 140 us -> none  [one_axis_at_a_time(): return functools.reduce(lax.psum, axes, shard)]
    all_gather x0 -> x16, blocking collectives: none -> 86.5 us  [pair_sum(): lax.all_gather(layer, axes, axis_index_groups=pair_groups(axes, offset))]
    ppermute x16 -> x0, starting transfers between devices: 71.1 us -> none  [the longest x8 42.8 us: extended(): lax.ppermute(lax.slice_in_dim(block, 0, width, axis=dim), axis, backward)]
    ppermute x16 -> x0, waiting for transfers between devices: 27.2 us -> none  [the longest x8 25.7 us: extended(): lax.ppermute(lax.slice_in_dim(block, block.shape[dim] - width, None, axis...]
    all_to_all x0 -> x2, waiting for transfers between devices: none -> 17.1 us  [total(): values = jnp.sum(lax.all_to_all(spread, axes, 0, 0, tiled=True), 0)]
    all_to_all x0 -> x2, starting transfers between devices: none -> 13.5 us  [total(): values = jnp.sum(lax.all_to_all(spread, axes, 0, 0, tiled=True), 0)]
    another operation x0 -> x1, local copies, waits for them, and re-layouts: none -> 5.73 us  [per_device(): products = jnp.stack([jnp.sum(owned[i] * owned[j]) for i, j in PAIRS])]
  transfers between devices with their start and end apart: 16 -> 2, of which waited for: 9 -> 2; matrix products, arithmetic and copies ran while one was open for 1% -> 0% of each run, Pallas kernels for 0% -> 0%
where the time goes in v1:
time: 228 us; the launch traced here: 226 us
  blocking collectives  86.5 us (38%)
  between operations  47.8 us (21%)
  local copies, waits for them, and re-layouts  40.4 us (18%)
  waiting for transfers between devices  17.1 us (8%)
  starting transfers between devices  13.5 us (6%)
  matrix products  12.2 us (5%)
  other arithmetic  9.07 us (4%)
    all_gather x16, blocking collectives, pair_sum(): lax.all_gather(layer, axes, axis_index_groups=pair_groups(axes, offset))  86.5 us
    slice x135, local copies, waits for them, and re-layouts, zone_corners(): by_depth[shift_z]  26.3 us
    all_to_all x2, waiting for transfers between devices, total(): values = jnp.sum(lax.all_to_all(spread, axes, 0, 0, tiled=True), 0)  17.1 us
    all_to_all x2, starting transfers between devices, total(): values = jnp.sum(lax.all_to_all(spread, axes, 0, 0, tiled=True), 0)  13.5 us
    another operation x1, local copies, waits for them, and re-layouts, per_device(): products = jnp.stack([jnp.sum(owned[i] * owned[j]) for i, j in PAIRS])  5.73 us
  transfers between devices with their start and end apart: 2, of which 2 were waited for; matrix products, arithmetic and copies ran while one was open for 0% of the time, Pallas kernels for 0%

profile of v1, /device:TPU:1, one launch (start us, length us, event | category | flops | bytes accessed | tf_op | source)
XLA Modules:
  0.0 226.5 jit_solution(14832472052091449163)
XLA Ops:
  0.7 1.4 convolution_bitcast_fusion.9
  7.9 1.1 fusion
  9.3 0.7 copy-done.4
  10.0 0.5 convolution_bitcast_fusion.5
  16.6 0.6 copy-done.2
  17.9 0.5 fusion.9
  18.4 0.8 fusion.29
  19.2 1.2 fusion.91
  20.4 1.5 fusion.156
  21.9 1.6 add_reduce_fusion
  23.8 1.1 fusion.2
  25.2 0.8 convolution_bitcast_fusion.4
  27.3 15.0 %all-gather = f32[6,5,1,128]{3,2,1,0:T(1,128)S(1)} all-gather(f32[3,5,1,128]{3,2,1,0:T(1,128)S(1)} %get-tuple-element.98), channel_id=2, replica_groups={{1,2},{3,4},{5,6},{7,8},{9,10},{11,0},{13,14},{15,16},{17,18},{19,20},{..., dimensions={0}, use_global_device_ids=true | all-gather | bytes 23040 | tf_op jit(solution)/shard_map/all_gather | solution.py:30
  42.2 3.2 %all-gather.1 = f32[6,5,1,128]{3,2,1,0:T(1,128)S(1)} all-gather(f32[3,5,1,128]{3,2,1,0:T(1,128)S(1)} %get-tuple-element.97), channel_id=3, replica_groups={{0,1},{2,3},{4,5},{6,7},{8,9},{10,11},{12,13},{14,15},{16,17},{18,19},{..., dimensions={0}, use_global_device_ids=true | all-gather | bytes 23040 | tf_op jit(solution)/shard_map/all_gather | solution.py:30
  45.6 5.9 %all-gather.2 = f32[6,1,9,128]{3,1,2,0:T(1,128)S(1)} all-gather(f32[3,1,9,128]{3,1,2,0:T(1,128)S(1)} %copy.338), channel_id=4, replica_groups={{12,24},{36,48},{60,72},{84,96},{108,120},{132,144},{156,168},{180,192}..., dimensions={0}, use_global_device_ids=true | all-gather | bytes 41472 | tf_op jit(solution)/shard_map/all_gather | solution.py:30
  51.5 5.5 %all-gather.3 = f32[6,1,9,128]{3,1,2,0:T(1,128)S(1)} all-gather(f32[3,1,9,128]{3,1,2,0:T(1,128)S(1)} %copy.341), channel_id=5, replica_groups={{0,12},{24,36},{48,60},{72,84},{96,108},{120,132},{144,156},{168,180},{..., dimensions={0}, use_global_device_ids=true | all-gather | bytes 41472 | tf_op jit(solution)/shard_map/all_gather | solution.py:30
  56.9 0.5 convolution_bitcast_fusion.8
  63.6 0.5 fusion.5
  64.1 0.5 fusion.171
  65.8 4.7 %all-gather.4 = f32[6,5,1,128]{3,2,1,0:T(1,128)S(1)} all-gather(f32[3,5,1,128]{3,2,1,0:T(1,128)S(1)} %get-tuple-element.96), channel_id=6, replica_groups={{1,2},{3,4},{5,6},{7,8},{9,10},{11,0},{13,14},{15,16},{17,18},{19,20},{..., dimensions={0}, use_global_device_ids=true | all-gather | bytes 23040 | tf_op jit(solution)/shard_map/all_gather | solution.py:30
  70.6 3.2 %all-gather.5 = f32[6,5,1,128]{3,2,1,0:T(1,128)S(1)} all-gather(f32[3,5,1,128]{3,2,1,0:T(1,128)S(1)} %get-tuple-element.95), channel_id=7, replica_groups={{0,1},{2,3},{4,5},{6,7},{8,9},{10,11},{12,13},{14,15},{16,17},{18,19},{..., dimensions={0}, use_global_device_ids=true | all-gather | bytes 23040 | tf_op jit(solution)/shard_map/all_gather | solution.py:30
  73.9 3.8 %all-gather.6 = f32[6,1,9,128]{3,1,2,0:T(1,128)S(1)} all-gather(f32[3,1,9,128]{3,1,2,0:T(1,128)S(1)} %copy.357), channel_id=8, replica_groups={{12,24},{36,48},{60,72},{84,96},{108,120},{132,144},{156,168},{180,192}..., dimensions={0}, use_global_device_ids=true | all-gather | bytes 41472 | tf_op jit(solution)/shard_map/all_gather | solution.py:30
  77.8 7.2 %all-gather.7 = f32[6,1,9,128]{3,1,2,0:T(1,128)S(1)} all-gather(f32[3,1,9,128]{3,1,2,0:T(1,128)S(1)} %copy.360), channel_id=9, replica_groups={{0,12},{24,36},{48,60},{72,84},{96,108},{120,132},{144,156},{168,180},{..., dimensions={0}, use_global_device_ids=true | all-gather | bytes 41472 | tf_op jit(solution)/shard_map/all_gather | solution.py:30
  85.0 0.5 convolution_bitcast_fusion.7
  91.3 0.5 fusion.4
  91.8 0.5 fusion.172
  93.6 4.7 %all-gather.8 = f32[6,5,1,128]{3,2,1,0:T(1,128)S(1)} all-gather(f32[3,5,1,128]{3,2,1,0:T(1,128)S(1)} %get-tuple-element.94), channel_id=10, replica_groups={{1,2},{3,4},{5,6},{7,8},{9,10},{11,0},{13,14},{15,16},{17,18},{19,20},{..., dimensions={0}, use_global_device_ids=true | all-gather | bytes 23040 | tf_op jit(solution)/shard_map/all_gather | solution.py:30
  98.3 3.2 %all-gather.9 = f32[6,5,1,128]{3,2,1,0:T(1,128)S(1)} all-gather(f32[3,5,1,128]{3,2,1,0:T(1,128)S(1)} %get-tuple-element.93), channel_id=11, replica_groups={{0,1},{2,3},{4,5},{6,7},{8,9},{10,11},{12,13},{14,15},{16,17},{18,19},{..., dimensions={0}, use_global_device_ids=true | all-gather | bytes 23040 | tf_op jit(solution)/shard_map/all_gather | solution.py:30
  101.7 3.8 %all-gather.10 = f32[6,1,9,128]{3,1,2,0:T(1,128)S(1)} all-gather(f32[3,1,9,128]{3,1,2,0:T(1,128)S(1)} %copy.375), channel_id=12, replica_groups={{12,24},{36,48},{60,72},{84,96},{108,120},{132,144},{156,168},{180,192}..., dimensions={0}, use_global_device_ids=true | all-gather | bytes 41472 | tf_op jit(solution)/shard_map/all_gather | solution.py:30
  105.5 7.2 %all-gather.11 = f32[6,1,9,128]{3,1,2,0:T(1,128)S(1)} all-gather(f32[3,1,9,128]{3,1,2,0:T(1,128)S(1)} %copy.378), channel_id=13, replica_groups={{0,12},{24,36},{48,60},{72,84},{96,108},{120,132},{144,156},{168,180},{..., dimensions={0}, use_global_device_ids=true | all-gather | bytes 41472 | tf_op jit(solution)/shard_map/all_gather | solution.py:30
  112.8 0.5 convolution_bitcast_fusion.6
  119.6 0.5 fusion.173
  121.4 4.7 %all-gather.12 = f32[6,5,1,128]{3,2,1,0:T(1,128)S(1)} all-gather(f32[3,5,1,128]{3,2,1,0:T(1,128)S(1)} %get-tuple-element.92), channel_id=14, replica_groups={{1,2},{3,4},{5,6},{7,8},{9,10},{11,0},{13,14},{15,16},{17,18},{19,20},{..., dimensions={0}, use_global_device_ids=true | all-gather | bytes 23040 | tf_op jit(solution)/shard_map/all_gather | solution.py:30
  126.1 3.2 %all-gather.13 = f32[6,5,1,128]{3,2,1,0:T(1,128)S(1)} all-gather(f32[3,5,1,128]{3,2,1,0:T(1,128)S(1)} %get-tuple-element.91), channel_id=15, replica_groups={{0,1},{2,3},{4,5},{6,7},{8,9},{10,11},{12,13},{14,15},{16,17},{18,19},{..., dimensions={0}, use_global_device_ids=true | all-gather | bytes 23040 | tf_op jit(solution)/shard_map/all_gather | solution.py:30
  129.4 3.8 %all-gather.14 = f32[6,1,9,128]{3,1,2,0:T(1,128)S(1)} all-gather(f32[3,1,9,128]{3,1,2,0:T(1,128)S(1)} %copy.393), channel_id=16, replica_groups={{12,24},{36,48},{60,72},{84,96},{108,120},{132,144},{156,168},{180,192}..., dimensions={0}, use_global_device_ids=true | all-gather | bytes 41472 | tf_op jit(solution)/shard_map/all_gather | solution.py:30
  133.3 7.2 %all-gather.15 = f32[6,1,9,128]{3,1,2,0:T(1,128)S(1)} all-gather(f32[3,1,9,128]{3,1,2,0:T(1,128)S(1)} %copy.396), channel_id=17, replica_groups={{0,12},{24,36},{48,60},{72,84},{96,108},{120,132},{144,156},{168,180},{..., dimensions={0}, use_global_device_ids=true | all-gather | bytes 41472 | tf_op jit(solution)/shard_map/all_gather | solution.py:30
  140.5 0.7 multiply_reduce_fusion
  141.2 5.7 %stack.672 = f32[9]{0:T(128)S(1)} concatenate(f32[1]{0:T(128)} %bitcast.72, f32[1]{0:T(128)} %bitcast.123, f32[1]{0:T(128)} %bitcast.171, f32[1]{0:T(128)} %bitcast.218, f32[1]{0:T(128)} %bitcast.219, f32[1]{0:T(128)} %bitcast.220, f32[1]{0:T(128)} %bitcast.221, f32[1]{0:T(128)} %bitcast.222, f32[1]{0:T(128)} %bitcast.223), dimensions={0} | concatenate | bytes 72 | tf_op jit(solution)/shard_map/stack | solution.py:310
  147.0 0.6 broadcast_in_dim.27
  147.6 8.0 %all-to-all-start = ((f32[64,1,16]{2,1,0:T(1,128)}), f32[64,1,16]{2,1,0:T(1,128)S(1)}, u32[]{:S(2)}, u32[]{:S(2)}) async-start(f32[64,1,16]{2,1,0:T(1,128)} %broadcast_in_dim.27), calls=%async_computation | async-start | bytes 65536 | tf_op jit(solution)/shard_map/all_to_all | solution.py:53
  155.9 9.1 %all-to-all-done = f32[64,1,16]{2,1,0:T(1,128)S(1)} async-done(((f32[64,1,16]{2,1,0:T(1,128)}), f32[64,1,16]{2,1,0:T(1,128)S(1)}, u32[]{:S(2)}, u32[]{:S(2)}) %all-to-all-start) | async-done | bytes 4128 | tf_op jit(solution)/shard_map/all_to_all | solution.py:53
  165.1 0.6 broadcast_in_dim.28
  165.7 5.4 %all-to-all-start.1 = ((f32[12,1,16]{2,1,0:T(1,128)}), f32[12,1,16]{2,1,0:T(1,128)S(1)}, u32[]{:S(2)}, u32[]{:S(2)}) async-start(f32[12,1,16]{2,1,0:T(1,128)} %broadcast_in_dim.28), calls=%async_computation.1 | async-start | bytes 12288 | tf_op jit(solution)/shard_map/all_to_all | solution.py:53
  171.3 0.6 copy.407
  172.0 8.0 %all-to-all-done.1 = f32[12,1,16]{2,1,0:T(1,128)S(1)} async-done(((f32[12,1,16]{2,1,0:T(1,128)}), f32[12,1,16]{2,1,0:T(1,128)S(1)}, u32[]{:S(2)}, u32[]{:S(2)}) %all-to-all-start.1) | async-done | bytes 800 | tf_op jit(solution)/shard_map/all_to_all | solution.py:53
  180.0 0.7 fusion.170
  225.1 0.7 copy.405
  225.8 0.7 copy.406
  (425 shorter events, 35.2 us)
Async XLA Ops:
  0.6 16.7 %copy-start = (f32[8,2,4,64]{3,2,1,0:T(4,128)S(1)}, f32[8,2,4,64]{3,2,1,0:T(4,128)}, u32[]{:S(2)}) copy-start(f32[8,2,4,64]{3,2,1,0:T(4,128)} %param.16) | copy-start | bytes 49156
  0.7 7.3 %copy-start.3 = (f32[3,27,27,1,1,1]{2,1,0,5,4,3:T(8,128)S(1)}, f32[3,27,27,1,1,1]{2,1,0,5,4,3:T(8,128)}, u32[]{:S(2)}) copy-start(f32[3,27,27,1,1,1]{2,1,0,5,4,3:T(8,128)} %constant.160) | copy-start | bytes 26248
  9.1 0.9 copy-start.4
  16.3 0.9 copy-start.2
  16.5 0.9 copy-start.6
  16.5 1.3 copy-start.5
  16.5 1.2 copy-start.7
  16.5 1.2 copy-start.11
  16.5 1.3 copy-start.8
  16.5 1.3 copy-start.9
  16.6 1.3 copy-start.10
  23.6 1.3 copy-start.12
  57.5 6.1 %copy-start.1 = (f32[27,27,1,1,1]{1,0,4,3,2:T(8,128)S(1)}, f32[27,27,1,1,1]{1,0,4,3,2:T(8,128)}, u32[]{:S(2)}) copy-start(f32[27,27,1,1,1]{1,0,4,3,2:T(8,128)} %constant.162) | copy-start | bytes 8752
  147.6 17.4 %all-to-all-start = ((f32[64,1,16]{2,1,0:T(1,128)}), f32[64,1,16]{2,1,0:T(1,128)S(1)}, u32[]{:S(2)}, u32[]{:S(2)}) async-start(f32[64,1,16]{2,1,0:T(1,128)} %broadcast_in_dim.27), calls=%async_computation | async-start | bytes 65536 | tf_op jit(solution)/shard_map/all_to_all | solution.py:53
  165.7 14.3 %all-to-all-start.1 = ((f32[12,1,16]{2,1,0:T(1,128)}), f32[12,1,16]{2,1,0:T(1,128)S(1)}, u32[]{:S(2)}, u32[]{:S(2)}) async-start(f32[12,1,16]{2,1,0:T(1,128)} %broadcast_in_dim.28), calls=%async_computation.1 | async-start | bytes 12288 | tf_op jit(solution)/shard_map/all_to_all | solution.py:53

commit v2 on v1

v2 whole, which is shorter than its diff:
```python
import functools
import math

import jax
import jax.numpy as jnp
from jax import lax
from jax.experimental import pallas as pl
from jax.experimental.pallas import tpu as pltpu
from jax.sharding import Mesh
from jax.sharding import PartitionSpec as P

MATS = 4
EQ_ITERS = 4
CG_ITERS = 3
DOM_SUB = ("dom_0", "dom_1", "dom_2", "sub")
DOM = ("dom_0", "dom_1", "dom_2")


gammas = (1.4, 1.67, 2.0, 3.0)
cold_terms = (0.3, 1.2, 0.6, 2.4)
highest = lax.Precision.HIGHEST


def pair_groups(axes, offset):
    count = 1
    for axis in axes:
        count *= lax.axis_size(axis)
    return [[(i + offset) % count, (i + offset + 1) % count] for i in range(0, count, 2)]


def pair_sum(layer, axes, offset):
    gathered = lax.all_gather(layer, axes, axis_index_groups=pair_groups(axes, offset))
    return gathered[0] + gathered[1]


def join_axis(block, axes, dim):
    even = lax.axis_index(axes) % 2 == 0
    last = block.shape[dim] - 1
    low = lax.slice_in_dim(block, 0, 1, axis=dim)
    high = lax.slice_in_dim(block, last, last + 1, axis=dim)
    inner = pair_sum(jnp.where(even, high, low), axes, 0)
    outer = pair_sum(jnp.where(even, low, high), axes, 1)
    middle = lax.slice_in_dim(block, 1, last, axis=dim)
    return jnp.concatenate(
        [jnp.where(even, outer, inner), middle, jnp.where(even, inner, outer)], dim
    )


def total(values):
    for axes in (DOM, ("sub",)):
        count = 1
        for axis in axes:
            count *= lax.axis_size(axis)
        spread = jnp.broadcast_to(values[None], (count, values.shape[0]))
        gathered = lax.all_to_all(spread, axes, 0, 0, tiled=True)
        values = jnp.sum(gathered, 0)
    return gathered


ROOT = math.sqrt(0.15)
POINTS = (0.5 - ROOT, 0.5, 0.5 + ROOT)
QUAD = (5.0 / 18.0, 8.0 / 18.0, 5.0 / 18.0)
VALUE = tuple((2.0 * (t - 0.5) * (t - 1.0), -4.0 * t * (t - 1.0), 2.0 * t * (t - 0.5)) for t in POINTS)
SLOPE = tuple((4.0 * t - 3.0, 4.0 - 8.0 * t, 4.0 * t - 1.0) for t in POINTS)
LINEAR = tuple((1.0 - t, t) for t in POINTS)


def value_of(nodes):
    first, middle, last = nodes
    a, b, c = VALUE[0]
    scaled = b * middle
    return (a * first + scaled + c * last, middle, c * first + scaled + a * last)


def value_back(points):
    first, middle, last = points
    a, b, c = VALUE[0]
    return (a * first + c * last, b * (first + last) + middle, c * first + a * last)


def slope_of(nodes):
    first, middle, last = nodes
    a, b, c = SLOPE[0]
    scaled = b * middle
    return (a * first + scaled + c * last, last - first, -c * first - scaled - a * last)


def slope_back(points):
    first, middle, last = points
    a, b, c = SLOPE[0]
    return (a * first - middle - c * last, b * (first - last), c * first + middle - a * last)


def turn(array, shift):
    return pltpu.roll(array, shift % array.shape[-1], array.ndim - 1)


def even_lanes(rows):
    return lax.broadcasted_iota(jnp.int32, (rows, 128), 1) % 2 == 0


def depth_value(nodes, even, one, two):
    a, b, c = VALUE[0]
    scaled = b * one
    return jnp.where(even, a * nodes + scaled + c * two, nodes), c * nodes + scaled + a * two


def depth_value_back(near, far, even):
    a, b, c = VALUE[0]
    near_even = jnp.where(even, near, 0.0)
    ahead = turn(b * (near_even + far), 1) + turn(c * near_even + a * far, 2)
    return jnp.where(even, a * near + c * far, near) + ahead


def corners(ref, c, packs, rows):
    out = []
    for i in range(3):
        line = []
        for j in range(3):
            parts = [ref[c, 2 * zone + i, pl.ds(j, rows, stride=2), :] for zone in packs]
            line.append(parts[0] if len(parts) == 1 else jnp.concatenate(parts, 0))
        out.append(line)
    return out


def scatter(ref, c, packs, rows, nodes):
    for i in range(3):
        for j in range(3):
            for at, zone in enumerate(packs):
                part = nodes[i][j][at * rows : (at + 1) * rows]
                spot = (c, 2 * zone + i, pl.ds(j, rows, stride=2), slice(None))
                ref[spot] = ref[spot] + part


def mass_nodes(nodes, near_mass, far_mass, even):
    near = [[None] * 3 for _ in range(3)]
    far = [[None] * 3 for _ in range(3)]
    for i in range(3):
        for j in range(3):
            u = nodes[i][j]
            near[i][j], far[i][j] = depth_value(u, even, turn(u, -1), turn(u, -2))
    sides = []
    for field, mass in ((near, near_mass), (far, far_mass)):
        field = [value_of(line) for line in field]
        field = [value_of([field[i][j] for i in range(3)]) for j in range(3)]
        field = [[field[j][i] * mass[3 * i + j] for j in range(3)] for i in range(3)]
        field = [value_back(line) for line in field]
        field = [value_back([field[i][j] for i in range(3)]) for j in range(3)]
        sides.append(field)
    return [[depth_value_back(sides[0][j][i], sides[1][j][i], even) for j in range(3)] for i in range(3)]


def spread_tables():
    zone = lax.broadcasted_iota(jnp.int32, (64, 128), 0)
    lane = lax.broadcasted_iota(jnp.int32, (64, 128), 1)
    one, zero = jnp.float32(1.0), jnp.float32(0.0)
    even = jnp.where(lane == 2 * zone, one, zero)
    odd = jnp.where(lane == 2 * zone + 1, one, zero)
    return even, odd


def collect_tables(which):
    lane = lax.broadcasted_iota(jnp.int32, (128, 64), 0)
    zone = lax.broadcasted_iota(jnp.int32, (128, 64), 1)
    even, odd = lane == 2 * zone, lane == 2 * zone + 1
    near = jnp.where(even, LINEAR[0][which], jnp.where(odd, LINEAR[1][which], 0.0))
    far = jnp.where(even, LINEAR[2][which], 0.0)
    return near.astype(jnp.float32), far.astype(jnp.float32)


def dot32(left, right):
    return jnp.dot(left, right, precision=highest, preferred_element_type=jnp.float32)


def force_kernel(disp, vel, energy, rho, share, portion, ident, mix, force, rate, near_out, far_out, grad, work):
    packs, rows = (0, 1), energy.shape[2]
    count = 2 * rows
    even = even_lanes(count)

    def packed(ref, at):
        return jnp.concatenate([ref[at, 0], ref[at, 1]], 0)

    even_table, odd_table = spread_tables()
    both_table = even_table + odd_table
    material = jnp.concatenate([ident[0], ident[1]], 0)
    present = [
        jnp.where((packed(mix, m) == 1) | (material == m), 1.0, 0.0).astype(jnp.float32) for m in range(MATS)
    ]
    weighted = [present[m] * packed(share, m) for m in range(MATS)]
    weight_sum = weighted[0] + weighted[1] + weighted[2] + weighted[3]
    present_sum = present[0] + present[1] + present[2] + present[3]
    zone_rows = [
        (gammas[m] - 1.0) * (weighted[m] / weight_sum * packed(portion, m)) for m in range(MATS)
    ]
    zone_rows += [present[m] / present_sum for m in range(MATS)]
    zone_rows += [packed(energy, j) for j in range(8)]
    wide = dot32(jnp.concatenate(zone_rows, 0), both_table)
    wide = [wide[count * k : count * (k + 1)] for k in range(16)]
    loads, start, corner_energy = wide[:4], wide[4:8], wide[8:]
    rho_rows = [jnp.concatenate([packed(rho, 3 * p + k) for p in range(9)], 0) for k in range(3)]
    near_rho = dot32(rho_rows[0], even_table) + dot32(rho_rows[1], odd_table)
    far_rho = dot32(rho_rows[2], even_table)
    near_rho = [near_rho[count * p : count * (p + 1)] for p in range(9)]
    far_rho = [far_rho[count * p : count * (p + 1)] for p in range(9)]
    near_weight = jnp.where(even, QUAD[0], QUAD[1])
    far_weight = jnp.where(even, QUAD[2], 0.0)
    near_point = jnp.where(even, POINTS[0], POINTS[1])
    a, b, c = SLOPE[0]

    for field, ref in enumerate((disp, vel)):
        for comp in range(3):
            nodes = corners(ref, comp, packs, rows)
            values = [[None] * 3 for _ in range(3)], [[None] * 3 for _ in range(3)]
            slopes = [[None] * 3 for _ in range(3)], [[None] * 3 for _ in range(3)]
            for i in range(3):
                for j in range(3):
                    u = nodes[i][j]
                    one, two = turn(u, -1), turn(u, -2)
                    near, far = depth_value(u, even, one, two)
                    values[0][i][j], values[1][i][j] = near, jnp.where(even, far, 0.0)
                    scaled = b * one
                    slopes[0][i][j] = jnp.where(even, a * u + scaled + c * two, one - turn(u, 1))
                    slopes[1][i][j] = jnp.where(even, -c * u - scaled - a * two, 0.0)
            for side in range(2):
                plain = [value_of(line) for line in values[side]]
                sloped = [slope_of(line) for line in values[side]]
                deep = [value_of(line) for line in slopes[side]]
                for j in range(3):
                    along = (
                        slope_of([plain[i][j] for i in range(3)]),
                        value_of([sloped[i][j] for i in range(3)]),
                        value_of([deep[i][j] for i in range(3)]),
                    )
                    for d in range(3):
                        for i in range(3):
                            grad[field, side, 3 * i + j, 3 * comp + d] = along[d][i]

    for i in range(3):
        for j in range(3):
            spot = 3 * i + j
            plane = QUAD[i] * QUAD[j]
            mixed = []
            for k in range(2):
                low = LINEAR[j][0] * corner_energy[k] + LINEAR[j][1] * corner_energy[2 + k]
                high = LINEAR[j][0] * corner_energy[4 + k] + LINEAR[j][1] * corner_energy[6 + k]
                mixed.append(LINEAR[i][0] * low + LINEAR[i][1] * high)
            rise = mixed[1] - mixed[0]
            for side in range(2):
                weight = plane * (near_weight if side == 0 else far_weight)
                density_weight = near_rho[spot] if side == 0 else far_rho[spot]
                point = near_point if side == 0 else POINTS[2]
                jac = [[grad[0, side, spot, 3 * cc + d] + (1.0 if cc == d else 0.0) for d in range(3)] for cc in range(3)]
                adj = [
                    [
                        jac[(line + 1) % 3][(col + 1) % 3] * jac[(line + 2) % 3][(col + 2) % 3]
                        - jac[(line + 1) % 3][(col + 2) % 3] * jac[(line + 2) % 3][(col + 1) % 3]
                        for line in range(3)
                    ]
                    for col in range(3)
                ]
                determinant = jac[0][0] * adj[0][0] + jac[0][1] * adj[1][0] + jac[0][2] * adj[2][0]
                scale = density_weight / determinant * (mixed[0] + point * rise)
                load = [loads[m] * scale for m in range(MATS)]
                fraction = list(start)
                for _ in range(EQ_ITERS):
                    grown = [
                        jnp.sqrt(fraction[m] * (load[m] + cold_terms[m] * fraction[m])) for m in range(MATS)
                    ]
                    inverse = 1.0 / (grown[0] + grown[1] + grown[2] + grown[3])
                    fraction = [grown[m] * inverse for m in range(MATS)]
                terms = [load[m] + cold_terms[m] * fraction[m] for m in range(MATS)]
                stress = weight * (terms[0] + terms[1] + terms[2] + terms[3])
                divergence = 0.0
                for cc in range(3):
                    for d in range(3):
                        divergence = divergence + grad[1, side, spot, 3 * cc + d] * adj[d][cc]
                work[side, spot] = stress * divergence
                for cc in range(3):
                    for d in range(3):
                        grad[0, side, spot, 3 * cc + d] = stress * adj[d][cc]
                (near_out if side == 0 else far_out)[spot] = weight * density_weight

    force[...] = jnp.zeros_like(force)
    for comp in range(3):
        plain = [[None] * 3 for _ in range(3)], [[None] * 3 for _ in range(3)]
        deep = [[None] * 3 for _ in range(3)], [[None] * 3 for _ in range(3)]
        for side in range(2):
            lines = []
            for j in range(3):
                part = [[grad[0, side, 3 * i + j, 3 * comp + d] for i in range(3)] for d in range(3)]
                lines.append((slope_back(part[0]), value_back(part[1]), value_back(part[2])))
            for i in range(3):
                first = value_back([lines[j][0][i] for j in range(3)])
                second = slope_back([lines[j][1][i] for j in range(3)])
                third = value_back([lines[j][2][i] for j in range(3)])
                for j in range(3):
                    plain[side][i][j] = first[j] + second[j]
                    deep[side][i][j] = third[j]
        out = [[None] * 3 for _ in range(3)]
        va, vb, vc = VALUE[0]
        for i in range(3):
            for j in range(3):
                near, far = plain[0][i][j], plain[1][i][j]
                near_s, far_s = deep[0][i][j], deep[1][i][j]
                near_even = jnp.where(even, near, 0.0)
                near_s_even = jnp.where(even, near_s, 0.0)
                here = jnp.where(even, va * near + vc * far + a * near_s - c * far_s, near)
                next_one = jnp.where(even, vb * (near + far) + b * (near_s - far_s), near_s)
                next_two = vc * near_even + va * far + c * near_s_even - a * far_s
                behind = jnp.where(even, 0.0, near_s)
                out[i][j] = here + turn(next_one, 1) + turn(next_two, 2) - turn(behind, -1)
        scatter(force, comp, packs, rows, out)

    def collected(read):
        lines = [[], []]
        for side in range(2):
            for jx in range(2):
                for jy in range(2):
                    value = None
                    for i in range(3):
                        inner = None
                        for j in range(3):
                            term = LINEAR[j][jy] * read(side, 3 * i + j)
                            inner = term if inner is None else inner + term
                        inner = LINEAR[i][jx] * inner
                        value = inner if value is None else value + inner
                    lines[side].append(value)
        near, far = jnp.concatenate(lines[0], 0), jnp.concatenate(lines[1], 0)
        out = []
        for jz in range(2):
            near_table, far_table = collect_tables(jz)
            out.append(dot32(near, near_table) + dot32(far, far_table))
        return out

    done = collected(lambda side, spot: work[side, spot])
    lumped = collected(lambda side, spot: (near_out if side == 0 else far_out)[spot])
    for jz in range(2):
        ratio = -done[jz] / lumped[jz]
        for jxy in range(4):
            for zone in range(2):
                base = count * jxy + rows * zone
                rate[2 * jxy + jz, zone] = ratio[base : base + rows]


def mass_kernel(first, image, older, old, near_mass, far_mass, new, partial):
    packs, rows = (0, 1), near_mass.shape[1] // 2
    even = even_lanes(2 * rows)
    if first == 0:
        new[...] = image[...]
    elif first == 1:
        new[...] = (1.0 / HALF_WIDTH) * image[...] - (CENTER / HALF_WIDTH) * old[...]
    else:
        new[...] = (2.0 / HALF_WIDTH) * image[...] - (2.0 * CENTER / HALF_WIDTH) * old[...] - older[...]
    near = [near_mass[p] for p in range(9)]
    far = [far_mass[p] for p in range(9)]
    partial[...] = jnp.zeros_like(partial)
    for comp in range(3):
        nodes = corners(new, comp, packs, rows)
        scatter(partial, comp, packs, rows, mass_nodes(nodes, near, far, even))


def product_kernel(image, t0, t1, t2, t3, products):
    t3[...] = (2.0 / HALF_WIDTH) * image[...] - (2.0 * CENTER / HALF_WIDTH) * t2[...] - t1[...]
    refs = (t0, t1, t2, t3)
    wide, tall = image.shape[1], image.shape[2]
    lane = lax.broadcasted_iota(jnp.int32, (1, 128), 1)
    sums = [None] * len(PAIRS)
    for comp in range(3):
        for x in range(wide - 1):
            parts = [ref[comp, x, 0 : tall - 1, :] for ref in refs]
            for at, (i, j) in enumerate(PAIRS):
                term = parts[i] * parts[j]
                sums[at] = term if sums[at] is None else sums[at] + term
    row = jnp.zeros((1, 128), jnp.float32)
    for at in range(len(PAIRS)):
        value = jnp.sum(jnp.sum(sums[at], 0, keepdims=True), 1, keepdims=True)
        row = jnp.where(lane == at, value, row)
    products[...] = row


def finish_kernel(gathered, t0, t1, t2, t3, accel, residual):
    row = jnp.sum(gathered[...], 0, keepdims=True)
    gram = {pair: row[:, at : at + 1] for at, pair in enumerate(PAIRS)}
    accel_of, residual_of = cg_coefficients(gram)
    fields = (t0, t1, t2, t3)
    wide = t0.shape[1]
    for comp in range(3):
        for x in range(wide):
            parts = [field[comp, x] for field in fields]
            accel[comp, x] = accel_of[0] * parts[0] + accel_of[1] * parts[1] + accel_of[2] * parts[2]
            residual[comp, x] = (
                residual_of[0] * parts[0] + residual_of[1] * parts[1] + residual_of[2] * parts[2] + residual_of[3] * parts[3]
            )


def local_call(kernel, name, outs, scratch=()):
    return pl.pallas_call(
        kernel,
        out_shape=[jax.ShapeDtypeStruct(shape, jnp.float32) for shape in outs],
        scratch_shapes=[pltpu.VMEM(shape, jnp.float32) for shape in scratch],
        name=name,
    )


def assemble(local_sum):
    return join_axis(join_axis(local_sum, ("sub",), 2), DOM, 1)


CENTER = 0.196
HALF_WIDTH = 0.194
PAIRS = ((0, 0), (0, 1), (0, 2), (0, 3), (1, 1), (1, 2), (1, 3), (2, 2), (2, 3))


def dot_in(gram, left, right):
    value = 0.0
    for i in range(4):
        for j in range(4):
            if left[i] is None or right[j] is None or (i == 3 and j == 3):
                continue
            value = value + gram[(min(i, j), max(i, j))] * left[i] * right[j]
    return value


def axpy(scale, left, right):
    out = []
    for a, b in zip(left, right):
        if a is None:
            out.append(b)
        elif b is None:
            out.append(scale * a)
        else:
            out.append(scale * a + b)
    return out


def mapped_coefficients(p):
    p0, p1, p2 = (0.0 if v is None else v for v in p[:3])
    shifted = [0.5 * p1, p0 + 0.5 * p2, 0.5 * p1, 0.5 * p2]
    return [HALF_WIDTH * b + CENTER * a for a, b in zip((p0, p1, p2, 0.0), shifted)]


def cg_coefficients(gram):
    accel = [0.0, 0.0, 0.0, 0.0]
    residual = [1.0, 0.0, 0.0, 0.0]
    direction = residual
    norm_now = gram[(0, 0)]
    for sweep_at in range(CG_ITERS):
        mapped = mapped_coefficients(direction)
        step = norm_now / dot_in(gram, direction, mapped)
        accel = axpy(step, direction, accel)
        residual = axpy(-step, mapped, residual)
        if sweep_at + 1 < CG_ITERS:
            norm_next = dot_in(gram, residual, residual)
            direction = axpy(norm_next / norm_now, direction, residual)
            norm_now = norm_next
    return accel, residual


def per_device(
    velocity, displacement, energy, rho_weight, mass_share, energy_share, material_id, mix_mask
):
    field = velocity.shape
    count = energy.shape[1] * energy.shape[2]
    mass = (9, count, 128)
    partial, energy_rate, near_mass, far_mass = local_call(
        force_kernel, "force", (field, energy.shape, mass, mass), ((2, 2, 9, 9, count, 128), (2, 9, count, 128))
    )(displacement, velocity, energy, rho_weight, mass_share, energy_share, material_id, mix_mask)
    image = assemble(partial)
    basis = [image, image]
    for at in range(CG_ITERS):
        new, partial = local_call(functools.partial(mass_kernel, at), f"mass_{at}", (field, field))(
            image, basis[-2], basis[-1], near_mass, far_mass
        )
        basis.append(new)
        image = assemble(partial)
    t0, t1, t2 = basis[2:]
    t3, products = local_call(product_kernel, "product", (field, (1, 128)))(image, t0, t1, t2)
    gathered = total(products[0, :16])
    accel, residual = local_call(finish_kernel, "finish", (field, field))(gathered, t0, t1, t2, t3)
    return (accel, residual, energy_rate)


def solution(mesh):
    torus = Mesh(
        mesh.devices.reshape(mesh.shape["dom"] // 8, 4, 2, mesh.shape["sub"]), ("dom_0", "dom_1", "dom_2", "sub")
    )
    return jax.shard_map(
        per_device,
        mesh=torus,
        in_specs=(
            P(None, DOM, "sub", None),
            P(None, DOM, "sub", None),
            P(None, DOM, "sub", None),
            P(None, DOM, "sub", None),
            P(None, DOM, "sub", None),
            P(None, DOM, "sub", None),
            P(DOM, "sub", None),
            P(None, DOM, "sub", None),
        ),
        out_specs=(P(None, DOM, "sub", None), P(None, DOM, "sub", None), P(None, DOM, "sub", None)),
        check_vma=False,
    )
```

time: 228 us -> 150 us (0.66)
  between operations: 47.8 us -> 0.85 us
  blocking collectives: 86.5 us -> 118 us
  local copies, waits for them, and re-layouts: 40.4 us -> 9.33 us
  waiting for transfers between devices: 17.1 us -> 0 us
  Pallas kernels: 0 us -> 14.3 us
  starting transfers between devices: 13.5 us -> 0 us
  matrix products: 12.2 us -> 0 us
  other arithmetic: 9.07 us -> 6.43 us
    all_to_all x0 -> x2, blocking collectives: none -> 34.3 us  [total(): gathered = lax.all_to_all(spread, axes, 0, 0, tiled=True)]
    slice x152 -> x1, local copies, waits for them, and re-layouts: 27.7 us -> 0.01 us  [per_device(): gathered = total(products[0, :16])]
    all_to_all x2 -> x0, waiting for transfers between devices: 17.1 us -> none  [total(): values = jnp.sum(lax.all_to_all(spread, axes, 0, 0, tiled=True), 0)]
    pallas_call x0 -> x6, Pallas kernels: none -> 14.3 us  [the longest x3 6.08 us: per_device(): local_call(functools.partial(mass_kernel, at), f'mass_{at}', (field, field))]
    all_to_all x2 -> x0, starting transfers between devices: 13.5 us -> none  [total(): values = jnp.sum(lax.all_to_all(spread, axes, 0, 0, tiled=True), 0)]
    dot_general x21 -> x0, matrix products: 12.2 us -> none  [the longest x5 3.59 us: zone_corners(): by_depth = jnp.einsum('cxyk,ksz->scxyz', nodes_in, table, precision=highest)]
    reduce_sum x10 -> x1, other arithmetic: 6.52 us -> 0.08 us  [total(): values = jnp.sum(gathered, 0)]
    another operation x14 -> x0, local copies, waits for them, and re-layouts: 6.32 us -> none  [the longest x1 5.73 us: per_device(): products = jnp.stack([jnp.sum(owned[i] * owned[j]) for i, j in PAIRS])]
  transfers between devices with their start and end apart: 2 -> 0, of which waited for: 2 -> 0; matrix products, arithmetic and copies ran while one was open for 0% -> 0% of each run, Pallas kernels for 0% -> 0%
where the time goes in v2:
time: 150 us; the launch traced here: 149 us
  blocking collectives  118 us (79%)
  Pallas kernels  14.3 us (10%)
  local copies, waits for them, and re-layouts  9.33 us (6%)
  other arithmetic  6.43 us (4%)
    all_gather x16, blocking collectives, pair_sum(): lax.all_gather(layer, axes, axis_index_groups=pair_groups(axes, offset))  83.5 us
    all_to_all x2, blocking collectives, total(): gathered = lax.all_to_all(spread, axes, 0, 0, tiled=True)  34.3 us
    pallas_call x3, Pallas kernels, per_device(): local_call(functools.partial(mass_kernel, at), f'mass_{at}', (field, field))  6.08 us
    unnamed x11, local copies, waits for them, and re-layouts  5.79 us
    pallas_call x1, Pallas kernels, per_device(): local_call(force_kernel, 'force', (field, energy.shape, mass, mass), ((2,...  3.79 us
    select_n x8, other arithmetic, join_axis(): inner = pair_sum(jnp.where(even, high, low), axes, 0)  3.54 us
    slice x4, local copies, waits for them, and re-layouts, join_axis(): middle = lax.slice_in_dim(block, 1, last, axis=dim)  3.35 us

profile of v2, /device:TPU:1, one launch (start us, length us, event | category | flops | bytes accessed | tf_op | source)
XLA Modules:
  0.0 148.8 jit_solution(13188910248516961320)
XLA Ops:
  0.7 0.0 copy-start.1
  0.7 1.6 %copy.72.vel = f32[3,5,9,128]{3,2,1,0:T(8,128)} copy(f32[3,5,9,128]{3,0,2,1:T(4,128)} %param.8) | data formatting | bytes 138240 | tf_op args[0]
  2.3 0.0 copy-done.1
  2.3 0.7 copy.71.disp
  2.9 3.8 %force.1 = (f32[3,5,9,128]{3,2,1,0:T(8,128)}, f32[8,2,4,64]{3,2,1,0:T(4,128)}, f32[9,8,128]{2,1,0:T(8,128)}, f32[9,8,128]{2,1,0:T(8,128)}) custom-call(f32[3,5,9,128]{3,2,1,0:T(8,128)} %copy.71.disp, f32[3,5,9,128]{3,2,1,0:T(8,128)} %copy.72.vel, f32[8,2,4,64]{3,2,1,0:T(4,128)} %energy.1, f32[27,2,4,64]{3,2,1,0:T(4,128)} %rho.1, f32[4,2,4,64]{3,2,1,0:T(4,128)} %share.1, ...), custom_call_target="tpu_custom_call" | custom-call | tf_op jit(solution)/shard_map/force/pallas_call | solution.py:465
  6.7 0.8 slice.179
  7.6 0.9 broadcast_select_fusion.13
  8.4 4.7 %all-gather.1 = f32[6,5,1,128]{3,2,1,0:T(1,128)S(1)} all-gather(f32[3,5,1,128]{3,2,1,0:T(1,128)S(1)} %get-tuple-element.61), channel_id=3, replica_groups={{0,1},{2,3},{4,5},{6,7},{8,9},{10,11},{12,13},{14,15},{16,17},{18,19},{..., dimensions={0}, use_global_device_ids=true | all-gather | bytes 23040 | tf_op jit(solution)/shard_map/all_gather | solution.py:32
  13.1 13.5 %all-gather = f32[6,5,1,128]{3,2,1,0:T(1,128)S(1)} all-gather(f32[3,5,1,128]{3,2,1,0:T(1,128)S(1)} %get-tuple-element.62), channel_id=2, replica_groups={{1,2},{3,4},{5,6},{7,8},{9,10},{11,0},{13,14},{15,16},{17,18},{19,20},{..., dimensions={0}, use_global_device_ids=true | all-gather | bytes 23040 | tf_op jit(solution)/shard_map/all_gather | solution.py:32
  26.7 4.2 %all-gather.3 = f32[6,1,9,128]{3,1,2,0:T(1,128)S(1)} all-gather(f32[3,1,9,128]{3,1,2,0:T(1,128)S(1)} %copy.76), channel_id=5, replica_groups={{0,12},{24,36},{48,60},{72,84},{96,108},{120,132},{144,156},{168,180},{..., dimensions={0}, use_global_device_ids=true | all-gather | bytes 41472 | tf_op jit(solution)/shard_map/all_gather | solution.py:32
  30.9 3.8 %all-gather.2 = f32[6,1,9,128]{3,1,2,0:T(1,128)S(1)} all-gather(f32[3,1,9,128]{3,1,2,0:T(1,128)S(1)} %copy.73), channel_id=4, replica_groups={{12,24},{36,48},{60,72},{84,96},{108,120},{132,144},{156,168},{180,192}..., dimensions={0}, use_global_device_ids=true | all-gather | bytes 41472 | tf_op jit(solution)/shard_map/all_gather | solution.py:32
  34.8 0.7 fusion.7.image.older.old
  35.5 2.0 %mass_0.1 = (f32[3,5,9,128]{3,2,1,0:T(8,128)}, f32[3,5,9,128]{3,2,1,0:T(8,128)}) custom-call(f32[3,5,9,128]{3,2,1,0:T(8,128)} %fusion.7.image.older.old, f32[3,5,9,128]{3,2,1,0:T(8,128)} %fusion.7.image.older.old, f32[3,5,9,128]{3,2,1,0:T(8,128)} %fusion.7.image.older.old, f32[9,8,128]{2,1,0:T(8,128)} %get-tuple-element.18.near_mass, ...), custom_call_target="tpu_custom_call" | custom-call | tf_op jit(solution)/shard_map/mass_0/pallas_call | solution.py:471
  37.5 0.9 broadcast_select_fusion.11
  38.4 0.8 slice.193
  39.2 3.2 %all-gather.5 = f32[6,5,1,128]{3,2,1,0:T(1,128)S(1)} all-gather(f32[3,5,1,128]{3,2,1,0:T(1,128)S(1)} %get-tuple-element.59), channel_id=7, replica_groups={{0,1},{2,3},{4,5},{6,7},{8,9},{10,11},{12,13},{14,15},{16,17},{18,19},{..., dimensions={0}, use_global_device_ids=true | all-gather | bytes 23040 | tf_op jit(solution)/shard_map/all_gather | solution.py:32
  42.4 4.7 %all-gather.4 = f32[6,5,1,128]{3,2,1,0:T(1,128)S(1)} all-gather(f32[3,5,1,128]{3,2,1,0:T(1,128)S(1)} %get-tuple-element.60), channel_id=6, replica_groups={{1,2},{3,4},{5,6},{7,8},{9,10},{11,0},{13,14},{15,16},{17,18},{19,20},{..., dimensions={0}, use_global_device_ids=true | all-gather | bytes 23040 | tf_op jit(solution)/shard_map/all_gather | solution.py:32
  47.2 7.5 %all-gather.7 = f32[6,1,9,128]{3,1,2,0:T(1,128)S(1)} all-gather(f32[3,1,9,128]{3,1,2,0:T(1,128)S(1)} %copy.82), channel_id=9, replica_groups={{0,12},{24,36},{48,60},{72,84},{96,108},{120,132},{144,156},{168,180},{..., dimensions={0}, use_global_device_ids=true | all-gather | bytes 41472 | tf_op jit(solution)/shard_map/all_gather | solution.py:32
  54.8 3.8 %all-gather.6 = f32[6,1,9,128]{3,1,2,0:T(1,128)S(1)} all-gather(f32[3,1,9,128]{3,1,2,0:T(1,128)S(1)} %copy.79), channel_id=8, replica_groups={{12,24},{36,48},{60,72},{84,96},{108,120},{132,144},{156,168},{180,192}..., dimensions={0}, use_global_device_ids=true | all-gather | bytes 41472 | tf_op jit(solution)/shard_map/all_gather | solution.py:32
  58.7 0.7 fusion.5.image
  59.3 2.0 %mass_1.1 = (f32[3,5,9,128]{3,2,1,0:T(8,128)}, f32[3,5,9,128]{3,2,1,0:T(8,128)}) custom-call(f32[3,5,9,128]{3,2,1,0:T(8,128)} %fusion.5.image, f32[3,5,9,128]{3,2,1,0:T(8,128)} %fusion.7.image.older.old, f32[3,5,9,128]{3,2,1,0:T(8,128)} %get-tuple-element.21.old.older.t0, f32[9,8,128]{2,1,0:T(8,128)} %get-tuple-element.18.near_mass, ...), custom_call_target="tpu_custom_call" | custom-call | tf_op jit(solution)/shard_map/mass_1/pallas_call | solution.py:471
  61.4 0.9 broadcast_select_fusion.9
  62.2 0.8 slice.207
  63.1 3.2 %all-gather.9 = f32[6,5,1,128]{3,2,1,0:T(1,128)S(1)} all-gather(f32[3,5,1,128]{3,2,1,0:T(1,128)S(1)} %get-tuple-element.57), channel_id=11, replica_groups={{0,1},{2,3},{4,5},{6,7},{8,9},{10,11},{12,13},{14,15},{16,17},{18,19},{..., dimensions={0}, use_global_device_ids=true | all-gather | bytes 23040 | tf_op jit(solution)/shard_map/all_gather | solution.py:32
  66.3 4.7 %all-gather.8 = f32[6,5,1,128]{3,2,1,0:T(1,128)S(1)} all-gather(f32[3,5,1,128]{3,2,1,0:T(1,128)S(1)} %get-tuple-element.58), channel_id=10, replica_groups={{1,2},{3,4},{5,6},{7,8},{9,10},{11,0},{13,14},{15,16},{17,18},{19,20},{..., dimensions={0}, use_global_device_ids=true | all-gather | bytes 23040 | tf_op jit(solution)/shard_map/all_gather | solution.py:32
  71.1 7.2 %all-gather.11 = f32[6,1,9,128]{3,1,2,0:T(1,128)S(1)} all-gather(f32[3,1,9,128]{3,1,2,0:T(1,128)S(1)} %copy.88), channel_id=13, replica_groups={{0,12},{24,36},{48,60},{72,84},{96,108},{120,132},{144,156},{168,180},{..., dimensions={0}, use_global_device_ids=true | all-gather | bytes 41472 | tf_op jit(solution)/shard_map/all_gather | solution.py:32
  78.3 3.8 %all-gather.10 = f32[6,1,9,128]{3,1,2,0:T(1,128)S(1)} all-gather(f32[3,1,9,128]{3,1,2,0:T(1,128)S(1)} %copy.85), channel_id=12, replica_groups={{12,24},{36,48},{60,72},{84,96},{108,120},{132,144},{156,168},{180,192}..., dimensions={0}, use_global_device_ids=true | all-gather | bytes 41472 | tf_op jit(solution)/shard_map/all_gather | solution.py:32
  82.1 0.7 fusion.3.image
  82.8 2.0 %mass_2.1 = (f32[3,5,9,128]{3,2,1,0:T(8,128)}, f32[3,5,9,128]{3,2,1,0:T(8,128)}) custom-call(f32[3,5,9,128]{3,2,1,0:T(8,128)} %fusion.3.image, f32[3,5,9,128]{3,2,1,0:T(8,128)} %get-tuple-element.21.old.older.t0, f32[3,5,9,128]{3,2,1,0:T(8,128)} %get-tuple-element.23.old.t1, f32[9,8,128]{2,1,0:T(8,128)} %get-tuple-element.18.near_mass, ...), custom_call_target="tpu_custom_call" | custom-call | tf_op jit(solution)/shard_map/mass_2/pallas_call | solution.py:471
  84.9 0.9 broadcast_select_fusion.7
  85.7 0.8 slice.221
  86.6 3.2 %all-gather.13 = f32[6,5,1,128]{3,2,1,0:T(1,128)S(1)} all-gather(f32[3,5,1,128]{3,2,1,0:T(1,128)S(1)} %get-tuple-element.55), channel_id=15, replica_groups={{0,1},{2,3},{4,5},{6,7},{8,9},{10,11},{12,13},{14,15},{16,17},{18,19},{..., dimensions={0}, use_global_device_ids=true | all-gather | bytes 23040 | tf_op jit(solution)/shard_map/all_gather | solution.py:32
  89.8 4.7 %all-gather.12 = f32[6,5,1,128]{3,2,1,0:T(1,128)S(1)} all-gather(f32[3,5,1,128]{3,2,1,0:T(1,128)S(1)} %get-tuple-element.56), channel_id=14, replica_groups={{1,2},{3,4},{5,6},{7,8},{9,10},{11,0},{13,14},{15,16},{17,18},{19,20},{..., dimensions={0}, use_global_device_ids=true | all-gather | bytes 23040 | tf_op jit(solution)/shard_map/all_gather | solution.py:32
  94.6 7.2 %all-gather.15 = f32[6,1,9,128]{3,1,2,0:T(1,128)S(1)} all-gather(f32[3,1,9,128]{3,1,2,0:T(1,128)S(1)} %copy.94), channel_id=17, replica_groups={{0,12},{24,36},{48,60},{72,84},{96,108},{120,132},{144,156},{168,180},{..., dimensions={0}, use_global_device_ids=true | all-gather | bytes 41472 | tf_op jit(solution)/shard_map/all_gather | solution.py:32
  101.8 3.8 %all-gather.14 = f32[6,1,9,128]{3,1,2,0:T(1,128)S(1)} all-gather(f32[3,1,9,128]{3,1,2,0:T(1,128)S(1)} %copy.91), channel_id=16, replica_groups={{12,24},{36,48},{60,72},{84,96},{108,120},{132,144},{156,168},{180,192}..., dimensions={0}, use_global_device_ids=true | all-gather | bytes 41472 | tf_op jit(solution)/shard_map/all_gather | solution.py:32
  105.7 0.7 fusion.1.image
  106.3 1.8 %product.1 = (f32[3,5,9,128]{3,2,1,0:T(8,128)}, f32[1,128]{1,0:T(1,128)}) custom-call(f32[3,5,9,128]{3,2,1,0:T(8,128)} %fusion.1.image, f32[3,5,9,128]{3,2,1,0:T(8,128)} %get-tuple-element.21.old.older.t0, f32[3,5,9,128]{3,2,1,0:T(8,128)} %get-tuple-element.23.old.t1, f32[3,5,9,128]{3,2,1,0:T(8,128)} %get-tuple-element.25.t2), custom_call_target="tpu_custom_call" | custom-call | tf_op jit(solution)/shard_map/product/pallas_call | solution.py:477
  108.1 0.0 copy-start.2
  108.1 0.7 copy-done.2
  108.8 20.1 %all_to_all.14 = f32[64,1,16]{2,1,0:T(1,128)S(1)} all-to-all(f32[64,1,16]{2,1,0:T(1,128)S(1)} %broadcast_in_dim.4), channel_id=1, replica_groups=mesh['dom_0'=8,'dom_1'=4,'dom_2'=2,'sub'=12] {'dom_0','dom_1','dom_2'}, dimensions={0} | all-to-all | bytes 8192 | tf_op jit(solution)/shard_map/all_to_all | solution.py:55
  128.9 0.1 reduce_sum.9
  129.0 14.2 %all_to_all.15 = f32[12,1,16]{2,1,0:T(1,128)S(1)} all-to-all(f32[12,1,16]{2,1,0:T(1,128)S(1)} %broadcast_in_dim.5), channel_id=1, replica_groups=mesh['dom_0'=8,'dom_1'=4,'dom_2'=2,'sub'=12] {'sub'}, dimensions={0} | all-to-all | bytes 1536 | tf_op jit(solution)/shard_map/all_to_all | solution.py:55
  143.2 0.6 copy.199
  143.8 2.6 %finish.1 = (f32[3,5,9,128]{3,2,1,0:T(8,128)}, f32[3,5,9,128]{3,2,1,0:T(8,128)}) custom-call(f32[12,16]{1,0:T(8,128)} %bitcast.5, f32[3,5,9,128]{3,2,1,0:T(8,128)} %get-tuple-element.21.old.older.t0, f32[3,5,9,128]{3,2,1,0:T(8,128)} %get-tuple-element.23.old.t1, f32[3,5,9,128]{3,2,1,0:T(8,128)} %get-tuple-element.25.t2, f32[3,5,9,128]{3,2,1,0:T(8,128)} %get-tuple-element.27.t3), custom_call_target="tpu_custom_call" | custom-call | tf_op jit(solution)/shard_map/finish/pallas_call | solution.py:479
  146.5 0.0 copy-start
  146.5 1.6 %copy.98 = f32[3,5,9,128]{3,0,2,1:T(4,128)} copy(f32[3,5,9,128]{3,2,1,0:T(8,128)} %get-tuple-element.40) | data formatting | bytes 138240
  148.1 0.0 copy-done
  148.1 0.7 copy.99
  (35 shorter events, 0.4 us)
Async XLA Ops:
  0.7 1.6 %copy-start.1 = (f32[3,5,9,128]{3,0,2,1:T(4,128)S(1)}, f32[3,5,9,128]{3,0,2,1:T(4,128)}, u32[]{:S(2)}) copy-start(f32[3,5,9,128]{3,0,2,1:T(4,128)} %param.9) | copy-start | bytes 207364
  108.1 0.7 copy-start.2
  146.5 1.6 %copy-start = (f32[3,5,9,128]{3,2,1,0:T(8,128)S(1)}, f32[3,5,9,128]{3,2,1,0:T(8,128)}, u32[]{:S(2)}) copy-start(f32[3,5,9,128]{3,2,1,0:T(8,128)} %get-tuple-element.41) | copy-start | bytes 207364

commit v3 on v2

--- a/solution.py
+++ b/solution.py
@@ -44,17 +44,6 @@
     return jnp.concatenate(
         [jnp.where(even, outer, inner), middle, jnp.where(even, inner, outer)], dim
     )
-
-
-def total(values):
-    for axes in (DOM, ("sub",)):
-        count = 1
-        for axis in axes:
-            count *= lax.axis_size(axis)
-        spread = jnp.broadcast_to(values[None], (count, values.shape[0]))
-        gathered = lax.all_to_all(spread, axes, 0, 0, tiled=True)
-        values = jnp.sum(gathered, 0)
-    return gathered
 
 
 ROOT = math.sqrt(0.15)
@@ -172,7 +161,7 @@
     return jnp.dot(left, right, precision=highest, preferred_element_type=jnp.float32)
 
 
-def force_kernel(disp, vel, energy, rho, share, portion, ident, mix, force, rate, near_out, far_out, grad, work):
+def force_kernel(place, disp, vel, energy, rho, share, portion, ident, mix, force, rate, near_out, far_out, inner, outer, grad, work):
     packs, rows = (0, 1), energy.shape[2]
     count = 2 * rows
     even = even_lanes(count)
@@ -341,69 +330,198 @@
                 base = count * jxy + rows * zone
                 rate[2 * jxy + jz, zone] = ratio[base : base + rows]
 
-
-def mass_kernel(first, image, older, old, near_mass, far_mass, new, partial):
-    packs, rows = (0, 1), near_mass.shape[1] // 2
-    even = even_lanes(2 * rows)
-    if first == 0:
-        new[...] = image[...]
-    elif first == 1:
-        new[...] = (1.0 / HALF_WIDTH) * image[...] - (CENTER / HALF_WIDTH) * old[...]
-    else:
-        new[...] = (2.0 / HALF_WIDTH) * image[...] - (2.0 * CENTER / HALF_WIDTH) * old[...] - older[...]
-    near = [near_mass[p] for p in range(9)]
-    far = [far_mass[p] for p in range(9)]
+    def pack(ref, high):
+        nodes_at, zones_at = (4, 2) if high else (0, 0)
+        ref[75:80] = jnp.zeros((5, 128), jnp.float32)
+        for x in range(5):
+            for comp in range(3):
+                spot = 5 * (3 * x + comp)
+                ref[spot : spot + 5] = force[comp, x, nodes_at : nodes_at + 5, :]
+        for zone in range(2):
+            for p in range(18):
+                spot = 80 + 2 * (18 * zone + p)
+                source = near_out if p < 9 else far_out
+                base = rows * zone + zones_at
+                ref[spot : spot + 2] = source[p % 9, base : base + 2, :]
+
+    @pl.when(place[1] == 0)
+    def _():
+        pack(inner, True)
+        pack(outer, False)
+
+    @pl.when(place[1] == 1)
+    def _():
+        pack(inner, False)
+        pack(outer, True)
+
+
+LAYER = 56
+MASS_AT = 5 * LAYER
+BLOCK = MASS_AT + 8 * 36
+
+
+def widen_kernel(place, inner, outer, force, near, far, wide):
+    def fill(lower, upper):
+        for x in range(5):
+            for comp in range(3):
+                base, spot = LAYER * x + 17 * comp, 5 * (3 * x + comp)
+                wide[base : base + 4] = lower[spot : spot + 4]
+                wide[base + 4 : base + 5] = lower[spot + 4 : spot + 5] + force[comp, x, 0:1, :]
+                wide[base + 5 : base + 12] = force[comp, x, 1:8, :]
+                wide[base + 12 : base + 13] = force[comp, x, 8:9, :] + upper[spot : spot + 1]
+                wide[base + 13 : base + 17] = upper[spot + 1 : spot + 5]
+            wide[LAYER * x + 51 : LAYER * (x + 1)] = jnp.zeros((5, 128), jnp.float32)
+        for zone in range(2):
+            for p in range(18):
+                base, spot = MASS_AT + 8 * (18 * zone + p), 80 + 2 * (18 * zone + p)
+                source = near if p < 9 else far
+                wide[base : base + 2] = lower[spot : spot + 2]
+                wide[base + 2 : base + 6] = source[p % 9, 4 * zone : 4 * zone + 4, :]
+                wide[base + 6 : base + 8] = upper[spot : spot + 2]
+
+    @pl.when(place[1] == 0)
+    def _():
+        fill(outer.at[0], inner.at[1])
+
+    @pl.when(place[1] == 1)
+    def _():
+        fill(inner.at[0], outer.at[1])
+
+
+def close_kernel(place, pair, wide, closed):
+    shared = pair[0, 4 * LAYER : 5 * LAYER] + pair[1, 0:LAYER]
+    closed[...] = wide[...]
+
+    @pl.when(place[0] == 0)
+    def _():
+        closed[4 * LAYER : 5 * LAYER] = shared
+
+    @pl.when(place[0] == 1)
+    def _():
+        closed[0:LAYER] = shared
+
+
+def krylov_kernel(place, pair, cross, edges, t0, t1, t2, partial, products, node, image, second, mass):
+    def fill(layers, blocks):
+        for at, (ref, base) in enumerate(layers):
+            for comp in range(3):
+                spot = base + 17 * comp
+                node[comp, at] = ref[spot : spot + 17]
+        for at, ref in enumerate(blocks):
+            for k in range(2):
+                for p in range(18):
+                    spot = MASS_AT + 8 * (18 * k + p)
+                    mass[2 * at + k, p] = ref[spot : spot + 8]
+
+    shared = pair[0, 4 * LAYER : 5 * LAYER] + pair[1, 0:LAYER]
+
+    @pl.when(place[0] == 0)
+    def _():
+        left, mine, right = cross.at[0], pair.at[0], pair.at[1]
+        layers = [(left, LAYER * x) for x in range(4)] + [(edges.at[0], 0)]
+        layers += [(mine, LAYER * x) for x in (1, 2, 3, 4)] + [(right, LAYER * x) for x in (1, 2, 3)]
+        fill(layers + [(edges.at[1], 0)], (left, mine, right))
+        for comp in range(3):
+            node[comp, 8] = shared[17 * comp : 17 * comp + 17]
+
+    @pl.when(place[0] == 1)
+    def _():
+        left, mine, right = pair.at[0], pair.at[1], cross.at[1]
+        layers = [(edges.at[0], 0)] + [(left, LAYER * x) for x in (1, 2, 3, 4)]
+        layers += [(mine, LAYER * x) for x in (1, 2, 3)] + [(edges.at[1], 0)]
+        fill(layers + [(right, LAYER * x) for x in (1, 2, 3, 4)], (left, mine, right))
+        for comp in range(3):
+            node[comp, 4] = shared[17 * comp : 17 * comp + 17]
+
+    def apply(source, target, comp, zones, start, rows):
+        even = even_lanes(rows)
+        first = start // 2
+        for zone in zones:
+            near = [mass[zone, p, first : first + rows, :] for p in range(9)]
+            far = [mass[zone, 9 + p, first : first + rows, :] for p in range(9)]
+            spots = [
+                [(comp, 2 * zone + i, pl.ds(start + j, rows, stride=2), slice(None)) for j in range(3)]
+                for i in range(3)
+            ]
+            out = mass_nodes([[source[spots[i][j]] for j in range(3)] for i in range(3)], near, far, even)
+            for i in range(3):
+                for j in range(3):
+                    target[spots[i][j]] = target[spots[i][j]] + out[i][j]
+
     partial[...] = jnp.zeros_like(partial)
+    lane = lax.broadcasted_iota(jnp.int32, (1, 128), 1)
+    sums = [None] * 9
+
+    def add(at, left, right):
+        term = left * right
+        term = jnp.sum(term, 0, keepdims=True)
+        sums[at] = term if sums[at] is None else sums[at] + term
+
     for comp in range(3):
-        nodes = corners(new, comp, packs, rows)
-        scatter(partial, comp, packs, rows, mass_nodes(nodes, near, far, even))
-
-
-def product_kernel(image, t0, t1, t2, t3, products):
-    t3[...] = (2.0 / HALF_WIDTH) * image[...] - (2.0 * CENTER / HALF_WIDTH) * t2[...] - t1[...]
-    refs = (t0, t1, t2, t3)
-    wide, tall = image.shape[1], image.shape[2]
-    lane = lax.broadcasted_iota(jnp.int32, (1, 128), 1)
-    sums = [None] * len(PAIRS)
-    for comp in range(3):
-        for x in range(wide - 1):
-            parts = [ref[comp, x, 0 : tall - 1, :] for ref in refs]
-            for at, (i, j) in enumerate(PAIRS):
-                term = parts[i] * parts[j]
-                sums[at] = term if sums[at] is None else sums[at] + term
+        image[comp] = jnp.zeros(image.shape[1:], jnp.float32)
+        apply(node, image, comp, range(6), 0, 8)
+        for x in range(2, 11):
+            second[comp, x] = (1.0 / HALF_WIDTH) * image[comp, x] - (CENTER / HALF_WIDTH) * node[comp, x]
+        image[comp] = jnp.zeros(image.shape[1:], jnp.float32)
+        apply(second, image, comp, range(1, 5), 2, 6)
+        for x in range(4, 9):
+            t0[comp, x - 4] = node[comp, x, 4:13, :]
+            t1[comp, x - 4] = second[comp, x, 4:13, :]
+            t2[comp, x - 4] = (
+                (2.0 / HALF_WIDTH) * image[comp, x, 4:13, :]
+                - (2.0 * CENTER / HALF_WIDTH) * second[comp, x, 4:13, :]
+                - node[comp, x, 4:13, :]
+            )
+        near = [jnp.concatenate([mass[2, p, 2:6, :], mass[3, p, 2:6, :]], 0) for p in range(9)]
+        far = [jnp.concatenate([mass[2, 9 + p, 2:6, :], mass[3, 9 + p, 2:6, :]], 0) for p in range(9)]
+        nodes = corners(t2, comp, (0, 1), 4)
+        scatter(partial, comp, (0, 1), 4, mass_nodes(nodes, near, far, even_lanes(8)))
+        for x in range(5):
+            fields = [ref[comp, x] for ref in (t0, t1, t2)]
+            last = partial[comp, x]
+            for i in range(3):
+                add(6 + i, fields[i], last)
+            if x < 4:
+                owned = [v[0:8] for v in fields]
+                for at, (i, j) in enumerate(((0, 0), (0, 1), (0, 2), (1, 1), (1, 2), (2, 2))):
+                    add(at, owned[i], owned[j])
+    value = [jnp.sum(v, 1, keepdims=True) for v in sums]
+    gram = {(0, 0): value[0], (0, 1): value[1], (0, 2): value[2], (1, 1): value[3], (1, 2): value[4], (2, 2): value[5]}
+    for i in range(3):
+        gram[(i, 3)] = (
+            (2.0 / HALF_WIDTH) * value[6 + i]
+            - (2.0 * CENTER / HALF_WIDTH) * gram[(i, 2)]
+            - gram[(min(i, 1), max(i, 1))]
+        )
     row = jnp.zeros((1, 128), jnp.float32)
-    for at in range(len(PAIRS)):
-        value = jnp.sum(jnp.sum(sums[at], 0, keepdims=True), 1, keepdims=True)
-        row = jnp.where(lane == at, value, row)
+    for at, spot in enumerate(PAIRS):
+        row = jnp.where(lane == at, gram[spot], row)
     products[...] = row
 
 
-def finish_kernel(gathered, t0, t1, t2, t3, accel, residual):
-    row = jnp.sum(gathered[...], 0, keepdims=True)
+def finish_kernel(place, gathered, image, t0, t1, t2, accel, residual):
+    row = gathered[0, 15:16, :]
+    for peer in range(1, gathered.shape[0]):
+        row = row + gathered[peer, 15:16, :]
     gram = {pair: row[:, at : at + 1] for at, pair in enumerate(PAIRS)}
     accel_of, residual_of = cg_coefficients(gram)
-    fields = (t0, t1, t2, t3)
-    wide = t0.shape[1]
+    low, high = gathered.at[place[2]], gathered.at[place[3]]
     for comp in range(3):
-        for x in range(wide):
-            parts = [field[comp, x] for field in fields]
+        for x in range(5):
+            spot = 5 * comp + x
+            last = image[comp, x]
+            at = lax.broadcasted_iota(jnp.int32, last.shape, 0)
+            last = last + jnp.where(at == 0, low[spot : spot + 1, :], 0.0)
+            last = last + jnp.where(at == 8, high[spot : spot + 1, :], 0.0)
+            parts = [t0[comp, x], t1[comp, x], t2[comp, x]]
+            parts.append((2.0 / HALF_WIDTH) * last - (2.0 * CENTER / HALF_WIDTH) * parts[2] - parts[1])
             accel[comp, x] = accel_of[0] * parts[0] + accel_of[1] * parts[1] + accel_of[2] * parts[2]
             residual[comp, x] = (
-                residual_of[0] * parts[0] + residual_of[1] * parts[1] + residual_of[2] * parts[2] + residual_of[3] * parts[3]
+                residual_of[0] * parts[0]
+                + residual_of[1] * parts[1]
+                + residual_of[2] * parts[2]
+                + residual_of[3] * parts[3]
             )
-
-
-def local_call(kernel, name, outs, scratch=()):
-    return pl.pallas_call(
-        kernel,
-        out_shape=[jax.ShapeDtypeStruct(shape, jnp.float32) for shape in outs],
-        scratch_shapes=[pltpu.VMEM(shape, jnp.float32) for shape in scratch],
-        name=name,
-    )
-
-
-def assemble(local_sum):
-    return join_axis(join_axis(local_sum, ("sub",), 2), DOM, 1)
 
 
 CENTER = 0.196
@@ -456,33 +574,73 @@
     return accel, residual
 
 
+def local_call(kernel, name, outs, scratch, place, *operands):
+    return pl.pallas_call(
+        kernel,
+        out_shape=[jax.ShapeDtypeStruct(shape, jnp.float32) for shape in outs],
+        in_specs=[pl.BlockSpec(memory_space=pltpu.SMEM)]
+        + [pl.BlockSpec(memory_space=pltpu.VMEM) for _ in operands],
+        scratch_shapes=[pltpu.VMEM(shape, jnp.float32) for shape in scratch],
+        name=name,
+    )(place, *operands)
+
+
+def pair_gather(block, axes, offset):
+    return lax.all_gather(block, axes, axis_index_groups=pair_groups(axes, offset))
+
+
 def per_device(
     velocity, displacement, energy, rho_weight, mass_share, energy_share, material_id, mix_mask
 ):
     field = velocity.shape
-    count = energy.shape[1] * energy.shape[2]
-    mass = (9, count, 128)
-    partial, energy_rate, near_mass, far_mass = local_call(
-        force_kernel, "force", (field, energy.shape, mass, mass), ((2, 2, 9, 9, count, 128), (2, 9, count, 128))
-    )(displacement, velocity, energy, rho_weight, mass_share, energy_share, material_id, mix_mask)
-    image = assemble(partial)
-    basis = [image, image]
-    for at in range(CG_ITERS):
-        new, partial = local_call(functools.partial(mass_kernel, at), f"mass_{at}", (field, field))(
-            image, basis[-2], basis[-1], near_mass, far_mass
-        )
-        basis.append(new)
-        image = assemble(partial)
-    t0, t1, t2 = basis[2:]
-    t3, products = local_call(product_kernel, "product", (field, (1, 128)))(image, t0, t1, t2)
-    gathered = total(products[0, :16])
-    accel, residual = local_call(finish_kernel, "finish", (field, field))(gathered, t0, t1, t2, t3)
+    subs = lax.axis_size("sub")
+    at_sub = lax.axis_index("sub")
+    below, above = (at_sub + subs - 1) % subs, (at_sub + 1) % subs
+    place = jnp.stack([lax.axis_index(DOM) % 2, at_sub % 2, below, above]).astype(jnp.int32)
+    mass = (9, 8, 128)
+    halo = (152, 128)
+    partial, energy_rate, near_mass, far_mass, inner, outer = local_call(
+        force_kernel,
+        "force",
+        (field, energy.shape, mass, mass, halo, halo),
+        ((2, 2, 9, 9, 8, 128), (2, 9, 8, 128)),
+        place, displacement, velocity, energy, rho_weight, mass_share, energy_share, material_id, mix_mask,
+    )
+    inner = pair_gather(inner, ("sub",), 0)
+    outer = pair_gather(outer, ("sub",), 1)
+    (wide,) = local_call(
+        widen_kernel, "widen", ((BLOCK, 128),), (), place, inner, outer, partial, near_mass, far_mass
+    )
+    pair = pair_gather(wide, DOM, 0)
+    (closed,) = local_call(close_kernel, "close", ((BLOCK, 128),), (), place, pair, wide)
+    cross = pair_gather(closed, DOM, 1)
+    edges = pair_gather(cross[0, 4 * LAYER : 5 * LAYER] + cross[1, :LAYER], DOM, 0)
+    extended = (3, 13, 17, 128)
+    t0, t1, t2, partial, products = local_call(
+        krylov_kernel,
+        "krylov",
+        (field, field, field, field, (1, 128)),
+        (extended, extended, extended, (6, 18, 8, 128)),
+        place, pair, cross, edges,
+    )
+    image = join_axis(partial, DOM, 1)
+    count = lax.axis_size(DOM)
+    spread = jnp.broadcast_to(products[:, :16], (count, 16))
+    row = jnp.sum(lax.all_to_all(spread, DOM, 0, 0, tiled=True), 0)
+    row = jnp.pad(row, (0, 112))[None]
+    low = jnp.concatenate([image[:, :, 0].reshape(15, 128), row], 0)
+    high = jnp.concatenate([image[:, :, 8].reshape(15, 128), row], 0)
+    peer = jnp.arange(subs, dtype=jnp.int32)[:, None, None]
+    gathered = lax.all_to_all(jnp.where(peer == above, high, low), "sub", 0, 0, tiled=True)
+    accel, residual = local_call(
+        finish_kernel, "finish", (field, field), (), place, gathered, image, t0, t1, t2
+    )
     return (accel, residual, energy_rate)
 
 
 def solution(mesh):
     torus = Mesh(
-        mesh.devices.reshape(mesh.shape["dom"] // 8, 4, 2, mesh.shape["sub"]), ("dom_0", "dom_1", "dom_2", "sub")
+        mesh.devices.reshape((8, 4, 2, mesh.shape["sub"]) if mesh.shape["dom"] == 64 else (1, 1, 2, mesh.shape["sub"])), ("dom_0", "dom_1", "dom_2", "sub")
     )
     return jax.shard_map(
         per_device,

time: 150 us -> 98.4 us (0.66)
  the two profiles are of different devices: /device:TPU:1 before, /device:TPU:32 now
where the time goes in v3:
time: 98.4 us; the launch traced here: 97.8 us
  blocking collectives  63.1 us (64%)
  Pallas kernels  16.2 us (16%)
  starting transfers between devices  8.88 us (9%)
  local copies, waits for them, and re-layouts  7.2 us (7%)
  other arithmetic  1.52 us (2%)
    all_gather x5, blocking collectives, pair_gather(): lax.all_gather(block, axes, axis_index_groups=pair_groups(axes, offset))  37.4 us
    all_to_all x1, blocking collectives, per_device(): lax.all_to_all(jnp.where(peer == above, high, low), 'sub', 0, 0, tiled=True)  16.7 us
    pallas_call x5, Pallas kernels, local_call(): pl.pallas_call(kernel, out_shape=[jax.ShapeDtypeStruct(shape, jnp.float32...  16.2 us
    all_gather x2, blocking collectives, pair_sum(): lax.all_gather(layer, axes, axis_index_groups=pair_groups(axes, offset))  8.98 us
    all_to_all x1, starting transfers between devices, per_device(): row = jnp.sum(lax.all_to_all(spread, DOM, 0, 0, tiled=True), 0)  8.88 us
    unnamed x16, local copies, waits for them, and re-layouts  5.57 us
  transfers between devices with their start and end apart: 1, of which 0 were waited for; matrix products, arithmetic and copies ran while one was open for 2% of the time, Pallas kernels for 0%

profile of v3, /device:TPU:32, one launch (start us, length us, event | category | flops | bytes accessed | tf_op | source)
XLA Modules:
  0.0 97.8 jit_solution(6195783380501799075)
XLA Ops:
  0.7 0.0 copy-start.3
  0.7 1.6 %copy.36.vel = f32[3,5,9,128]{3,2,1,0:T(8,128)} copy(f32[3,5,9,128]{3,0,2,1:T(4,128)} %param.8) | data formatting | bytes 138240 | tf_op args[0]
  2.3 0.0 copy-done.3
  2.3 0.7 copy.35.disp
  3.0 0.6 pad_add_fusion.place
  3.5 3.9 %force.1 = (f32[3,5,9,128]{3,2,1,0:T(8,128)}, f32[8,2,4,64]{3,2,1,0:T(4,128)}, f32[9,8,128]{2,1,0:T(8,128)}, f32[9,8,128]{2,1,0:T(8,128)}, f32[152,128]{1,0:T(8,128)}, /*index=5*/f32[152,128]{1,0:T(8,128)}) custom-call(s32[4]{0:T(128)} %pad_add_fusion.place, f32[3,5,9,128]{3,2,1,0:T(8,128)} %copy.35.disp, f32[3,5,9,128]{3,2,1,0:T(8,128)} %copy.36.vel, ...), custom_call_target="tpu_custom_call" | custom-call | tf_op jit(solution)/shard_map/force/pallas_call | solution.py:578
  7.4 0.0 copy-start.4
  7.4 7.4 %all-gather = f32[304,128]{1,0:T(8,128)} all-gather(f32[152,128]{1,0:T(8,128)} %get-tuple-element.16), channel_id=2, replica_groups={{0,1},{2,3},{4,5},{6,7},{8,9},{10,11},{12,13},{14,15},{16,17},{18,19},{..., dimensions={0}, use_global_device_ids=true | all-gather | bytes 233472 | tf_op jit(solution)/shard_map/all_gather | solution.py:589
  14.8 0.0 copy-done.4
  14.8 14.0 %all-gather.1 = f32[304,128]{1,0:T(8,128)} all-gather(f32[152,128]{1,0:T(8,128)S(1)} %copy-done.4), channel_id=3, replica_groups={{1,2},{3,4},{5,6},{7,8},{9,10},{11,0},{13,14},{15,16},{17,18},{19,20},{..., dimensions={0}, use_global_device_ids=true | all-gather | bytes 233472 | tf_op jit(solution)/shard_map/all_gather | solution.py:589
  28.8 1.9 %widen.1.wide = f32[568,128]{1,0:T(8,128)} custom-call(s32[4]{0:T(128)} %pad_add_fusion.place, f32[2,152,128]{2,1,0:T(8,128)} %bitcast.16, f32[2,152,128]{2,1,0:T(8,128)} %bitcast.17, f32[3,5,9,128]{3,2,1,0:T(8,128)} %get-tuple-element.18.force, f32[9,8,128]{2,1,0:T(8,128)} %get-tuple-element.19.near, f32[9,8,128]{2,1,0:T(8,128)} %get-tuple-element.20.far), custom_call_target="tpu_custom_call" | custom-call | tf_op jit(solution)/shard_map/widen/pallas_call | solution.py:578
  30.7 3.9 %all-gather.2 = f32[1136,128]{1,0:T(8,128)} all-gather(f32[568,128]{1,0:T(8,128)} %widen.1.wide), channel_id=4, replica_groups={{0,12},{24,36},{48,60},{72,84},{96,108},{120,132},{144,156},{168,180},{..., dimensions={0}, use_global_device_ids=true | all-gather | bytes 872448 | tf_op jit(solution)/shard_map/all_gather | solution.py:589
  34.5 1.9 %close.1 = f32[568,128]{1,0:T(8,128)} custom-call(s32[4]{0:T(128)} %pad_add_fusion.place, f32[2,568,128]{2,1,0:T(8,128)} %bitcast.12, f32[568,128]{1,0:T(8,128)} %widen.1.wide), custom_call_target="tpu_custom_call" | custom-call | tf_op jit(solution)/shard_map/close/pallas_call | solution.py:578
  36.4 10.3 %all-gather.3 = f32[1136,128]{1,0:T(8,128)S(1)} all-gather(f32[568,128]{1,0:T(8,128)} %close.1), channel_id=5, replica_groups={{12,24},{36,48},{60,72},{84,96},{108,120},{132,144},{156,168},{180,192}..., dimensions={0}, use_global_device_ids=true | all-gather | bytes 872448 | tf_op jit(solution)/shard_map/all_gather | solution.py:589
  46.7 0.0 copy-start
  46.7 2.0 %all_gather.48.edges = f32[2,56,128]{2,1,0:T(8,128)} all-gather(f32[1,56,128]{2,1,0:T(8,128)S(1)} %slice_add_fusion), channel_id=1, replica_groups={{0,12},{24,36},{48,60},{72,84},{96,108},{120,132},{144,156},{168,180},{..., dimensions={0}, use_global_device_ids=true | all-gather | bytes 86016 | tf_op jit(solution)/shard_map/all_gather | solution.py:589
  48.7 0.0 copy-done
  48.7 5.9 %krylov.1 = (f32[3,5,9,128]{3,2,1,0:T(8,128)}, f32[3,5,9,128]{3,2,1,0:T(8,128)}, f32[3,5,9,128]{3,2,1,0:T(8,128)}, f32[3,5,9,128]{3,2,1,0:T(8,128)}, f32[1,128]{1,0:T(1,128)}) custom-call(s32[4]{0:T(128)} %pad_add_fusion.place, f32[2,568,128]{2,1,0:T(8,128)} %bitcast.13, f32[2,568,128]{2,1,0:T(8,128)} %bitcast.15, f32[2,56,128]{2,1,0:T(8,128)} %all_gather.48.edges), custom_call_target="tpu_custom_call" | custom-call | tf_op jit(solution)/shard_map/krylov/pallas_call | solution.py:578
  54.6 0.0 copy-start.5
  54.6 0.7 copy-done.5
  55.2 0.6 broadcast_in_dim.26
  55.9 8.9 %all-to-all-start = ((f32[64,1,16]{2,1,0:T(1,128)}), f32[64,1,16]{2,1,0:T(1,128)S(1)}, u32[]{:S(2)}, u32[]{:S(2)}) async-start(f32[64,1,16]{2,1,0:T(1,128)} %broadcast_in_dim.26), calls=%async_computation | async-start | bytes 65536 | tf_op jit(solution)/shard_map/all_to_all | solution.py:629
  64.8 0.9 slice.46
  65.6 0.8 slice_select_fusion
  66.4 1.8 %all-gather.5 = f32[6,1,9,128]{3,1,2,0:T(1,128)S(1)} all-gather(f32[3,1,9,128]{3,1,2,0:T(1,128)S(1)} %copy.40), channel_id=7, replica_groups={{0,12},{24,36},{48,60},{72,84},{96,108},{120,132},{144,156},{168,180},{..., dimensions={0}, use_global_device_ids=true | all-gather | bytes 41472 | tf_op jit(solution)/shard_map/all_gather | solution.py:32
  68.3 7.1 %all-gather.4 = f32[6,1,9,128]{3,1,2,0:T(1,128)S(1)} all-gather(f32[3,1,9,128]{3,1,2,0:T(1,128)S(1)} %copy.37), channel_id=6, replica_groups={{12,24},{36,48},{60,72},{84,96},{108,120},{132,144},{156,168},{180,192}..., dimensions={0}, use_global_device_ids=true | all-gather | bytes 41472 | tf_op jit(solution)/shard_map/all_gather | solution.py:32
  75.5 0.0 copy-start.1
  75.6 0.0 all-to-all-done
  75.6 0.1 reduce_sum.9
  75.7 0.1 broadcast_select_fusion
  75.8 0.4 copy-done.1
  76.1 16.7 %all_to_all.11.gathered = f32[12,16,128]{2,1,0:T(8,128)} all-to-all(f32[12,16,128]{2,1,0:T(8,128)S(1)} %broadcast_select_fusion), channel_id=1, replica_groups=mesh['dom_0'=8,'dom_1'=4,'dom_2'=2,'sub'=12] {'sub'}, dimensions={0} | all-to-all | bytes 196608 | tf_op jit(solution)/shard_map/all_to_all | solution.py:634
  92.8 2.7 %finish.1 = (f32[3,5,9,128]{3,2,1,0:T(8,128)}, f32[3,5,9,128]{3,2,1,0:T(8,128)}) custom-call(s32[4]{0:T(128)} %pad_add_fusion.place, f32[12,16,128]{2,1,0:T(8,128)} %all_to_all.11.gathered, f32[3,5,9,128]{3,2,1,0:T(8,128)} %copy-done.1, f32[3,5,9,128]{3,2,1,0:T(8,128)} %get-tuple-element.23.t0, f32[3,5,9,128]{3,2,1,0:T(8,128)} %get-tuple-element.24.t1, ...), custom_call_target="tpu_custom_call" | custom-call | tf_op jit(solution)/shard_map/finish/pallas_call | solution.py:578
  95.5 0.0 copy-start.2
  95.5 1.6 %copy.44 = f32[3,5,9,128]{3,0,2,1:T(4,128)} copy(f32[3,5,9,128]{3,2,1,0:T(8,128)} %get-tuple-element.38) | data formatting | bytes 138240
  97.1 0.0 copy-done.2
  97.1 0.7 copy.45
  (14 shorter events, 0.1 us)
Async XLA Ops:
  0.7 1.6 %copy-start.3 = (f32[3,5,9,128]{3,0,2,1:T(4,128)S(1)}, f32[3,5,9,128]{3,0,2,1:T(4,128)}, u32[]{:S(2)}) copy-start(f32[3,5,9,128]{3,0,2,1:T(4,128)} %param.9) | copy-start | bytes 207364
  7.4 7.4 %copy-start.4 = (f32[152,128]{1,0:T(8,128)S(1)}, f32[152,128]{1,0:T(8,128)}, u32[]{:S(2)}) copy-start(f32[152,128]{1,0:T(8,128)} %get-tuple-element.17) | copy-start | bytes 233476
  46.7 2.0 %copy-start = (f32[1136,128]{1,0:T(8,128)}, f32[1136,128]{1,0:T(8,128)S(1)}, u32[]{:S(2)}) copy-start(f32[1136,128]{1,0:T(8,128)S(1)} %all-gather.3) | copy-start | bytes 1744900
  54.6 0.7 copy-start.5
  55.9 19.7 %all-to-all-start = ((f32[64,1,16]{2,1,0:T(1,128)}), f32[64,1,16]{2,1,0:T(1,128)S(1)}, u32[]{:S(2)}, u32[]{:S(2)}) async-start(f32[64,1,16]{2,1,0:T(1,128)} %broadcast_in_dim.26), calls=%async_computation | async-start | bytes 65536 | tf_op jit(solution)/shard_map/all_to_all | solution.py:629
  75.5 0.7 copy-start.1
  95.5 1.6 %copy-start.2 = (f32[3,5,9,128]{3,2,1,0:T(8,128)S(1)}, f32[3,5,9,128]{3,2,1,0:T(8,128)}, u32[]{:S(2)}) copy-start(f32[3,5,9,128]{3,2,1,0:T(8,128)} %get-tuple-element.39) | copy-start | bytes 207364

commit v4 on v3

--- a/solution.py
+++ b/solution.py
@@ -26,24 +26,6 @@
     for axis in axes:
         count *= lax.axis_size(axis)
     return [[(i + offset) % count, (i + offset + 1) % count] for i in range(0, count, 2)]
-
-
-def pair_sum(layer, axes, offset):
-    gathered = lax.all_gather(layer, axes, axis_index_groups=pair_groups(axes, offset))
-    return gathered[0] + gathered[1]
-
-
-def join_axis(block, axes, dim):
-    even = lax.axis_index(axes) % 2 == 0
-    last = block.shape[dim] - 1
-    low = lax.slice_in_dim(block, 0, 1, axis=dim)
-    high = lax.slice_in_dim(block, last, last + 1, axis=dim)
-    inner = pair_sum(jnp.where(even, high, low), axes, 0)
-    outer = pair_sum(jnp.where(even, low, high), axes, 1)
-    middle = lax.slice_in_dim(block, 1, last, axis=dim)
-    return jnp.concatenate(
-        [jnp.where(even, outer, inner), middle, jnp.where(even, inner, outer)], dim
-    )
 
 
 ROOT = math.sqrt(0.15)
@@ -161,8 +143,13 @@
     return jnp.dot(left, right, precision=highest, preferred_element_type=jnp.float32)
 
 
-def force_kernel(place, disp, vel, energy, rho, share, portion, ident, mix, force, rate, near_out, far_out, inner, outer, grad, work):
+def force_kernel(disp, vel, energy, rho, share, portion, ident, mix, force, rate, near_out, far_out, inner, outer, grad, work, node):
     packs, rows = (0, 1), energy.shape[2]
+    for field, ref in enumerate((disp, vel)):
+        for x in range(5):
+            for y in range(9):
+                for comp in range(3):
+                    node[field, comp, x, y : y + 1, :] = ref[x, y, comp : comp + 1, :]
     count = 2 * rows
     even = even_lanes(count)
 
@@ -196,9 +183,9 @@
     near_point = jnp.where(even, POINTS[0], POINTS[1])
     a, b, c = SLOPE[0]
 
-    for field, ref in enumerate((disp, vel)):
+    for field in range(2):
         for comp in range(3):
-            nodes = corners(ref, comp, packs, rows)
+            nodes = corners(node.at[field], comp, packs, rows)
             values = [[None] * 3 for _ in range(3)], [[None] * 3 for _ in range(3)]
             slopes = [[None] * 3 for _ in range(3)], [[None] * 3 for _ in range(3)]
             for i in range(3):
@@ -344,12 +331,14 @@
                 base = rows * zone + zones_at
                 ref[spot : spot + 2] = source[p % 9, base : base + 2, :]
 
-    @pl.when(place[1] == 0)
+    odd_sub = lax.rem(lax.axis_index("sub"), 2)
+
+    @pl.when(odd_sub == 0)
     def _():
         pack(inner, True)
         pack(outer, False)
 
-    @pl.when(place[1] == 1)
+    @pl.when(odd_sub == 1)
     def _():
         pack(inner, False)
         pack(outer, True)
@@ -360,7 +349,7 @@
 BLOCK = MASS_AT + 8 * 36
 
 
-def widen_kernel(place, inner, outer, force, near, far, wide):
+def widen_kernel(inner, outer, force, near, far, wide):
     def fill(lower, upper):
         for x in range(5):
             for comp in range(3):
@@ -379,29 +368,19 @@
                 wide[base + 2 : base + 6] = source[p % 9, 4 * zone : 4 * zone + 4, :]
                 wide[base + 6 : base + 8] = upper[spot : spot + 2]
 
-    @pl.when(place[1] == 0)
-    def _():
-        fill(outer.at[0], inner.at[1])
-
-    @pl.when(place[1] == 1)
-    def _():
-        fill(inner.at[0], outer.at[1])
-
-
-def close_kernel(place, pair, wide, closed):
-    shared = pair[0, 4 * LAYER : 5 * LAYER] + pair[1, 0:LAYER]
-    closed[...] = wide[...]
-
-    @pl.when(place[0] == 0)
-    def _():
-        closed[4 * LAYER : 5 * LAYER] = shared
-
-    @pl.when(place[0] == 1)
-    def _():
-        closed[0:LAYER] = shared
-
-
-def krylov_kernel(place, pair, cross, edges, t0, t1, t2, partial, products, node, image, second, mass):
+    odd_sub = lax.rem(lax.axis_index("sub"), 2)
+
+    @pl.when(odd_sub == 0)
+    def _():
+        fill(outer, inner)
+
+    @pl.when(odd_sub == 1)
+    def _():
+        fill(inner, outer)
+
+
+def krylov_kernel(pair, cross, edges, t0, t1, t2, partial, inner, outer, products, node, image, second, mass):
+    core = lax.axis_index("dom_2")
     def fill(layers, blocks):
         for at, (ref, base) in enumerate(layers):
             for comp in range(3):
@@ -415,7 +394,7 @@
 
     shared = pair[0, 4 * LAYER : 5 * LAYER] + pair[1, 0:LAYER]
 
-    @pl.when(place[0] == 0)
+    @pl.when(core == 0)
     def _():
         left, mine, right = cross.at[0], pair.at[0], pair.at[1]
         layers = [(left, LAYER * x) for x in range(4)] + [(edges.at[0], 0)]
@@ -424,7 +403,7 @@
         for comp in range(3):
             node[comp, 8] = shared[17 * comp : 17 * comp + 17]
 
-    @pl.when(place[0] == 1)
+    @pl.when(core == 1)
     def _():
         left, mine, right = pair.at[0], pair.at[1], cross.at[1]
         layers = [(edges.at[0], 0)] + [(left, LAYER * x) for x in (1, 2, 3, 4)]
@@ -496,16 +475,33 @@
     row = jnp.zeros((1, 128), jnp.float32)
     for at, spot in enumerate(PAIRS):
         row = jnp.where(lane == at, gram[spot], row)
-    products[...] = row
-
-
-def finish_kernel(place, gathered, image, t0, t1, t2, accel, residual):
+    products[...] = jnp.broadcast_to(row[None, :, :16], products.shape)
+
+    def edge(ref, x):
+        ref[27:32] = jnp.zeros((5, 128), jnp.float32)
+        for comp in range(3):
+            ref[9 * comp : 9 * comp + 9] = partial[comp, x]
+
+    @pl.when(core == 0)
+    def _():
+        edge(inner, 4)
+        edge(outer, 0)
+
+    @pl.when(core == 1)
+    def _():
+        edge(inner, 0)
+        edge(outer, 4)
+
+
+def finish_kernel(gathered, image, t0, t1, t2, accel, residual):
     row = gathered[0, 15:16, :]
     for peer in range(1, gathered.shape[0]):
         row = row + gathered[peer, 15:16, :]
     gram = {pair: row[:, at : at + 1] for at, pair in enumerate(PAIRS)}
     accel_of, residual_of = cg_coefficients(gram)
-    low, high = gathered.at[place[2]], gathered.at[place[3]]
+    subs = gathered.shape[0]
+    at_sub = lax.axis_index("sub")
+    low, high = gathered.at[lax.rem(at_sub + subs - 1, subs)], gathered.at[lax.rem(at_sub + 1, subs)]
     for comp in range(3):
         for x in range(5):
             spot = 5 * comp + x
@@ -515,8 +511,8 @@
             last = last + jnp.where(at == 8, high[spot : spot + 1, :], 0.0)
             parts = [t0[comp, x], t1[comp, x], t2[comp, x]]
             parts.append((2.0 / HALF_WIDTH) * last - (2.0 * CENTER / HALF_WIDTH) * parts[2] - parts[1])
-            accel[comp, x] = accel_of[0] * parts[0] + accel_of[1] * parts[1] + accel_of[2] * parts[2]
-            residual[comp, x] = (
+            accel[x, :, comp, :] = accel_of[0] * parts[0] + accel_of[1] * parts[1] + accel_of[2] * parts[2]
+            residual[x, :, comp, :] = (
                 residual_of[0] * parts[0]
                 + residual_of[1] * parts[1]
                 + residual_of[2] * parts[2]
@@ -574,68 +570,80 @@
     return accel, residual
 
 
-def local_call(kernel, name, outs, scratch, place, *operands):
+def local_call(kernel, name, outs, scratch, *operands):
     return pl.pallas_call(
         kernel,
         out_shape=[jax.ShapeDtypeStruct(shape, jnp.float32) for shape in outs],
-        in_specs=[pl.BlockSpec(memory_space=pltpu.SMEM)]
-        + [pl.BlockSpec(memory_space=pltpu.VMEM) for _ in operands],
+        in_specs=[pl.BlockSpec(memory_space=pltpu.VMEM) for _ in operands],
+        out_specs=[pl.BlockSpec(memory_space=pltpu.VMEM) for _ in outs],
         scratch_shapes=[pltpu.VMEM(shape, jnp.float32) for shape in scratch],
         name=name,
-    )(place, *operands)
+    )(*operands)
 
 
 def pair_gather(block, axes, offset):
     return lax.all_gather(block, axes, axis_index_groups=pair_groups(axes, offset))
+
+
+def pair_swap(block, axes, offset):
+    groups = pair_groups(axes, offset)
+    return lax.ppermute(block, axes, [edge for a, b in groups for edge in ((a, b), (b, a))])
 
 
 def per_device(
     velocity, displacement, energy, rho_weight, mass_share, energy_share, material_id, mix_mask
 ):
     field = velocity.shape
+    turned = (field[1], field[2], field[0], field[3])
     subs = lax.axis_size("sub")
-    at_sub = lax.axis_index("sub")
-    below, above = (at_sub + subs - 1) % subs, (at_sub + 1) % subs
-    place = jnp.stack([lax.axis_index(DOM) % 2, at_sub % 2, below, above]).astype(jnp.int32)
+    above = (lax.axis_index("sub") + 1) % subs
+    core = lax.axis_index("dom_2")
     mass = (9, 8, 128)
     halo = (152, 128)
     partial, energy_rate, near_mass, far_mass, inner, outer = local_call(
         force_kernel,
         "force",
         (field, energy.shape, mass, mass, halo, halo),
-        ((2, 2, 9, 9, 8, 128), (2, 9, 8, 128)),
-        place, displacement, velocity, energy, rho_weight, mass_share, energy_share, material_id, mix_mask,
+        ((2, 2, 9, 9, 8, 128), (2, 9, 8, 128), (2,) + field),
+        jnp.transpose(displacement, (1, 2, 0, 3)),
+        jnp.transpose(velocity, (1, 2, 0, 3)),
+        energy, rho_weight, mass_share, energy_share, material_id, mix_mask,
     )
-    inner = pair_gather(inner, ("sub",), 0)
-    outer = pair_gather(outer, ("sub",), 1)
+    inner = pair_swap(inner, ("sub",), 0)
+    outer = pair_swap(outer, ("sub",), 1)
     (wide,) = local_call(
-        widen_kernel, "widen", ((BLOCK, 128),), (), place, inner, outer, partial, near_mass, far_mass
+        widen_kernel, "widen", ((BLOCK, 128),), (), inner, outer, partial, near_mass, far_mass
     )
     pair = pair_gather(wide, DOM, 0)
-    (closed,) = local_call(close_kernel, "close", ((BLOCK, 128),), (), place, pair, wide)
+    shared = pair[0, 4 * LAYER : 5 * LAYER] + pair[1, 0:LAYER]
+    closed = lax.dynamic_update_slice(wide, shared, (4 * LAYER * (1 - core), 0))
     cross = pair_gather(closed, DOM, 1)
     edges = pair_gather(cross[0, 4 * LAYER : 5 * LAYER] + cross[1, :LAYER], DOM, 0)
     extended = (3, 13, 17, 128)
-    t0, t1, t2, partial, products = local_call(
+    count = lax.axis_size(DOM)
+    t0, t1, t2, partial, inner, outer, spread = local_call(
         krylov_kernel,
         "krylov",
-        (field, field, field, field, (1, 128)),
+        (field, field, field, field, (32, 128), (32, 128), (count, 1, 16)),
         (extended, extended, extended, (6, 18, 8, 128)),
-        place, pair, cross, edges,
+        pair, cross, edges,
     )
-    image = join_axis(partial, DOM, 1)
-    count = lax.axis_size(DOM)
-    spread = jnp.broadcast_to(products[:, :16], (count, 16))
+    inner = pair_gather(inner, DOM, 0)
+    outer = pair_gather(outer, DOM, 1)
+    inner = (inner[0] + inner[1])[:27].reshape(3, 1, 9, 128)
+    outer = (outer[0] + outer[1])[:27].reshape(3, 1, 9, 128)
+    low_x, high_x = jnp.where(core == 0, outer, inner), jnp.where(core == 0, inner, outer)
+    image = jnp.concatenate([low_x, partial[:, 1:4], high_x], 1)
     row = jnp.sum(lax.all_to_all(spread, DOM, 0, 0, tiled=True), 0)
-    row = jnp.pad(row, (0, 112))[None]
+    row = jnp.pad(row, ((0, 0), (0, 112)))
     low = jnp.concatenate([image[:, :, 0].reshape(15, 128), row], 0)
     high = jnp.concatenate([image[:, :, 8].reshape(15, 128), row], 0)
     peer = jnp.arange(subs, dtype=jnp.int32)[:, None, None]
     gathered = lax.all_to_all(jnp.where(peer == above, high, low), "sub", 0, 0, tiled=True)
     accel, residual = local_call(
-        finish_kernel, "finish", (field, field), (), place, gathered, image, t0, t1, t2
+        finish_kernel, "finish", (turned, turned), (), gathered, image, t0, t1, t2
     )
-    return (accel, residual, energy_rate)
+    return (jnp.transpose(accel, (2, 0, 1, 3)), jnp.transpose(residual, (2, 0, 1, 3)), energy_rate)
 
 
 def solution(mesh):

time: 98.4 us -> 87 us (0.88)
  the two profiles are of different devices: /device:TPU:32 before, /device:TPU:1 now
where the time goes in v4:
time: 87 us; the launch traced here: 86.1 us
  blocking collectives  40.8 us (47%)
  starting transfers between devices  25.9 us (30%)
  Pallas kernels  14.6 us (17%)
  waiting for transfers between devices  1.92 us (2%)
  local copies, waits for them, and re-layouts  1.8 us (2%)
    all_gather x5, blocking collectives, pair_gather(): lax.all_gather(block, axes, axis_index_groups=pair_groups(axes, offset))  25.7 us
    ppermute x2, starting transfers between devices, pair_swap(): lax.ppermute(block, axes, [edge for a, b in groups for edge in ((a, b), (...  17.3 us
    all_to_all x1, blocking collectives, per_device(): lax.all_to_all(jnp.where(peer == above, high, low), 'sub', 0, 0, tiled=True)  15.1 us
    pallas_call x4, Pallas kernels, local_call(): pl.pallas_call(kernel, out_shape=[jax.ShapeDtypeStruct(shape, jnp.float32...  14.6 us
    all_to_all x1, starting transfers between devices, per_device(): row = jnp.sum(lax.all_to_all(spread, DOM, 0, 0, tiled=True), 0)  8.58 us
    ppermute x2, waiting for transfers between devices, pair_swap(): lax.ppermute(block, axes, [edge for a, b in groups for edge in ((a, b), (...  1.92 us
  transfers between devices with their start and end apart: 3, of which 1 were waited for; matrix products, arithmetic and copies ran while one was open for 0% of the time, Pallas kernels for 0%

profile of v4, /device:TPU:1, one launch (start us, length us, event | category | flops | bytes accessed | tf_op | source)
XLA Modules:
  0.0 86.1 jit_solution(8427779497542815731)
XLA Ops:
  0.6 3.9 %force.1 = (f32[3,5,9,128]{3,2,1,0:T(8,128)}, f32[8,2,4,64]{3,2,1,0:T(4,128)}, f32[9,8,128]{2,1,0:T(8,128)}, f32[9,8,128]{2,1,0:T(8,128)}, f32[152,128]{1,0:T(8,128)}, /*index=5*/f32[152,128]{1,0:T(8,128)}) custom-call(f32[5,9,3,128]{3,2,1,0:T(4,128)} %bitcast.14, f32[5,9,3,128]{3,2,1,0:T(4,128)} %bitcast.15, f32[8,2,4,64]{3,2,1,0:T(4,128)} %energy.1, ...), custom_call_target="tpu_custom_call" | custom-call | tf_op jit(solution)/shard_map/force/pallas_call | solution.py:574
  4.6 4.8 %collective-permute-start = (f32[152,128]{1,0:T(8,128)}, f32[152,128]{1,0:T(8,128)S(1)}, u32[]{:S(2)}, u32[]{:S(2)}) collective-permute-start(f32[152,128]{1,0:T(8,128)} %get-tuple-element.18), channel_id=1, source_target_pairs={{0,1},{1,0},{2,3},{3,2},{4,5},{5,4},{6,7},{7,6},{8,9},{9,8},{10,11... | collective-permute-start | bytes 233480 | tf_op jit(solution)/shard_map/ppermute | solution.py:590
  9.4 12.5 %collective-permute-start.1 = (f32[152,128]{1,0:T(8,128)}, f32[152,128]{1,0:T(8,128)S(1)}, u32[]{:S(2)}, u32[]{:S(2)}) collective-permute-start(f32[152,128]{1,0:T(8,128)} %get-tuple-element.19), channel_id=1, source_target_pairs={{1,2},{2,1},{3,4},{4,3},{5,6},{6,5},{7,8},{8,7},{9,10},{10,9},{11,... | collective-permute-start | bytes 233480 | tf_op jit(solution)/shard_map/ppermute | solution.py:590
  21.9 0.0 collective-permute-done.inner
  21.9 0.0 copy-start.4
  21.9 1.9 %collective-permute-done.1.outer = f32[152,128]{1,0:T(8,128)S(1)} collective-permute-done((f32[152,128]{1,0:T(8,128)}, f32[152,128]{1,0:T(8,128)S(1)}, u32[]{:S(2)}, u32[]{:S(2)}) %collective-permute-start.1) | collective-permute-done | bytes 77856 | tf_op jit(solution)/shard_map/ppermute | solution.py:590
  23.9 0.0 copy-start.5
  23.9 0.0 copy-done.4
  23.9 0.6 copy-done.5
  24.5 1.8 %widen.1 = f32[568,128]{1,0:T(8,128)} custom-call(f32[152,128]{1,0:T(8,128)} %copy-done.4, f32[152,128]{1,0:T(8,128)} %copy-done.5, f32[3,5,9,128]{3,2,1,0:T(8,128)} %get-tuple-element.20.force, f32[9,8,128]{2,1,0:T(8,128)} %get-tuple-element.21.near, f32[9,8,128]{2,1,0:T(8,128)} %get-tuple-element.22.far), custom_call_target="tpu_custom_call" | custom-call | tf_op jit(solution)/shard_map/widen/pallas_call | solution.py:574
  26.3 0.0 copy-start
  26.3 4.0 %all-gather = f32[1136,128]{1,0:T(8,128)S(1)} all-gather(f32[568,128]{1,0:T(8,128)} %widen.1), channel_id=2, replica_groups={{0,12},{24,36},{48,60},{72,84},{96,108},{120,132},{144,156},{168,180},{..., dimensions={0}, use_global_device_ids=true | all-gather | bytes 872448 | tf_op jit(solution)/shard_map/all_gather | solution.py:585
  30.3 0.0 copy-start.1
  30.3 0.0 copy-done
  30.3 7.1 %all_gather.28.cross = f32[2,568,128]{2,1,0:T(8,128)S(1)} all-gather(f32[1,568,128]{2,1,0:T(8,128)S(1)} %fusion), channel_id=1, replica_groups={{12,24},{36,48},{60,72},{84,96},{108,120},{132,144},{156,168},{180,192}..., dimensions={0}, use_global_device_ids=true | all-gather | bytes 872448 | tf_op jit(solution)/shard_map/all_gather | solution.py:585
  37.4 0.0 copy-start.2
  37.4 5.4 %all_gather.29.edges = f32[2,56,128]{2,1,0:T(8,128)} all-gather(f32[1,56,128]{2,1,0:T(8,128)S(1)} %slice_add_fusion), channel_id=1, replica_groups={{0,12},{24,36},{48,60},{72,84},{96,108},{120,132},{144,156},{168,180},{..., dimensions={0}, use_global_device_ids=true | all-gather | bytes 86016 | tf_op jit(solution)/shard_map/all_gather | solution.py:585
  42.8 0.0 copy-done.1
  42.8 0.0 copy-done.2
  42.8 6.2 %krylov.1 = (f32[3,5,9,128]{3,2,1,0:T(8,128)}, f32[3,5,9,128]{3,2,1,0:T(8,128)}, f32[3,5,9,128]{3,2,1,0:T(8,128)}, f32[3,5,9,128]{3,2,1,0:T(8,128)}, f32[32,128]...) custom-call(f32[2,568,128]{2,1,0:T(8,128)} %bitcast.13, f32[2,568,128]{2,1,0:T(8,128)} %copy-done.2, ...), custom_call_target="tpu_custom_call" | custom-call | tf_op jit(solution)/shard_map/krylov/pallas_call | solution.py:574
  48.9 0.0 copy-start.8
  48.9 8.6 %all-to-all-start = ((f32[64,1,16]{2,1,0:T(1,128)}), f32[64,1,16]{2,1,0:T(1,128)S(1)}, u32[]{:S(2)}, u32[]{:S(2)}) async-start(f32[64,1,16]{2,1,0:T(1,128)} %get-tuple-element.26), calls=%async_computation | async-start | bytes 65536 | tf_op jit(solution)/shard_map/all_to_all | solution.py:637
  57.5 0.0 copy-done.8
  57.5 4.2 %all-gather.1 = f32[64,128]{1,0:T(8,128)S(1)} all-gather(f32[32,128]{1,0:T(8,128)S(1)} %copy-done.8), channel_id=3, replica_groups={{12,24},{36,48},{60,72},{84,96},{108,120},{132,144},{156,168},{180,192}..., dimensions={0}, use_global_device_ids=true | all-gather | bytes 49152 | tf_op jit(solution)/shard_map/all_gather | solution.py:585
  61.7 0.0 copy-start.7
  61.7 0.7 copy-done.7
  62.4 0.0 copy-start.6
  62.4 5.1 %all-gather.2 = f32[64,128]{1,0:T(8,128)S(1)} all-gather(f32[32,128]{1,0:T(8,128)S(1)} %copy-done.7), channel_id=4, replica_groups={{0,12},{24,36},{48,60},{72,84},{96,108},{120,132},{144,156},{168,180},{..., dimensions={0}, use_global_device_ids=true | all-gather | bytes 49152 | tf_op jit(solution)/shard_map/all_gather | solution.py:585
  67.5 0.0 copy-done.6
  67.6 0.0 copy-start.3
  67.7 0.0 all-to-all-done
  67.7 0.1 reduce_sum.11
  67.8 0.1 broadcast_select_fusion
  67.9 0.4 copy-done.3
  68.2 15.1 %all_to_all.10.gathered = f32[12,16,128]{2,1,0:T(8,128)} all-to-all(f32[12,16,128]{2,1,0:T(8,128)S(1)} %broadcast_select_fusion), channel_id=1, replica_groups=mesh['dom_0'=8,'dom_1'=4,'dom_2'=2,'sub'=12] {'sub'}, dimensions={0} | all-to-all | bytes 196608 | tf_op jit(solution)/shard_map/all_to_all | solution.py:642
  83.4 2.7 %finish.1 = (f32[5,9,3,128]{3,2,1,0:T(4,128)}, f32[5,9,3,128]{3,2,1,0:T(4,128)}) custom-call(f32[12,16,128]{2,1,0:T(8,128)} %all_to_all.10.gathered, f32[3,5,9,128]{3,2,1,0:T(8,128)} %copy-done.3, f32[3,5,9,128]{3,2,1,0:T(8,128)} %get-tuple-element.27.t0, f32[3,5,9,128]{3,2,1,0:T(8,128)} %get-tuple-element.28.t1, f32[3,5,9,128]{3,2,1,0:T(8,128)} %get-tuple-element.29.t2), custom_call_target="tpu_custom_call" | custom-call | tf_op jit(solution)/shard_map/finish/pallas_call | solution.py:574
  (14 shorter events, 0.1 us)
Async XLA Ops:
  4.6 17.4 %collective-permute-start = (f32[152,128]{1,0:T(8,128)}, f32[152,128]{1,0:T(8,128)S(1)}, u32[]{:S(2)}, u32[]{:S(2)}) collective-permute-start(f32[152,128]{1,0:T(8,128)} %get-tuple-element.18), channel_id=1, source_target_pairs={{0,1},{1,0},{2,3},{3,2},{4,5},{5,4},{6,7},{7,6},{8,9},{9,8},{10,11... | collective-permute-start | bytes 233480 | tf_op jit(solution)/shard_map/ppermute | solution.py:590
  9.4 14.4 %collective-permute-start.1 = (f32[152,128]{1,0:T(8,128)}, f32[152,128]{1,0:T(8,128)S(1)}, u32[]{:S(2)}, u32[]{:S(2)}) collective-permute-start(f32[152,128]{1,0:T(8,128)} %get-tuple-element.19), channel_id=1, source_target_pairs={{1,2},{2,1},{3,4},{4,3},{5,6},{6,5},{7,8},{8,7},{9,10},{10,9},{11,... | collective-permute-start | bytes 233480 | tf_op jit(solution)/shard_map/ppermute | solution.py:590
  21.9 1.9 %copy-start.4 = (f32[152,128]{1,0:T(8,128)}, f32[152,128]{1,0:T(8,128)S(1)}, u32[]{:S(2)}) copy-start(f32[152,128]{1,0:T(8,128)S(1)} %collective-permute-done.inner) | copy-start | bytes 233476
  23.9 0.6 copy-start.5
  26.3 4.0 %copy-start = (f32[568,128]{1,0:T(8,128)S(1)}, f32[568,128]{1,0:T(8,128)}, u32[]{:S(2)}) copy-start(f32[568,128]{1,0:T(8,128)} %widen.1) | copy-start | bytes 872452
  30.3 12.5 %copy-start.1 = (f32[1136,128]{1,0:T(8,128)}, f32[1136,128]{1,0:T(8,128)S(1)}, u32[]{:S(2)}) copy-start(f32[1136,128]{1,0:T(8,128)S(1)} %all-gather) | copy-start | bytes 1744900
  37.4 5.4 %copy-start.2 = (f32[2,568,128]{2,1,0:T(8,128)}, f32[2,568,128]{2,1,0:T(8,128)S(1)}, u32[]{:S(2)}) copy-start(f32[2,568,128]{2,1,0:T(8,128)S(1)} %all_gather.28.cross) | copy-start | bytes 1744900
  48.9 8.6 %copy-start.8 = (f32[32,128]{1,0:T(8,128)S(1)}, f32[32,128]{1,0:T(8,128)}, u32[]{:S(2)}) copy-start(f32[32,128]{1,0:T(8,128)} %get-tuple-element.23) | copy-start | bytes 49156
  48.9 18.7 %all-to-all-start = ((f32[64,1,16]{2,1,0:T(1,128)}), f32[64,1,16]{2,1,0:T(1,128)S(1)}, u32[]{:S(2)}, u32[]{:S(2)}) async-start(f32[64,1,16]{2,1,0:T(1,128)} %get-tuple-element.26), calls=%async_computation | async-start | bytes 65536 | tf_op jit(solution)/shard_map/all_to_all | solution.py:637
  61.7 0.7 copy-start.7
  62.4 5.1 %copy-start.6 = (f32[3,5,9,128]{3,2,1,0:T(8,128)S(1)}, f32[3,5,9,128]{3,2,1,0:T(8,128)}, u32[]{:S(2)}) copy-start(f32[3,5,9,128]{3,2,1,0:T(8,128)} %get-tuple-element.25) | copy-start | bytes 207364
  67.6 0.6 copy-start.3

commit v5 on v4

--- a/solution.py
+++ b/solution.py
@@ -577,6 +577,7 @@
         in_specs=[pl.BlockSpec(memory_space=pltpu.VMEM) for _ in operands],
         out_specs=[pl.BlockSpec(memory_space=pltpu.VMEM) for _ in outs],
         scratch_shapes=[pltpu.VMEM(shape, jnp.float32) for shape in scratch],
+        compiler_params=pltpu.CompilerParams(vmem_limit_bytes=12 * 1024 * 1024),
         name=name,
     )(*operands)
 

time: 87 us -> 85.3 us (0.980)
  Pallas kernels: 14.6 us -> 9.21 us
  local copies, waits for them, and re-layouts: 1.8 us -> 6.33 us
    pallas_call x4, Pallas kernels: 14.6 us -> 9.21 us  [local_call(): pl.pallas_call(kernel, out_shape=[jax.ShapeDtypeStruct(shape, jnp.float32...]
    unnamed x18 -> x16, local copies, waits for them, and re-layouts: 1.74 us -> 6.26 us
  transfers between devices with their start and end apart: 3 -> 3, of which waited for: 1 -> 2; matrix products, arithmetic and copies ran while one was open for 0% -> 0% of each run, Pallas kernels for 0% -> 0%
where the time goes in v5:
time: 85.3 us; the launch traced here: 84.2 us
  blocking collectives  40.1 us (47%)
  starting transfers between devices  25.7 us (30%)
  Pallas kernels  9.21 us (11%)
  local copies, waits for them, and re-layouts  6.33 us (7%)
  waiting for transfers between devices  1.78 us (2%)
    all_gather x5, blocking collectives, pair_gather(): lax.all_gather(block, axes, axis_index_groups=pair_groups(axes, offset))  25.1 us
    ppermute x2, starting transfers between devices, pair_swap(): lax.ppermute(block, axes, [edge for a, b in groups for edge in ((a, b), (...  17.3 us
    all_to_all x1, blocking collectives, per_device(): lax.all_to_all(jnp.where(peer == above, high, low), 'sub', 0, 0, tiled=True)  15 us
    pallas_call x4, Pallas kernels, local_call(): pl.pallas_call(kernel, out_shape=[jax.ShapeDtypeStruct(shape, jnp.float32...  9.21 us
    all_to_all x1, starting transfers between devices, per_device(): row = jnp.sum(lax.all_to_all(spread, DOM, 0, 0, tiled=True), 0)  8.44 us
    unnamed x16, local copies, waits for them, and re-layouts  6.26 us
    ppermute x2, waiting for transfers between devices, pair_swap(): lax.ppermute(block, axes, [edge for a, b in groups for edge in ((a, b), (...  1.72 us
  transfers between devices with their start and end apart: 3, of which 2 were waited for; matrix products, arithmetic and copies ran while one was open for 0% of the time, Pallas kernels for 0%

profile of v5, /device:TPU:1, one launch (start us, length us, event | category | flops | bytes accessed | tf_op | source)
XLA Modules:
  0.0 84.2 jit_solution(3948959778177215059)
XLA Ops:
  0.6 0.0 copy-start
  0.6 0.9 %copy-done = f32[27,2,4,64]{3,2,1,0:T(4,128)S(1)} copy-done((f32[27,2,4,64]{3,2,1,0:T(4,128)S(1)}, f32[27,2,4,64]{3,2,1,0:T(4,128)}, u32[]{:S(2)}) %copy-start) | copy-done | bytes 55320
  1.5 0.0 copy-start.1
  1.5 0.9 %copy-done.1 = f32[3,5,9,128]{3,0,2,1:T(4,128)S(1)} copy-done((f32[3,5,9,128]{3,0,2,1:T(4,128)S(1)}, f32[3,5,9,128]{3,0,2,1:T(4,128)}, u32[]{:S(2)}) %copy-start.1) | copy-done | bytes 69144
  2.4 0.0 copy-start.2
  2.4 0.9 %copy-done.2 = f32[3,5,9,128]{3,0,2,1:T(4,128)S(1)} copy-done((f32[3,5,9,128]{3,0,2,1:T(4,128)S(1)}, f32[3,5,9,128]{3,0,2,1:T(4,128)}, u32[]{:S(2)}) %copy-start.2) | copy-done | bytes 69144
  3.3 0.0 copy-start.3
  3.3 0.8 copy-done.3
  4.1 0.0 copy-start.4
  4.1 0.7 copy-done.4
  4.8 0.0 copy-start.5
  4.8 0.7 copy-done.5
  5.5 0.0 copy-start.6
  5.5 0.7 copy-done.6
  6.2 0.0 copy-start.7
  6.2 0.7 copy-done.7
  6.9 2.8 %force.1 = (f32[3,5,9,128]{3,2,1,0:T(8,128)S(1)}, f32[8,2,4,64]{3,2,1,0:T(4,128)}, f32[9,8,128]{2,1,0:T(8,128)S(1)}, f32[9,8,128]{2,1,0:T(8,128)S(1)}, f32[152,128]{1,0:T(8,128)S(1)}, /*index=5*/f32[152,128]{1,0:T(8,128)S(1)}) custom-call(f32[5,9,3,128]{3,2,1,0:T(4,128)S(1)} %bitcast.14, f32[5,9,3,128]{3,2,1,0:T(4,128)S(1)} %bitcast.15, ...), custom_call_target="tpu_custom_call" | custom-call | tf_op jit(solution)/shard_map/force/pallas_call | solution.py:574
  9.7 4.8 %collective-permute-start = (f32[152,128]{1,0:T(8,128)S(1)}, f32[152,128]{1,0:T(8,128)S(1)}, u32[]{:S(2)}, u32[]{:S(2)}) collective-permute-start(f32[152,128]{1,0:T(8,128)S(1)} %get-tuple-element.18), channel_id=1, source_target_pairs={{0,1},{1,0},{2,3},{3,2},{4,5},{5,4},{6,7},{7,6},{8,9},{9,8},{10,11... | collective-permute-start | bytes 233480 | tf_op jit(solution)/shard_map/ppermute | solution.py:591
  14.6 12.5 %collective-permute-start.1 = (f32[152,128]{1,0:T(8,128)S(1)}, f32[152,128]{1,0:T(8,128)S(1)}, u32[]{:S(2)}, u32[]{:S(2)}) collective-permute-start(f32[152,128]{1,0:T(8,128)S(1)} %get-tuple-element.19), channel_id=1, source_target_pairs={{1,2},{2,1},{3,4},{4,3},{5,6},{6,5},{7,8},{8,7},{9,10},{10,9},{11,... | collective-permute-start | bytes 233480 | tf_op jit(solution)/shard_map/ppermute | solution.py:591
  27.1 0.0 collective-permute-done.inner
  27.1 1.7 %collective-permute-done.1.outer = f32[152,128]{1,0:T(8,128)S(1)} collective-permute-done((f32[152,128]{1,0:T(8,128)S(1)}, f32[152,128]{1,0:T(8,128)S(1)}, u32[]{:S(2)}, u32[]{:S(2)}) %collective-permute-start.1) | collective-permute-done | bytes 77856 | tf_op jit(solution)/shard_map/ppermute | solution.py:591
  28.8 0.1 widen.1
  28.9 3.7 %all-gather = f32[1136,128]{1,0:T(8,128)S(1)} all-gather(f32[568,128]{1,0:T(8,128)S(1)} %widen.1), channel_id=2, replica_groups={{0,12},{24,36},{48,60},{72,84},{96,108},{120,132},{144,156},{168,180},{..., dimensions={0}, use_global_device_ids=true | all-gather | bytes 872448 | tf_op jit(solution)/shard_map/all_gather | solution.py:586
  32.6 7.1 %all_gather.28.cross = f32[2,568,128]{2,1,0:T(8,128)S(1)} all-gather(f32[1,568,128]{2,1,0:T(8,128)S(1)} %fusion), channel_id=1, replica_groups={{12,24},{36,48},{60,72},{84,96},{108,120},{132,144},{156,168},{180,192}..., dimensions={0}, use_global_device_ids=true | all-gather | bytes 872448 | tf_op jit(solution)/shard_map/all_gather | solution.py:586
  39.6 5.2 %all_gather.29.edges = f32[2,56,128]{2,1,0:T(8,128)S(1)} all-gather(f32[1,56,128]{2,1,0:T(8,128)S(1)} %slice_add_fusion), channel_id=1, replica_groups={{0,12},{24,36},{48,60},{72,84},{96,108},{120,132},{144,156},{168,180},{..., dimensions={0}, use_global_device_ids=true | all-gather | bytes 86016 | tf_op jit(solution)/shard_map/all_gather | solution.py:586
  44.9 4.7 %krylov.1 = (f32[3,5,9,128]{3,2,1,0:T(8,128)S(1)}, f32[3,5,9,128]{3,2,1,0:T(8,128)S(1)}, f32[3,5,9,128]{3,2,1,0:T(8,128)S(1)}, f32[3,5,9,128]{3,2,1,0:T(8,128)S(...) custom-call(f32[2,568,128]{2,1,0:T(8,128)S(1)} %bitcast.13, ...), custom_call_target="tpu_custom_call" | custom-call | tf_op jit(solution)/shard_map/krylov/pallas_call | solution.py:574
  49.6 8.4 %all-to-all-start = ((f32[64,1,16]{2,1,0:T(1,128)}), f32[64,1,16]{2,1,0:T(1,128)S(1)}, u32[]{:S(2)}, u32[]{:S(2)}) async-start(f32[64,1,16]{2,1,0:T(1,128)} %get-tuple-element.26), calls=%async_computation | async-start | bytes 65536 | tf_op jit(solution)/shard_map/all_to_all | solution.py:638
  58.0 4.2 %all-gather.1 = f32[64,128]{1,0:T(8,128)S(1)} all-gather(f32[32,128]{1,0:T(8,128)S(1)} %get-tuple-element.23), channel_id=3, replica_groups={{12,24},{36,48},{60,72},{84,96},{108,120},{132,144},{156,168},{180,192}..., dimensions={0}, use_global_device_ids=true | all-gather | bytes 49152 | tf_op jit(solution)/shard_map/all_gather | solution.py:586
  62.2 5.0 %all-gather.2 = f32[64,128]{1,0:T(8,128)S(1)} all-gather(f32[32,128]{1,0:T(8,128)S(1)} %get-tuple-element.24), channel_id=4, replica_groups={{0,12},{24,36},{48,60},{72,84},{96,108},{120,132},{144,156},{168,180},{..., dimensions={0}, use_global_device_ids=true | all-gather | bytes 49152 | tf_op jit(solution)/shard_map/all_gather | solution.py:586
  67.3 0.1 all-to-all-done
  67.4 0.1 reduce_sum.11
  67.5 0.1 broadcast_select_fusion
  67.6 15.0 %all_to_all.10.gathered = f32[12,16,128]{2,1,0:T(8,128)S(1)} all-to-all(f32[12,16,128]{2,1,0:T(8,128)S(1)} %broadcast_select_fusion), channel_id=1, replica_groups=mesh['dom_0'=8,'dom_1'=4,'dom_2'=2,'sub'=12] {'sub'}, dimensions={0} | all-to-all | bytes 196608 | tf_op jit(solution)/shard_map/all_to_all | solution.py:643
  82.6 1.6 %finish.1 = (f32[5,9,3,128]{3,2,1,0:T(4,128)}, f32[5,9,3,128]{3,2,1,0:T(4,128)}) custom-call(f32[12,16,128]{2,1,0:T(8,128)S(1)} %all_to_all.10.gathered, f32[3,5,9,128]{3,2,1,0:T(8,128)S(1)} %pad_maximum_fusion.image, f32[3,5,9,128]{3,2,1,0:T(8,128)S(1)} %get-tuple-element.27.t0, f32[3,5,9,128]{3,2,1,0:T(8,128)S(1)} %get-tuple-element.28.t1, ...), custom_call_target="tpu_custom_call" | custom-call | tf_op jit(solution)/shard_map/finish/pallas_call | solution.py:574
  (14 shorter events, 0.1 us)
Async XLA Ops:
  0.6 0.9 %copy-start = (f32[27,2,4,64]{3,2,1,0:T(4,128)S(1)}, f32[27,2,4,64]{3,2,1,0:T(4,128)}, u32[]{:S(2)}) copy-start(f32[27,2,4,64]{3,2,1,0:T(4,128)} %rho.1) | copy-start | bytes 165892
  1.5 0.9 %copy-start.1 = (f32[3,5,9,128]{3,0,2,1:T(4,128)S(1)}, f32[3,5,9,128]{3,0,2,1:T(4,128)}, u32[]{:S(2)}) copy-start(f32[3,5,9,128]{3,0,2,1:T(4,128)} %param.9) | copy-start | bytes 207364
  2.4 0.9 %copy-start.2 = (f32[3,5,9,128]{3,0,2,1:T(4,128)S(1)}, f32[3,5,9,128]{3,0,2,1:T(4,128)}, u32[]{:S(2)}) copy-start(f32[3,5,9,128]{3,0,2,1:T(4,128)} %param.8) | copy-start | bytes 207364
  3.3 0.8 copy-start.3
  4.1 0.7 copy-start.4
  4.8 0.7 copy-start.5
  5.5 0.7 copy-start.6
  6.2 0.7 copy-start.7
  9.7 17.4 %collective-permute-start = (f32[152,128]{1,0:T(8,128)S(1)}, f32[152,128]{1,0:T(8,128)S(1)}, u32[]{:S(2)}, u32[]{:S(2)}) collective-permute-start(f32[152,128]{1,0:T(8,128)S(1)} %get-tuple-element.18), channel_id=1, source_target_pairs={{0,1},{1,0},{2,3},{3,2},{4,5},{5,4},{6,7},{7,6},{8,9},{9,8},{10,11... | collective-permute-start | bytes 233480 | tf_op jit(solution)/shard_map/ppermute | solution.py:591
  14.6 14.2 %collective-permute-start.1 = (f32[152,128]{1,0:T(8,128)S(1)}, f32[152,128]{1,0:T(8,128)S(1)}, u32[]{:S(2)}, u32[]{:S(2)}) collective-permute-start(f32[152,128]{1,0:T(8,128)S(1)} %get-tuple-element.19), channel_id=1, source_target_pairs={{1,2},{2,1},{3,4},{4,3},{5,6},{6,5},{7,8},{8,7},{9,10},{10,9},{11,... | collective-permute-start | bytes 233480 | tf_op jit(solution)/shard_map/ppermute | solution.py:591
  49.6 17.8 %all-to-all-start = ((f32[64,1,16]{2,1,0:T(1,128)}), f32[64,1,16]{2,1,0:T(1,128)S(1)}, u32[]{:S(2)}, u32[]{:S(2)}) async-start(f32[64,1,16]{2,1,0:T(1,128)} %get-tuple-element.26), calls=%async_computation | async-start | bytes 65536 | tf_op jit(solution)/shard_map/all_to_all | solution.py:638

commit v6 on v4

--- a/solution.py
+++ b/solution.py
@@ -143,13 +143,17 @@
     return jnp.dot(left, right, precision=highest, preferred_element_type=jnp.float32)
 
 
-def force_kernel(disp, vel, energy, rho, share, portion, ident, mix, force, rate, near_out, far_out, inner, outer, grad, work, node):
+def force_kernel(*refs):
+    sources, (force, rate, planes, inner, outer) = refs[:8], refs[8:13]
+    grad, work, node, sems = refs[13:16] + refs[24:]
+    near_out, far_out = planes.at[0:9], planes.at[9:18]
+    disp, vel, energy, rho, share, portion, ident, mix = refs[16:24]
+    copies = [pltpu.make_async_copy(a, b, sems.at[k]) for k, (a, b) in enumerate(zip(sources, refs[16:24]))]
+    for copy in copies:
+        copy.start()
+    for copy in copies[2:]:
+        copy.wait()
     packs, rows = (0, 1), energy.shape[2]
-    for field, ref in enumerate((disp, vel)):
-        for x in range(5):
-            for y in range(9):
-                for comp in range(3):
-                    node[field, comp, x, y : y + 1, :] = ref[x, y, comp : comp + 1, :]
     count = 2 * rows
     even = even_lanes(count)
 
@@ -183,6 +187,13 @@
     near_point = jnp.where(even, POINTS[0], POINTS[1])
     a, b, c = SLOPE[0]
 
+    copies[0].wait()
+    copies[1].wait()
+    for field, ref in enumerate((disp, vel)):
+        for x in range(5):
+            for y in range(9):
+                for comp in range(3):
+                    node[field, comp, x, y : y + 1, :] = ref[x, y, comp : comp + 1, :]
     for field in range(2):
         for comp in range(3):
             nodes = corners(node.at[field], comp, packs, rows)
@@ -349,7 +360,7 @@
 BLOCK = MASS_AT + 8 * 36
 
 
-def widen_kernel(inner, outer, force, near, far, wide):
+def widen_kernel(inner, outer, force, planes, wide):
     def fill(lower, upper):
         for x in range(5):
             for comp in range(3):
@@ -363,9 +374,8 @@
         for zone in range(2):
             for p in range(18):
                 base, spot = MASS_AT + 8 * (18 * zone + p), 80 + 2 * (18 * zone + p)
-                source = near if p < 9 else far
                 wide[base : base + 2] = lower[spot : spot + 2]
-                wide[base + 2 : base + 6] = source[p % 9, 4 * zone : 4 * zone + 4, :]
+                wide[base + 2 : base + 6] = planes[p, 4 * zone : 4 * zone + 4, :]
                 wide[base + 6 : base + 8] = upper[spot : spot + 2]
 
     odd_sub = lax.rem(lax.axis_index("sub"), 2)
@@ -570,13 +580,15 @@
     return accel, residual
 
 
-def local_call(kernel, name, outs, scratch, *operands):
+def local_call(kernel, name, outs, scratch, *operands, fetch=False):
+    landing = [pltpu.VMEM(x.shape, x.dtype) for x in operands] + [pltpu.SemaphoreType.DMA((len(operands),))]
     return pl.pallas_call(
         kernel,
         out_shape=[jax.ShapeDtypeStruct(shape, jnp.float32) for shape in outs],
-        in_specs=[pl.BlockSpec(memory_space=pltpu.VMEM) for _ in operands],
+        in_specs=[pl.BlockSpec(memory_space=pltpu.HBM if fetch else pltpu.VMEM) for _ in operands],
         out_specs=[pl.BlockSpec(memory_space=pltpu.VMEM) for _ in outs],
-        scratch_shapes=[pltpu.VMEM(shape, jnp.float32) for shape in scratch],
+        scratch_shapes=[pltpu.VMEM(shape, jnp.float32) for shape in scratch] + (landing if fetch else []),
+        compiler_params=pltpu.CompilerParams(vmem_limit_bytes=(60 * 1024 if fetch else 12288) * 1024),
         name=name,
     )(*operands)
 
@@ -598,21 +610,21 @@
     subs = lax.axis_size("sub")
     above = (lax.axis_index("sub") + 1) % subs
     core = lax.axis_index("dom_2")
-    mass = (9, 8, 128)
     halo = (152, 128)
-    partial, energy_rate, near_mass, far_mass, inner, outer = local_call(
+    partial, energy_rate, planes, inner, outer = local_call(
         force_kernel,
         "force",
-        (field, energy.shape, mass, mass, halo, halo),
+        (field, energy.shape, (18, 8, 128), halo, halo),
         ((2, 2, 9, 9, 8, 128), (2, 9, 8, 128), (2,) + field),
         jnp.transpose(displacement, (1, 2, 0, 3)),
         jnp.transpose(velocity, (1, 2, 0, 3)),
         energy, rho_weight, mass_share, energy_share, material_id, mix_mask,
+        fetch=True,
     )
     inner = pair_swap(inner, ("sub",), 0)
     outer = pair_swap(outer, ("sub",), 1)
     (wide,) = local_call(
-        widen_kernel, "widen", ((BLOCK, 128),), (), inner, outer, partial, near_mass, far_mass
+        widen_kernel, "widen", ((BLOCK, 128),), (), inner, outer, partial, planes
     )
     pair = pair_gather(wide, DOM, 0)
     shared = pair[0, 4 * LAYER : 5 * LAYER] + pair[1, 0:LAYER]

time: 87 us -> 82.2 us (0.945)
  Pallas kernels: 14.6 us -> 10.6 us
    pallas_call x4, Pallas kernels: 14.6 us -> 10.6 us  [local_call(): pl.pallas_call(kernel, out_shape=[jax.ShapeDtypeStruct(shape, jnp.float32...]
    unnamed x18 -> x4, local copies, waits for them, and re-layouts: 1.74 us -> 1.79 us
  transfers between devices with their start and end apart: 3 -> 3, of which waited for: 1 -> 2; matrix products, arithmetic and copies ran while one was open for 0% -> 0% of each run, Pallas kernels for 0% -> 0%
where the time goes in v6:
time: 82.2 us; the launch traced here: 81.3 us
  blocking collectives  40.1 us (49%)
  starting transfers between devices  25.7 us (31%)
  Pallas kernels  10.6 us (13%)
  waiting for transfers between devices  1.99 us (2%)
  local copies, waits for them, and re-layouts  1.85 us (2%)
    all_gather x5, blocking collectives, pair_gather(): lax.all_gather(block, axes, axis_index_groups=pair_groups(axes, offset))  25.1 us
    ppermute x2, starting transfers between devices, pair_swap(): lax.ppermute(block, axes, [edge for a, b in groups for edge in ((a, b), (...  17.3 us
    all_to_all x1, blocking collectives, per_device(): lax.all_to_all(jnp.where(peer == above, high, low), 'sub', 0, 0, tiled=True)  15 us
    pallas_call x4, Pallas kernels, local_call(): pl.pallas_call(kernel, out_shape=[jax.ShapeDtypeStruct(shape, jnp.float32...  10.6 us
    all_to_all x1, starting transfers between devices, per_device(): row = jnp.sum(lax.all_to_all(spread, DOM, 0, 0, tiled=True), 0)  8.44 us
    ppermute x2, waiting for transfers between devices, pair_swap(): lax.ppermute(block, axes, [edge for a, b in groups for edge in ((a, b), (...  1.93 us
    unnamed x4, local copies, waits for them, and re-layouts  1.79 us
  transfers between devices with their start and end apart: 3, of which 2 were waited for; matrix products, arithmetic and copies ran while one was open for 0% of the time, Pallas kernels for 0%

profile of v6, /device:TPU:1, one launch (start us, length us, event | category | flops | bytes accessed | tf_op | source)
XLA Modules:
  0.0 81.3 jit_solution(9172866626063374636)
XLA Ops:
  0.6 4.2 %force.1 = (f32[3,5,9,128]{3,2,1,0:T(8,128)}, f32[8,2,4,64]{3,2,1,0:T(4,128)}, f32[18,8,128]{2,1,0:T(8,128)}, f32[152,128]{1,0:T(8,128)}, f32[152,128]{1,0:T(8,128)}) custom-call(f32[5,9,3,128]{3,2,1,0:T(4,128)} %bitcast.14, f32[5,9,3,128]{3,2,1,0:T(4,128)} %bitcast.15, f32[8,2,4,64]{3,2,1,0:T(4,128)} %refs_2_.1, f32[27,2,4,64]{3,2,1,0:T(4,128)} %refs_3_.1, ...), custom_call_target="tpu_custom_call" | custom-call | tf_op jit(solution)/shard_map/force/pallas_call | solution.py:585
  4.8 4.8 %collective-permute-start = (f32[152,128]{1,0:T(8,128)}, f32[152,128]{1,0:T(8,128)S(1)}, u32[]{:S(2)}, u32[]{:S(2)}) collective-permute-start(f32[152,128]{1,0:T(8,128)} %get-tuple-element.17), channel_id=1, source_target_pairs={{0,1},{1,0},{2,3},{3,2},{4,5},{5,4},{6,7},{7,6},{8,9},{9,8},{10,11... | collective-permute-start | bytes 233480 | tf_op jit(solution)/shard_map/ppermute | solution.py:602
  9.7 12.5 %collective-permute-start.1 = (f32[152,128]{1,0:T(8,128)}, f32[152,128]{1,0:T(8,128)S(1)}, u32[]{:S(2)}, u32[]{:S(2)}) collective-permute-start(f32[152,128]{1,0:T(8,128)} %get-tuple-element.18), channel_id=1, source_target_pairs={{1,2},{2,1},{3,4},{4,3},{5,6},{6,5},{7,8},{8,7},{9,10},{10,9},{11,... | collective-permute-start | bytes 233480 | tf_op jit(solution)/shard_map/ppermute | solution.py:602
  22.2 0.0 collective-permute-done.inner
  22.2 1.9 %collective-permute-done.1.outer = f32[152,128]{1,0:T(8,128)S(1)} collective-permute-done((f32[152,128]{1,0:T(8,128)}, f32[152,128]{1,0:T(8,128)S(1)}, u32[]{:S(2)}, u32[]{:S(2)}) %collective-permute-start.1) | collective-permute-done | bytes 77856 | tf_op jit(solution)/shard_map/ppermute | solution.py:602
  24.1 0.0 copy-start
  24.1 0.9 %copy-done = f32[3,5,9,128]{3,2,1,0:T(8,128)S(1)} copy-done((f32[3,5,9,128]{3,2,1,0:T(8,128)S(1)}, f32[3,5,9,128]{3,2,1,0:T(8,128)}, u32[]{:S(2)}) %copy-start) | copy-done | bytes 69144
  25.0 0.0 copy-start.1
  25.1 0.9 %copy-done.1 = f32[18,8,128]{2,1,0:T(8,128)S(1)} copy-done((f32[18,8,128]{2,1,0:T(8,128)S(1)}, f32[18,8,128]{2,1,0:T(8,128)}, u32[]{:S(2)}) %copy-start.1) | copy-done | bytes 73752
  25.9 0.1 widen.1
  26.0 3.7 %all-gather = f32[1136,128]{1,0:T(8,128)S(1)} all-gather(f32[568,128]{1,0:T(8,128)S(1)} %widen.1), channel_id=2, replica_groups={{0,12},{24,36},{48,60},{72,84},{96,108},{120,132},{144,156},{168,180},{..., dimensions={0}, use_global_device_ids=true | all-gather | bytes 872448 | tf_op jit(solution)/shard_map/all_gather | solution.py:597
  29.7 7.1 %all_gather.28.cross = f32[2,568,128]{2,1,0:T(8,128)S(1)} all-gather(f32[1,568,128]{2,1,0:T(8,128)S(1)} %fusion), channel_id=1, replica_groups={{12,24},{36,48},{60,72},{84,96},{108,120},{132,144},{156,168},{180,192}..., dimensions={0}, use_global_device_ids=true | all-gather | bytes 872448 | tf_op jit(solution)/shard_map/all_gather | solution.py:597
  36.8 5.2 %all_gather.29.edges = f32[2,56,128]{2,1,0:T(8,128)S(1)} all-gather(f32[1,56,128]{2,1,0:T(8,128)S(1)} %slice_add_fusion), channel_id=1, replica_groups={{0,12},{24,36},{48,60},{72,84},{96,108},{120,132},{144,156},{168,180},{..., dimensions={0}, use_global_device_ids=true | all-gather | bytes 86016 | tf_op jit(solution)/shard_map/all_gather | solution.py:597
  42.0 4.7 %krylov.1 = (f32[3,5,9,128]{3,2,1,0:T(8,128)S(1)}, f32[3,5,9,128]{3,2,1,0:T(8,128)S(1)}, f32[3,5,9,128]{3,2,1,0:T(8,128)S(1)}, f32[3,5,9,128]{3,2,1,0:T(8,128)S(...) custom-call(f32[2,568,128]{2,1,0:T(8,128)S(1)} %bitcast.13, ...), custom_call_target="tpu_custom_call" | custom-call | tf_op jit(solution)/shard_map/krylov/pallas_call | solution.py:585
  46.7 8.4 %all-to-all-start = ((f32[64,1,16]{2,1,0:T(1,128)}), f32[64,1,16]{2,1,0:T(1,128)S(1)}, u32[]{:S(2)}, u32[]{:S(2)}) async-start(f32[64,1,16]{2,1,0:T(1,128)} %get-tuple-element.24), calls=%async_computation | async-start | bytes 65536 | tf_op jit(solution)/shard_map/all_to_all | solution.py:649
  55.2 4.2 %all-gather.1 = f32[64,128]{1,0:T(8,128)S(1)} all-gather(f32[32,128]{1,0:T(8,128)S(1)} %get-tuple-element.21), channel_id=3, replica_groups={{12,24},{36,48},{60,72},{84,96},{108,120},{132,144},{156,168},{180,192}..., dimensions={0}, use_global_device_ids=true | all-gather | bytes 49152 | tf_op jit(solution)/shard_map/all_gather | solution.py:597
  59.3 5.0 %all-gather.2 = f32[64,128]{1,0:T(8,128)S(1)} all-gather(f32[32,128]{1,0:T(8,128)S(1)} %get-tuple-element.22), channel_id=4, replica_groups={{0,12},{24,36},{48,60},{72,84},{96,108},{120,132},{144,156},{168,180},{..., dimensions={0}, use_global_device_ids=true | all-gather | bytes 49152 | tf_op jit(solution)/shard_map/all_gather | solution.py:597
  64.4 0.1 all-to-all-done
  64.5 0.1 reduce_sum.11
  64.6 0.1 broadcast_select_fusion
  64.7 15.0 %all_to_all.10.gathered = f32[12,16,128]{2,1,0:T(8,128)S(1)} all-to-all(f32[12,16,128]{2,1,0:T(8,128)S(1)} %broadcast_select_fusion), channel_id=1, replica_groups=mesh['dom_0'=8,'dom_1'=4,'dom_2'=2,'sub'=12] {'sub'}, dimensions={0} | all-to-all | bytes 196608 | tf_op jit(solution)/shard_map/all_to_all | solution.py:654
  79.7 1.6 %finish.1 = (f32[5,9,3,128]{3,2,1,0:T(4,128)}, f32[5,9,3,128]{3,2,1,0:T(4,128)}) custom-call(f32[12,16,128]{2,1,0:T(8,128)S(1)} %all_to_all.10.gathered, f32[3,5,9,128]{3,2,1,0:T(8,128)S(1)} %pad_maximum_fusion.image, f32[3,5,9,128]{3,2,1,0:T(8,128)S(1)} %get-tuple-element.25.t0, f32[3,5,9,128]{3,2,1,0:T(8,128)S(1)} %get-tuple-element.26.t1, ...), custom_call_target="tpu_custom_call" | custom-call | tf_op jit(solution)/shard_map/finish/pallas_call | solution.py:585
  (14 shorter events, 0.1 us)
Async XLA Ops:
  4.8 17.4 %collective-permute-start = (f32[152,128]{1,0:T(8,128)}, f32[152,128]{1,0:T(8,128)S(1)}, u32[]{:S(2)}, u32[]{:S(2)}) collective-permute-start(f32[152,128]{1,0:T(8,128)} %get-tuple-element.17), channel_id=1, source_target_pairs={{0,1},{1,0},{2,3},{3,2},{4,5},{5,4},{6,7},{7,6},{8,9},{9,8},{10,11... | collective-permute-start | bytes 233480 | tf_op jit(solution)/shard_map/ppermute | solution.py:602
  9.7 14.4 %collective-permute-start.1 = (f32[152,128]{1,0:T(8,128)}, f32[152,128]{1,0:T(8,128)S(1)}, u32[]{:S(2)}, u32[]{:S(2)}) collective-permute-start(f32[152,128]{1,0:T(8,128)} %get-tuple-element.18), channel_id=1, source_target_pairs={{1,2},{2,1},{3,4},{4,3},{5,6},{6,5},{7,8},{8,7},{9,10},{10,9},{11,... | collective-permute-start | bytes 233480 | tf_op jit(solution)/shard_map/ppermute | solution.py:602
  24.1 0.9 %copy-start = (f32[3,5,9,128]{3,2,1,0:T(8,128)S(1)}, f32[3,5,9,128]{3,2,1,0:T(8,128)}, u32[]{:S(2)}) copy-start(f32[3,5,9,128]{3,2,1,0:T(8,128)} %get-tuple-element.19.force) | copy-start | bytes 207364
  25.0 0.9 %copy-start.1 = (f32[18,8,128]{2,1,0:T(8,128)S(1)}, f32[18,8,128]{2,1,0:T(8,128)}, u32[]{:S(2)}) copy-start(f32[18,8,128]{2,1,0:T(8,128)} %get-tuple-element.20.planes) | copy-start | bytes 221188
  46.7 17.8 %all-to-all-start = ((f32[64,1,16]{2,1,0:T(1,128)}), f32[64,1,16]{2,1,0:T(1,128)S(1)}, u32[]{:S(2)}, u32[]{:S(2)}) async-start(f32[64,1,16]{2,1,0:T(1,128)} %get-tuple-element.24), calls=%async_computation | async-start | bytes 65536 | tf_op jit(solution)/shard_map/all_to_all | solution.py:649

commit v7 on v6

--- a/solution.py
+++ b/solution.py
@@ -144,11 +144,10 @@
 
 
 def force_kernel(*refs):
-    sources, (force, rate, planes, inner, outer) = refs[:8], refs[8:13]
-    grad, work, node, sems = refs[13:16] + refs[24:]
-    near_out, far_out = planes.at[0:9], planes.at[9:18]
-    disp, vel, energy, rho, share, portion, ident, mix = refs[16:24]
-    copies = [pltpu.make_async_copy(a, b, sems.at[k]) for k, (a, b) in enumerate(zip(sources, refs[16:24]))]
+    sources, (own, rate, inner, outer) = refs[:8], refs[8:12]
+    grad, work, node, force, near_out, far_out, sems = refs[12:18] + refs[26:]
+    disp, vel, energy, rho, share, portion, ident, mix = refs[18:26]
+    copies = [pltpu.make_async_copy(a, b, sems.at[k]) for k, (a, b) in enumerate(zip(sources, refs[18:26]))]
     for copy in copies:
         copy.start()
     for copy in copies[2:]:
@@ -328,6 +327,16 @@
                 base = count * jxy + rows * zone
                 rate[2 * jxy + jz, zone] = ratio[base : base + rows]
 
+    for p in range(9):
+        own[8 * p : 8 * p + 8] = near_out[p]
+    for k in range(5):
+        paired = far_out[2 * k] if k == 4 else far_out[2 * k] + turn(far_out[2 * k + 1], 1)
+        own[8 * (9 + k) : 8 * (10 + k)] = paired
+    own[247:248] = jnp.zeros((1, 128), jnp.float32)
+    for comp in range(3):
+        for x in range(5):
+            own[112 + 9 * (5 * comp + x) : 121 + 9 * (5 * comp + x)] = force[comp, x]
+
     def pack(ref, high):
         nodes_at, zones_at = (4, 2) if high else (0, 0)
         ref[75:80] = jnp.zeros((5, 128), jnp.float32)
@@ -336,11 +345,10 @@
                 spot = 5 * (3 * x + comp)
                 ref[spot : spot + 5] = force[comp, x, nodes_at : nodes_at + 5, :]
         for zone in range(2):
-            for p in range(18):
-                spot = 80 + 2 * (18 * zone + p)
-                source = near_out if p < 9 else far_out
-                base = rows * zone + zones_at
-                ref[spot : spot + 2] = source[p % 9, base : base + 2, :]
+            for p in range(14):
+                spot = 80 + 2 * (14 * zone + p)
+                base = 8 * p + rows * zone + zones_at
+                ref[spot : spot + 2] = own[base : base + 2]
 
     odd_sub = lax.rem(lax.axis_index("sub"), 2)
 
@@ -357,25 +365,25 @@
 
 LAYER = 56
 MASS_AT = 5 * LAYER
-BLOCK = MASS_AT + 8 * 36
-
-
-def widen_kernel(inner, outer, force, planes, wide):
+BLOCK = MASS_AT + 8 * 28
+
+
+def widen_kernel(inner, outer, own, wide):
     def fill(lower, upper):
         for x in range(5):
             for comp in range(3):
-                base, spot = LAYER * x + 17 * comp, 5 * (3 * x + comp)
+                base, spot, at = LAYER * x + 17 * comp, 5 * (3 * x + comp), 112 + 9 * (5 * comp + x)
                 wide[base : base + 4] = lower[spot : spot + 4]
-                wide[base + 4 : base + 5] = lower[spot + 4 : spot + 5] + force[comp, x, 0:1, :]
-                wide[base + 5 : base + 12] = force[comp, x, 1:8, :]
-                wide[base + 12 : base + 13] = force[comp, x, 8:9, :] + upper[spot : spot + 1]
+                wide[base + 4 : base + 5] = lower[spot + 4 : spot + 5] + own[at : at + 1]
+                wide[base + 5 : base + 12] = own[at + 1 : at + 8]
+                wide[base + 12 : base + 13] = own[at + 8 : at + 9] + upper[spot : spot + 1]
                 wide[base + 13 : base + 17] = upper[spot + 1 : spot + 5]
             wide[LAYER * x + 51 : LAYER * (x + 1)] = jnp.zeros((5, 128), jnp.float32)
         for zone in range(2):
-            for p in range(18):
-                base, spot = MASS_AT + 8 * (18 * zone + p), 80 + 2 * (18 * zone + p)
+            for p in range(14):
+                base, spot = MASS_AT + 8 * (14 * zone + p), 80 + 2 * (14 * zone + p)
                 wide[base : base + 2] = lower[spot : spot + 2]
-                wide[base + 2 : base + 6] = planes[p, 4 * zone : 4 * zone + 4, :]
+                wide[base + 2 : base + 6] = own[8 * p + 4 * zone : 8 * p + 4 * zone + 4]
                 wide[base + 6 : base + 8] = upper[spot : spot + 2]
 
     odd_sub = lax.rem(lax.axis_index("sub"), 2)
@@ -391,6 +399,8 @@
 
 def krylov_kernel(pair, cross, edges, t0, t1, t2, partial, inner, outer, products, node, image, second, mass):
     core = lax.axis_index("dom_2")
+    lanes = even_lanes(8)
+
     def fill(layers, blocks):
         for at, (ref, base) in enumerate(layers):
             for comp in range(3):
@@ -398,9 +408,15 @@
                 node[comp, at] = ref[spot : spot + 17]
         for at, ref in enumerate(blocks):
             for k in range(2):
-                for p in range(18):
-                    spot = MASS_AT + 8 * (18 * k + p)
-                    mass[2 * at + k, p] = ref[spot : spot + 8]
+                for p in range(14):
+                    spot = MASS_AT + 8 * (14 * k + p)
+                    plane = ref[spot : spot + 8]
+                    if p < 9:
+                        mass[2 * at + k, p] = plane
+                    else:
+                        mass[2 * at + k, 2 * p - 9] = jnp.where(lanes, plane, 0.0)
+                        if p < 13:
+                            mass[2 * at + k, 2 * p - 8] = jnp.where(lanes, turn(plane, -1), 0.0)
 
     shared = pair[0, 4 * LAYER : 5 * LAYER] + pair[1, 0:LAYER]
 
@@ -610,12 +626,12 @@
     subs = lax.axis_size("sub")
     above = (lax.axis_index("sub") + 1) % subs
     core = lax.axis_index("dom_2")
-    halo = (152, 128)
-    partial, energy_rate, planes, inner, outer = local_call(
+    halo = (136, 128)
+    own, energy_rate, inner, outer = local_call(
         force_kernel,
         "force",
-        (field, energy.shape, (18, 8, 128), halo, halo),
-        ((2, 2, 9, 9, 8, 128), (2, 9, 8, 128), (2,) + field),
+        ((248, 128), energy.shape, halo, halo),
+        ((2, 2, 9, 9, 8, 128), (2, 9, 8, 128), (2,) + field, field, (9, 8, 128), (9, 8, 128)),
         jnp.transpose(displacement, (1, 2, 0, 3)),
         jnp.transpose(velocity, (1, 2, 0, 3)),
         energy, rho_weight, mass_share, energy_share, material_id, mix_mask,
@@ -624,7 +640,7 @@
     inner = pair_swap(inner, ("sub",), 0)
     outer = pair_swap(outer, ("sub",), 1)
     (wide,) = local_call(
-        widen_kernel, "widen", ((BLOCK, 128),), (), inner, outer, partial, planes
+        widen_kernel, "widen", ((BLOCK, 128),), (), inner, outer, own
     )
     pair = pair_gather(wide, DOM, 0)
     shared = pair[0, 4 * LAYER : 5 * LAYER] + pair[1, 0:LAYER]

time: 82.2 us -> 80.8 us (0.983)
  local copies, waits for them, and re-layouts: 1.85 us -> 0.96 us
    unnamed x4 -> x2, local copies, waits for them, and re-layouts: 1.79 us -> 0.9 us
where the time goes in v7:
time: 80.8 us; the launch traced here: 79.9 us
  blocking collectives  39.7 us (49%)
  starting transfers between devices  25.8 us (32%)
  Pallas kernels  10.6 us (13%)
  waiting for transfers between devices  1.91 us (2%)
  local copies, waits for them, and re-layouts  0.96 us (1%)
    all_gather x5, blocking collectives, pair_gather(): lax.all_gather(block, axes, axis_index_groups=pair_groups(axes, offset))  24.7 us
    ppermute x2, starting transfers between devices, pair_swap(): lax.ppermute(block, axes, [edge for a, b in groups for edge in ((a, b), (...  17.3 us
    all_to_all x1, blocking collectives, per_device(): lax.all_to_all(jnp.where(peer == above, high, low), 'sub', 0, 0, tiled=True)  15 us
    pallas_call x4, Pallas kernels, local_call(): pl.pallas_call(kernel, out_shape=[jax.ShapeDtypeStruct(shape, jnp.float32...  10.6 us
    all_to_all x1, starting transfers between devices, per_device(): row = jnp.sum(lax.all_to_all(spread, DOM, 0, 0, tiled=True), 0)  8.45 us
    ppermute x2, waiting for transfers between devices, pair_swap(): lax.ppermute(block, axes, [edge for a, b in groups for edge in ((a, b), (...  1.84 us
  transfers between devices with their start and end apart: 3, of which 2 were waited for; matrix products, arithmetic and copies ran while one was open for 0% of the time, Pallas kernels for 0%

profile of v7, /device:TPU:1, one launch (start us, length us, event | category | flops | bytes accessed | tf_op | source)
XLA Modules:
  0.0 79.9 jit_solution(5654708197711042822)
XLA Ops:
  0.6 4.2 %force.1 = (f32[248,128]{1,0:T(8,128)}, f32[8,2,4,64]{3,2,1,0:T(4,128)}, f32[136,128]{1,0:T(8,128)}, f32[136,128]{1,0:T(8,128)}) custom-call(f32[5,9,3,128]{3,2,1,0:T(4,128)} %bitcast.14, f32[5,9,3,128]{3,2,1,0:T(4,128)} %bitcast.15, f32[8,2,4,64]{3,2,1,0:T(4,128)} %refs_2_.1, f32[27,2,4,64]{3,2,1,0:T(4,128)} %refs_3_.1, f32[4,2,4,64]{3,2,1,0:T(4,128)} %refs_4_.1, ...), custom_call_target="tpu_custom_call" | custom-call | tf_op jit(solution)/shard_map/force/pallas_call | solution.py:601
  4.8 4.8 %collective-permute-start = (f32[136,128]{1,0:T(8,128)}, f32[136,128]{1,0:T(8,128)S(1)}, u32[]{:S(2)}, u32[]{:S(2)}) collective-permute-start(f32[136,128]{1,0:T(8,128)} %get-tuple-element.16), channel_id=1, source_target_pairs={{0,1},{1,0},{2,3},{3,2},{4,5},{5,4},{6,7},{7,6},{8,9},{9,8},{10,11... | collective-permute-start | bytes 208904 | tf_op jit(solution)/shard_map/ppermute | solution.py:618
  9.7 12.5 %collective-permute-start.1 = (f32[136,128]{1,0:T(8,128)}, f32[136,128]{1,0:T(8,128)S(1)}, u32[]{:S(2)}, u32[]{:S(2)}) collective-permute-start(f32[136,128]{1,0:T(8,128)} %get-tuple-element.17), channel_id=1, source_target_pairs={{1,2},{2,1},{3,4},{4,3},{5,6},{6,5},{7,8},{8,7},{9,10},{10,9},{11,... | collective-permute-start | bytes 208904 | tf_op jit(solution)/shard_map/ppermute | solution.py:618
  22.2 0.0 collective-permute-done.inner
  22.2 1.8 %collective-permute-done.1.outer = f32[136,128]{1,0:T(8,128)S(1)} collective-permute-done((f32[136,128]{1,0:T(8,128)}, f32[136,128]{1,0:T(8,128)S(1)}, u32[]{:S(2)}, u32[]{:S(2)}) %collective-permute-start.1) | collective-permute-done | bytes 69664 | tf_op jit(solution)/shard_map/ppermute | solution.py:618
  24.0 0.0 copy-start
  24.0 0.9 %copy-done = f32[248,128]{1,0:T(8,128)S(1)} copy-done((f32[248,128]{1,0:T(8,128)S(1)}, f32[248,128]{1,0:T(8,128)}, u32[]{:S(2)}) %copy-start) | copy-done | bytes 127000
  24.9 0.1 widen.1
  25.0 3.6 %all-gather = f32[1008,128]{1,0:T(8,128)S(1)} all-gather(f32[504,128]{1,0:T(8,128)S(1)} %widen.1), channel_id=2, replica_groups={{0,12},{24,36},{48,60},{72,84},{96,108},{120,132},{144,156},{168,180},{..., dimensions={0}, use_global_device_ids=true | all-gather | bytes 774144 | tf_op jit(solution)/shard_map/all_gather | solution.py:613
  28.7 6.7 %all_gather.28.cross = f32[2,504,128]{2,1,0:T(8,128)S(1)} all-gather(f32[1,504,128]{2,1,0:T(8,128)S(1)} %fusion), channel_id=1, replica_groups={{12,24},{36,48},{60,72},{84,96},{108,120},{132,144},{156,168},{180,192}..., dimensions={0}, use_global_device_ids=true | all-gather | bytes 774144 | tf_op jit(solution)/shard_map/all_gather | solution.py:613
  35.4 5.2 %all_gather.29.edges = f32[2,56,128]{2,1,0:T(8,128)S(1)} all-gather(f32[1,56,128]{2,1,0:T(8,128)S(1)} %slice_add_fusion), channel_id=1, replica_groups={{0,12},{24,36},{48,60},{72,84},{96,108},{120,132},{144,156},{168,180},{..., dimensions={0}, use_global_device_ids=true | all-gather | bytes 86016 | tf_op jit(solution)/shard_map/all_gather | solution.py:613
  40.6 4.8 %krylov.1 = (f32[3,5,9,128]{3,2,1,0:T(8,128)S(1)}, f32[3,5,9,128]{3,2,1,0:T(8,128)S(1)}, f32[3,5,9,128]{3,2,1,0:T(8,128)S(1)}, f32[3,5,9,128]{3,2,1,0:T(8,128)S(...) custom-call(f32[2,504,128]{2,1,0:T(8,128)S(1)} %bitcast.13, ...), custom_call_target="tpu_custom_call" | custom-call | tf_op jit(solution)/shard_map/krylov/pallas_call | solution.py:601
  45.4 8.4 %all-to-all-start = ((f32[64,1,16]{2,1,0:T(1,128)}), f32[64,1,16]{2,1,0:T(1,128)S(1)}, u32[]{:S(2)}, u32[]{:S(2)}) async-start(f32[64,1,16]{2,1,0:T(1,128)} %get-tuple-element.22), calls=%async_computation | async-start | bytes 65536 | tf_op jit(solution)/shard_map/all_to_all | solution.py:665
  53.8 4.2 %all-gather.1 = f32[64,128]{1,0:T(8,128)S(1)} all-gather(f32[32,128]{1,0:T(8,128)S(1)} %get-tuple-element.19), channel_id=3, replica_groups={{12,24},{36,48},{60,72},{84,96},{108,120},{132,144},{156,168},{180,192}..., dimensions={0}, use_global_device_ids=true | all-gather | bytes 49152 | tf_op jit(solution)/shard_map/all_gather | solution.py:613
  58.0 5.0 %all-gather.2 = f32[64,128]{1,0:T(8,128)S(1)} all-gather(f32[32,128]{1,0:T(8,128)S(1)} %get-tuple-element.20), channel_id=4, replica_groups={{0,12},{24,36},{48,60},{72,84},{96,108},{120,132},{144,156},{168,180},{..., dimensions={0}, use_global_device_ids=true | all-gather | bytes 49152 | tf_op jit(solution)/shard_map/all_gather | solution.py:613
  63.1 0.1 all-to-all-done
  63.2 0.1 reduce_sum.11
  63.3 0.1 broadcast_select_fusion
  63.3 15.0 %all_to_all.10.gathered = f32[12,16,128]{2,1,0:T(8,128)S(1)} all-to-all(f32[12,16,128]{2,1,0:T(8,128)S(1)} %broadcast_select_fusion), channel_id=1, replica_groups=mesh['dom_0'=8,'dom_1'=4,'dom_2'=2,'sub'=12] {'sub'}, dimensions={0} | all-to-all | bytes 196608 | tf_op jit(solution)/shard_map/all_to_all | solution.py:670
  78.3 1.6 %finish.1 = (f32[5,9,3,128]{3,2,1,0:T(4,128)}, f32[5,9,3,128]{3,2,1,0:T(4,128)}) custom-call(f32[12,16,128]{2,1,0:T(8,128)S(1)} %all_to_all.10.gathered, f32[3,5,9,128]{3,2,1,0:T(8,128)S(1)} %pad_maximum_fusion.image, f32[3,5,9,128]{3,2,1,0:T(8,128)S(1)} %get-tuple-element.23.t0, f32[3,5,9,128]{3,2,1,0:T(8,128)S(1)} %get-tuple-element.24.t1, ...), custom_call_target="tpu_custom_call" | custom-call | tf_op jit(solution)/shard_map/finish/pallas_call | solution.py:601
  (14 shorter events, 0.1 us)
Async XLA Ops:
  4.8 17.4 %collective-permute-start = (f32[136,128]{1,0:T(8,128)}, f32[136,128]{1,0:T(8,128)S(1)}, u32[]{:S(2)}, u32[]{:S(2)}) collective-permute-start(f32[136,128]{1,0:T(8,128)} %get-tuple-element.16), channel_id=1, source_target_pairs={{0,1},{1,0},{2,3},{3,2},{4,5},{5,4},{6,7},{7,6},{8,9},{9,8},{10,11... | collective-permute-start | bytes 208904 | tf_op jit(solution)/shard_map/ppermute | solution.py:618
  9.7 14.4 %collective-permute-start.1 = (f32[136,128]{1,0:T(8,128)}, f32[136,128]{1,0:T(8,128)S(1)}, u32[]{:S(2)}, u32[]{:S(2)}) collective-permute-start(f32[136,128]{1,0:T(8,128)} %get-tuple-element.17), channel_id=1, source_target_pairs={{1,2},{2,1},{3,4},{4,3},{5,6},{6,5},{7,8},{8,7},{9,10},{10,9},{11,... | collective-permute-start | bytes 208904 | tf_op jit(solution)/shard_map/ppermute | solution.py:618
  24.0 0.9 %copy-start = (f32[248,128]{1,0:T(8,128)S(1)}, f32[248,128]{1,0:T(8,128)}, u32[]{:S(2)}) copy-start(f32[248,128]{1,0:T(8,128)} %get-tuple-element.18.own) | copy-start | bytes 380932
  45.4 17.8 %all-to-all-start = ((f32[64,1,16]{2,1,0:T(1,128)}), f32[64,1,16]{2,1,0:T(1,128)S(1)}, u32[]{:S(2)}, u32[]{:S(2)}) async-start(f32[64,1,16]{2,1,0:T(1,128)} %get-tuple-element.22), calls=%async_computation | async-start | bytes 65536 | tf_op jit(solution)/shard_map/all_to_all | solution.py:665

commit v8 on v7

--- a/solution.py
+++ b/solution.py
@@ -657,9 +657,9 @@
         pair, cross, edges,
     )
     inner = pair_gather(inner, DOM, 0)
-    outer = pair_gather(outer, DOM, 1)
+    outer_far = pair_swap(outer, DOM, 1)
     inner = (inner[0] + inner[1])[:27].reshape(3, 1, 9, 128)
-    outer = (outer[0] + outer[1])[:27].reshape(3, 1, 9, 128)
+    outer = (outer + outer_far)[:27].reshape(3, 1, 9, 128)
     low_x, high_x = jnp.where(core == 0, outer, inner), jnp.where(core == 0, inner, outer)
     image = jnp.concatenate([low_x, partial[:, 1:4], high_x], 1)
     row = jnp.sum(lax.all_to_all(spread, DOM, 0, 0, tiled=True), 0)

time: 80.8 us -> 81.3 us (level)
  blocking collectives: 39.7 us -> 32.6 us
  waiting for transfers between devices: 1.91 us -> 5.78 us
  starting transfers between devices: 25.8 us -> 29.2 us
    all_gather x5 -> x4, blocking collectives: 24.7 us -> 17.5 us  [pair_gather(): lax.all_gather(block, axes, axis_index_groups=pair_groups(axes, offset))]
    all_to_all x1, waiting for transfers between devices: 0.06 us -> 3.94 us  [per_device(): row = jnp.sum(lax.all_to_all(spread, DOM, 0, 0, tiled=True), 0)]
    ppermute x2 -> x3, starting transfers between devices: 17.3 us -> 20.7 us  [pair_swap(): lax.ppermute(block, axes, [edge for a, b in groups for edge in ((a, b), (...]
    ppermute x2 -> x3, waiting for transfers between devices: 1.84 us -> 1.85 us  [pair_swap(): lax.ppermute(block, axes, [edge for a, b in groups for edge in ((a, b), (...]
  transfers between devices with their start and end apart: 3 -> 4, of which waited for: 2 -> 2; matrix products, arithmetic and copies ran while one was open for 0% -> 0% of each run, Pallas kernels for 0% -> 0%
where the time goes in v8:
time: 81.3 us; the launch traced here: 80.1 us
  blocking collectives  32.6 us (40%)
  starting transfers between devices  29.2 us (36%)
  Pallas kernels  10.6 us (13%)
  waiting for transfers between devices  5.78 us (7%)
  local copies, waits for them, and re-layouts  0.96 us (1%)
  between operations  0.82 us (1%)
    ppermute x3, starting transfers between devices, pair_swap(): lax.ppermute(block, axes, [edge for a, b in groups for edge in ((a, b), (...  20.7 us
    all_gather x4, blocking collectives, pair_gather(): lax.all_gather(block, axes, axis_index_groups=pair_groups(axes, offset))  17.5 us
    all_to_all x1, blocking collectives, per_device(): lax.all_to_all(jnp.where(peer == above, high, low), 'sub', 0, 0, tiled=True)  15.1 us
    pallas_call x4, Pallas kernels, local_call(): pl.pallas_call(kernel, out_shape=[jax.ShapeDtypeStruct(shape, jnp.float32...  10.6 us
    all_to_all x1, starting transfers between devices, per_device(): row = jnp.sum(lax.all_to_all(spread, DOM, 0, 0, tiled=True), 0)  8.45 us
    all_to_all x1, waiting for transfers between devices, per_device(): row = jnp.sum(lax.all_to_all(spread, DOM, 0, 0, tiled=True), 0)  3.94 us
    ppermute x3, waiting for transfers between devices, pair_swap(): lax.ppermute(block, axes, [edge for a, b in groups for edge in ((a, b), (...  1.85 us
  transfers between devices with their start and end apart: 4, of which 2 were waited for; matrix products, arithmetic and copies ran while one was open for 0% of the time, Pallas kernels for 0%

profile of v8, /device:TPU:1, one launch (start us, length us, event | category | flops | bytes accessed | tf_op | source)
XLA Modules:
  0.0 80.1 jit_solution(17217315794402274940)
XLA Ops:
  0.6 4.2 %force.1 = (f32[248,128]{1,0:T(8,128)}, f32[8,2,4,64]{3,2,1,0:T(4,128)}, f32[136,128]{1,0:T(8,128)}, f32[136,128]{1,0:T(8,128)}) custom-call(f32[5,9,3,128]{3,2,1,0:T(4,128)} %bitcast.22, f32[5,9,3,128]{3,2,1,0:T(4,128)} %bitcast.23, f32[8,2,4,64]{3,2,1,0:T(4,128)} %refs_2_.1, f32[27,2,4,64]{3,2,1,0:T(4,128)} %refs_3_.1, f32[4,2,4,64]{3,2,1,0:T(4,128)} %refs_4_.1, ...), custom_call_target="tpu_custom_call" | custom-call | tf_op jit(solution)/shard_map/force/pallas_call | solution.py:601
  4.8 4.8 %collective-permute-start = (f32[136,128]{1,0:T(8,128)}, f32[136,128]{1,0:T(8,128)S(1)}, u32[]{:S(2)}, u32[]{:S(2)}) collective-permute-start(f32[136,128]{1,0:T(8,128)} %get-tuple-element.16), channel_id=1, source_target_pairs={{0,1},{1,0},{2,3},{3,2},{4,5},{5,4},{6,7},{7,6},{8,9},{9,8},{10,11... | collective-permute-start | bytes 208904 | tf_op jit(solution)/shard_map/ppermute | solution.py:618
  9.7 12.5 %collective-permute-start.1 = (f32[136,128]{1,0:T(8,128)}, f32[136,128]{1,0:T(8,128)S(1)}, u32[]{:S(2)}, u32[]{:S(2)}) collective-permute-start(f32[136,128]{1,0:T(8,128)} %get-tuple-element.17), channel_id=1, source_target_pairs={{1,2},{2,1},{3,4},{4,3},{5,6},{6,5},{7,8},{8,7},{9,10},{10,9},{11,... | collective-permute-start | bytes 208904 | tf_op jit(solution)/shard_map/ppermute | solution.py:618
  22.2 0.0 collective-permute-done.inner
  22.2 1.8 %collective-permute-done.1.outer = f32[136,128]{1,0:T(8,128)S(1)} collective-permute-done((f32[136,128]{1,0:T(8,128)}, f32[136,128]{1,0:T(8,128)S(1)}, u32[]{:S(2)}, u32[]{:S(2)}) %collective-permute-start.1) | collective-permute-done | bytes 69664 | tf_op jit(solution)/shard_map/ppermute | solution.py:618
  24.0 0.0 copy-start
  24.0 0.9 %copy-done = f32[248,128]{1,0:T(8,128)S(1)} copy-done((f32[248,128]{1,0:T(8,128)S(1)}, f32[248,128]{1,0:T(8,128)}, u32[]{:S(2)}) %copy-start) | copy-done | bytes 127000
  24.9 0.1 widen.1
  25.0 3.6 %all-gather = f32[1008,128]{1,0:T(8,128)S(1)} all-gather(f32[504,128]{1,0:T(8,128)S(1)} %widen.1), channel_id=2, replica_groups={{0,12},{24,36},{48,60},{72,84},{96,108},{120,132},{144,156},{168,180},{..., dimensions={0}, use_global_device_ids=true | all-gather | bytes 774144 | tf_op jit(solution)/shard_map/all_gather | solution.py:613
  28.7 6.7 %all_gather.22.cross = f32[2,504,128]{2,1,0:T(8,128)S(1)} all-gather(f32[1,504,128]{2,1,0:T(8,128)S(1)} %fusion), channel_id=1, replica_groups={{12,24},{36,48},{60,72},{84,96},{108,120},{132,144},{156,168},{180,192}..., dimensions={0}, use_global_device_ids=true | all-gather | bytes 774144 | tf_op jit(solution)/shard_map/all_gather | solution.py:613
  35.4 5.2 %all_gather.23.edges = f32[2,56,128]{2,1,0:T(8,128)S(1)} all-gather(f32[1,56,128]{2,1,0:T(8,128)S(1)} %slice_add_fusion), channel_id=1, replica_groups={{0,12},{24,36},{48,60},{72,84},{96,108},{120,132},{144,156},{168,180},{..., dimensions={0}, use_global_device_ids=true | all-gather | bytes 86016 | tf_op jit(solution)/shard_map/all_gather | solution.py:613
  40.6 4.8 %krylov.1 = (f32[3,5,9,128]{3,2,1,0:T(8,128)S(1)}, f32[3,5,9,128]{3,2,1,0:T(8,128)S(1)}, f32[3,5,9,128]{3,2,1,0:T(8,128)S(1)}, f32[3,5,9,128]{3,2,1,0:T(8,128)S(...) custom-call(f32[2,504,128]{2,1,0:T(8,128)S(1)} %bitcast.19, ...), custom_call_target="tpu_custom_call" | custom-call | tf_op jit(solution)/shard_map/krylov/pallas_call | solution.py:601
  45.4 8.4 %all-to-all-start = ((f32[64,1,16]{2,1,0:T(1,128)}), f32[64,1,16]{2,1,0:T(1,128)S(1)}, u32[]{:S(2)}, u32[]{:S(2)}) async-start(f32[64,1,16]{2,1,0:T(1,128)} %get-tuple-element.22), calls=%async_computation | async-start | bytes 65536 | tf_op jit(solution)/shard_map/all_to_all | solution.py:665
  53.8 1.9 %all-gather.1 = f32[64,128]{1,0:T(8,128)S(1)} all-gather(f32[32,128]{1,0:T(8,128)S(1)} %get-tuple-element.20), channel_id=3, replica_groups={{0,12},{24,36},{48,60},{72,84},{96,108},{120,132},{144,156},{168,180},{..., dimensions={0}, use_global_device_ids=true | all-gather | bytes 49152 | tf_op jit(solution)/shard_map/all_gather | solution.py:613
  55.8 3.4 %collective-permute-start.2 = (f32[32,128]{1,0:T(8,128)S(1)}, f32[32,128]{1,0:T(8,128)S(1)}, u32[]{:S(2)}, u32[]{:S(2)}) collective-permute-start(f32[32,128]{1,0:T(8,128)S(1)} %get-tuple-element.19), channel_id=1, source_target_pairs={{12,24},{24,12},{36,48},{48,36},{60,72},{72,60},{84,96},{96,84},{1... | collective-permute-start | bytes 49160 | tf_op jit(solution)/shard_map/ppermute | solution.py:618
  59.2 3.9 %all-to-all-done = f32[64,1,16]{2,1,0:T(1,128)S(1)} async-done(((f32[64,1,16]{2,1,0:T(1,128)}), f32[64,1,16]{2,1,0:T(1,128)S(1)}, u32[]{:S(2)}, u32[]{:S(2)}) %all-to-all-start) | async-done | bytes 4128 | tf_op jit(solution)/shard_map/all_to_all | solution.py:665
  63.2 0.1 reduce_sum.11
  63.2 0.0 collective-permute-done.2
  63.4 0.1 broadcast_select_fusion
  63.5 15.1 %all_to_all.10.gathered = f32[12,16,128]{2,1,0:T(8,128)S(1)} all-to-all(f32[12,16,128]{2,1,0:T(8,128)S(1)} %broadcast_select_fusion), channel_id=1, replica_groups=mesh['dom_0'=8,'dom_1'=4,'dom_2'=2,'sub'=12] {'sub'}, dimensions={0} | all-to-all | bytes 196608 | tf_op jit(solution)/shard_map/all_to_all | solution.py:670
  78.6 1.6 %finish.1 = (f32[5,9,3,128]{3,2,1,0:T(4,128)}, f32[5,9,3,128]{3,2,1,0:T(4,128)}) custom-call(f32[12,16,128]{2,1,0:T(8,128)S(1)} %all_to_all.10.gathered, f32[3,5,9,128]{3,2,1,0:T(8,128)S(1)} %pad_maximum_fusion.image, f32[3,5,9,128]{3,2,1,0:T(8,128)S(1)} %get-tuple-element.23.t0, f32[3,5,9,128]{3,2,1,0:T(8,128)S(1)} %get-tuple-element.24.t1, ...), custom_call_target="tpu_custom_call" | custom-call | tf_op jit(solution)/shard_map/finish/pallas_call | solution.py:601
  (13 shorter events, 0.1 us)
Async XLA Ops:
  4.8 17.4 %collective-permute-start = (f32[136,128]{1,0:T(8,128)}, f32[136,128]{1,0:T(8,128)S(1)}, u32[]{:S(2)}, u32[]{:S(2)}) collective-permute-start(f32[136,128]{1,0:T(8,128)} %get-tuple-element.16), channel_id=1, source_target_pairs={{0,1},{1,0},{2,3},{3,2},{4,5},{5,4},{6,7},{7,6},{8,9},{9,8},{10,11... | collective-permute-start | bytes 208904 | tf_op jit(solution)/shard_map/ppermute | solution.py:618
  9.7 14.4 %collective-permute-start.1 = (f32[136,128]{1,0:T(8,128)}, f32[136,128]{1,0:T(8,128)S(1)}, u32[]{:S(2)}, u32[]{:S(2)}) collective-permute-start(f32[136,128]{1,0:T(8,128)} %get-tuple-element.17), channel_id=1, source_target_pairs={{1,2},{2,1},{3,4},{4,3},{5,6},{6,5},{7,8},{8,7},{9,10},{10,9},{11,... | collective-permute-start | bytes 208904 | tf_op jit(solution)/shard_map/ppermute | solution.py:618
  24.0 0.9 %copy-start = (f32[248,128]{1,0:T(8,128)S(1)}, f32[248,128]{1,0:T(8,128)}, u32[]{:S(2)}) copy-start(f32[248,128]{1,0:T(8,128)} %get-tuple-element.18.own) | copy-start | bytes 380932
  45.4 17.8 %all-to-all-start = ((f32[64,1,16]{2,1,0:T(1,128)}), f32[64,1,16]{2,1,0:T(1,128)S(1)}, u32[]{:S(2)}, u32[]{:S(2)}) async-start(f32[64,1,16]{2,1,0:T(1,128)} %get-tuple-element.22), calls=%async_computation | async-start | bytes 65536 | tf_op jit(solution)/shard_map/all_to_all | solution.py:665
  55.8 7.5 %collective-permute-start.2 = (f32[32,128]{1,0:T(8,128)S(1)}, f32[32,128]{1,0:T(8,128)S(1)}, u32[]{:S(2)}, u32[]{:S(2)}) collective-permute-start(f32[32,128]{1,0:T(8,128)S(1)} %get-tuple-element.19), channel_id=1, source_target_pairs={{12,24},{24,12},{36,48},{48,36},{60,72},{72,60},{84,96},{96,84},{1... | collective-permute-start | bytes 49160 | tf_op jit(solution)/shard_map/ppermute | solution.py:618
